TPU v7x, 1024 devices: a whole 8x8x8 slice. The times are simulated.
1024 devices in a mesh: row: 16 (over z_hi, y), col: 64 (over z_lo, x, core).
Axes of the slice: x: 8, y: 8, z: 8 (z_hi: 2, z_lo: 4; z = z_hi * 4 + z_lo), core: 2. Of those that a mesh axis runs over, the one named last changes fastest.
Arguments:
- query_states: bfloat16 [16, 64, 128, 768], P('row', 'col'), may hold values from -15 to 15
- key_states: bfloat16 [16, 64, 128, 768], P('row', 'col'), may hold values from -6 to 6
- value_states: bfloat16 [16, 64, 128, 768], P('row', 'col'), may hold values from -6 to 6
- tissue_map: int32 [16, 64], replicated, may hold values 0 or 1
Outputs:
- attended: bfloat16 [16, 64, 128, 768], P('row', 'col')
All inputs are finite; a program needn't handle non-finite values.
Results may differ from a plain program's by a relative error of at most 0.0032.
Values may be sent and summed in bfloat16 or wider, within the bound.
No kernel may reach another device: no remote copies, remote signals or barrier semaphores. Data moves between devices by JAX's collectives and lax.ppermute only.
A program may use at most 32 MiB of HBM per device.

v0:
```python
import jax
import jax.numpy as jnp
from jax import lax
from jax.sharding import PartitionSpec as P

HDIM = 64
HEADS = 12


def extended(x, sides, width):
    for axis, dim in sides:
        devices, length = (lax.axis_size(axis), x.shape[dim])
        up = [(i, (i + 1) % devices) for i in range(devices - 1)]
        down = [(j, i) for i, j in up]
        last = lax.slice_in_dim(x, length - width, length, axis=dim)
        initial = lax.slice_in_dim(x, 0, width, axis=dim)
        before = lax.ppermute(last, axis, up)
        after = lax.ppermute(initial, axis, down)
        x = jnp.concatenate([before, x, after], axis=dim)
    return x


def attend_row(query_row, keys_row, values_row, key_keep, own_tile):
    score_scale = HDIM ** (-0.5)
    tile_count = query_row.shape[0]
    tokens = query_row.shape[1]
    query_heads = query_row.reshape(tile_count, tokens, HEADS, HDIM)
    key_heads = keys_row.reshape(tile_count, keys_row.shape[1], HEADS, HDIM)
    value_heads = values_row.reshape(tile_count, values_row.shape[1], HEADS, HDIM)
    scores = (
        jnp.einsum("bqhd,bkhd->bhqk", query_heads, key_heads, preferred_element_type=jnp.float32)
        * score_scale
    )
    scores = jnp.where(key_keep[:, None, None, :], scores, -jnp.inf)
    row_top = jnp.max(scores, axis=-1, keepdims=True)
    weights = jnp.exp(scores - row_top)
    totals = jnp.sum(weights, axis=-1)
    rounded = weights.astype(jnp.bfloat16)
    mixed = jnp.einsum("bhqk,bkhd->bqhd", rounded, value_heads, preferred_element_type=jnp.float32)
    mixed = mixed / jnp.transpose(totals, (0, 2, 1))[:, :, :, None]
    mixed = mixed * own_tile[:, None, None, None]
    return mixed.reshape(tile_count, tokens, HEADS * HDIM).astype(jnp.bfloat16)


def on_device(query_states, key_states, value_states, tissue_map):
    tile_rows = query_states.shape[0]
    tile_cols = query_states.shape[1]
    tokens = query_states.shape[2]
    paired = jnp.stack([key_states, value_states])
    padded = extended(paired, (("row", 1), ("col", 2)), 1)
    row_start = lax.axis_index("row") * tile_rows
    col_start = lax.axis_index("col") * tile_cols
    framed = jnp.pad(tissue_map, 1)
    nearby = lax.dynamic_slice(framed, (row_start, col_start), (tile_rows + 2, tile_cols + 2))
    centre = jnp.arange(9) == 4
    pieces = []
    markers = []
    for row_off in range(3):
        for col_off in range(3):
            pieces.append(padded[:, row_off, col_off : col_off + tile_cols])
            markers.append(nearby[row_off, col_off : col_off + tile_cols])
    gathered = jnp.concatenate(pieces, axis=2)
    present = (jnp.stack(markers, axis=1) > 0) | centre[None, :]
    key_keep = jnp.repeat(present, tokens, axis=1)
    own_tile = nearby[1, 1 : 1 + tile_cols].astype(jnp.float32)
    results = [attend_row(query_states[0], gathered[0], gathered[1], key_keep, own_tile)]
    return jnp.stack(results)


def solution(mesh):
    return jax.shard_map(
        on_device,
        mesh=mesh,
        in_specs=(
            P("row", "col", None, None),
            P("row", "col", None, None),
            P("row", "col", None, None),
            P(),
        ),
        out_specs=P("row", "col", None, None),
        check_vma=False,
    )
```

profile of v0, /device:TPU:655, one launch (start us, length us, event | category | flops | bytes accessed | tf_op | source)
XLA Modules:
  0.0 70.4 jit_solution(15476056597958810464)
XLA Ops:
  0.0 0.0 copy-start.2
  0.0 0.0 copy-start.3
  0.0 1.1 %fusion.24 = bf16[2,1,1,128,768]{4,3,0,2,1:T(8,128)(2,1)S(1)} fusion(bf16[1,1,1,128,768]{4,3,2,1,0:T(8,128)(2,1)} %bitcast.87, bf16[1,1,1,128,768]{4,3,2,1,0:T(8,128)(2,1)} %bitcast.89), kind=kLoop, calls=%fused_computation.29 | loop fusion | flops 196608 | bytes 786432 | tf_op jit(solution)/shard_map/stack | solution.py:49
  1.1 1.9 %collective-permute-start.1 = (bf16[2,1,1,128,768]{4,3,0,2,1:T(8,128)(2,1)S(1)}, bf16[2,1,1,128,768]{4,3,0,2,1:T(8,128)(2,1)S(1)}, u32[]{:S(2)}, u32[]{:S(2)}) collective-permute-start(bf16[2,1,1,128,768]{4,3,0,2,1:T(8,128)(2,1)S(1)} %fusion.24), channel_id=1, source_target_pairs={{64,0},{128,64},{192,128},{256,192},{320,256},{384,320},{448,384},... | collective-permute-start | bytes 1179656 | tf_op jit(solution)/shard_map/ppermute | solution.py:18
  3.0 3.4 %collective-permute-start = (bf16[2,1,1,128,768]{4,3,0,2,1:T(8,128)(2,1)S(1)}, bf16[2,1,1,128,768]{4,3,0,2,1:T(8,128)(2,1)S(1)}, u32[]{:S(2)}, u32[]{:S(2)}) collective-permute-start(bf16[2,1,1,128,768]{4,3,0,2,1:T(8,128)(2,1)S(1)} %fusion.24), channel_id=1, source_target_pairs={{0,64},{64,128},{128,192},{192,256},{256,320},{320,384},{384,448},... | collective-permute-start | bytes 1179656 | tf_op jit(solution)/shard_map/ppermute | solution.py:17
  6.4 6.6 %collective-permute-done.1 = bf16[2,1,1,128,768]{4,3,0,2,1:T(8,128)(2,1)S(1)} collective-permute-done((bf16[2,1,1,128,768]{4,3,0,2,1:T(8,128)(2,1)S(1)}, bf16[2,1,1,128,768]{4,3,0,2,1:T(8,128)(2,1)S(1)}, u32[]{:S(2)}, u32[]{:S(2)}) %collective-permute-start.1) | collective-permute-done | bytes 393248 | tf_op jit(solution)/shard_map/ppermute | solution.py:18
  13.0 13.1 %collective-permute-done = bf16[2,1,1,128,768]{4,3,0,2,1:T(8,128)(2,1)S(1)} collective-permute-done((bf16[2,1,1,128,768]{4,3,0,2,1:T(8,128)(2,1)S(1)}, bf16[2,1,1,128,768]{4,3,0,2,1:T(8,128)(2,1)S(1)}, u32[]{:S(2)}, u32[]{:S(2)}) %collective-permute-start) | collective-permute-done | bytes 393248 | tf_op jit(solution)/shard_map/ppermute | solution.py:17
  26.1 1.1 %pad_maximum_fusion = bf16[2,3,1,128,768]{4,3,0,2,1:T(8,128)(2,1)} fusion(bf16[2,1,1,128,768]{4,3,0,2,1:T(8,128)(2,1)S(1)} %collective-permute-done.1, bf16[2,1,1,128,768]{4,3,0,2,1:T(8,128)(2,1)S(1)} %fusion.24, bf16[2,1,1,128,768]{4,3,0,2,1:T(8,128)(2,1)S(1)} %collective-permute-done), kind=kLoop, calls=%fused_computation.9 | loop fusion | flops 1179648 | bytes 2359296 | tf_op jit(solution)/shard_map/concatenate | solution.py:19
  27.3 11.0 %collective-permute-start.2 = (bf16[2,3,1,128,768]{4,3,0,2,1:T(8,128)(2,1)}, bf16[2,3,1,128,768]{4,3,0,2,1:T(8,128)(2,1)S(1)}, u32[]{:S(2)}, u32[]{:S(2)}) collective-permute-start(bf16[2,3,1,128,768]{4,3,0,2,1:T(8,128)(2,1)} %pad_maximum_fusion), channel_id=1, source_target_pairs={{0,1},{1,2},{2,3},{3,4},{4,5},{5,6},{6,7},{7,8},{8,9},{9,10},{10,1... | collective-permute-start | bytes 3538952 | tf_op jit(solution)/shard_map/ppermute | solution.py:17
  38.2 1.9 %collective-permute-start.3 = (bf16[2,3,1,128,768]{4,3,0,2,1:T(8,128)(2,1)}, bf16[2,3,1,128,768]{4,3,0,2,1:T(8,128)(2,1)S(1)}, u32[]{:S(2)}, u32[]{:S(2)}) collective-permute-start(bf16[2,3,1,128,768]{4,3,0,2,1:T(8,128)(2,1)} %pad_maximum_fusion), channel_id=1, source_target_pairs={{1,0},{2,1},{3,2},{4,3},{5,4},{6,5},{7,6},{8,7},{9,8},{10,9},{11,1... | collective-permute-start | bytes 3538952 | tf_op jit(solution)/shard_map/ppermute | solution.py:18
  40.2 0.8 %pad_dynamic-slice_fusion = s32[3,3]{1,0:T(4,128)S(1)} fusion(s32[]{:T(128)S(6)} %select_n.14, s32[]{:T(128)S(6)} %select_n.15, s32[16,64]{1,0:T(8,128)} %param.7), kind=kLoop, calls=%fused_computation.30 | loop fusion | bytes 4140 | tf_op jit(solution)/shard_map/dynamic_slice | solution.py:54
  41.0 0.6 slice.56
  42.2 1.7 %copy.18 = bf16[1,1,128,768]{2,3,1,0:T(8,128)(2,1)} copy(bf16[1,1,128,768]{3,2,1,0:T(8,128)(2,1)} %param.4) | data formatting | bytes 393216 | tf_op args[0]
  43.9 0.1 compare_or_fusion
  44.0 0.1 broadcast_bitcast_fusion
  44.1 7.6 %collective-permute-done.2 = bf16[2,3,1,128,768]{4,3,0,2,1:T(8,128)(2,1)S(1)} collective-permute-done((bf16[2,3,1,128,768]{4,3,0,2,1:T(8,128)(2,1)}, bf16[2,3,1,128,768]{4,3,0,2,1:T(8,128)(2,1)S(1)}, u32[]{:S(2)}, u32[]{:S(2)}) %collective-permute-start.2) | collective-permute-done | bytes 1179680 | tf_op jit(solution)/shard_map/ppermute | solution.py:17
  51.7 6.3 %collective-permute-done.3 = bf16[2,3,1,128,768]{4,3,0,2,1:T(8,128)(2,1)S(1)} collective-permute-done((bf16[2,3,1,128,768]{4,3,0,2,1:T(8,128)(2,1)}, bf16[2,3,1,128,768]{4,3,0,2,1:T(8,128)(2,1)S(1)}, u32[]{:S(2)}, u32[]{:S(2)}) %collective-permute-start.3) | collective-permute-done | bytes 1179680 | tf_op jit(solution)/shard_map/ppermute | solution.py:18
  58.1 0.0 copy-done.2
  58.2 0.0 copy-done.3
  58.3 0.2 fusion.27
  58.6 2.2 %copy.17 = bf16[1,1,1152,768]{2,3,1,0:T(8,128)(2,1)} copy(bf16[1,1,1152,768]{3,2,0,1:T(8,128)(2,1)S(1)} %get-tuple-element.5) | data formatting | bytes 3538944 | tf_op jit(solution)/shard_map/slice | solution.py:66
  60.8 0.0 copy-start
  60.8 2.2 %copy.16 = bf16[1,1,1152,768]{2,3,1,0:T(8,128)(2,1)} copy(bf16[1,1,1152,768]{3,2,0,1:T(8,128)(2,1)S(1)} %get-tuple-element.6) | data formatting | bytes 3538944 | tf_op jit(solution)/shard_map/slice | solution.py:66
  63.1 0.0 copy-done
  63.1 2.6 %bitcast_reduce_fusion = (f32[12,128]{1,0:T(8,128)S(1)}, f32[12,1152,128]{2,1,0:T(8,128)S(1)}) fusion(pred[1152]{0:T(1024)(128)(4,1)S(1)} %broadcast_bitcast_fusion, bf16[1152,12,64]{0,2,1:T(8,128)(2,1)S(1)} %bitcast.85, bf16[128,12,64]{0,2,1:T(8,128)(2,1)} %bitcast.91), kind=kOutput, calls=%fused_computation.1 | convolution fusion | flops 231799296 | bytes 9051264 | tf_op jit(solution)/shard_map/bqhd,bkhd->bhqk/dot_general | solution.py:31
  65.7 0.0 copy-start.1
  65.7 1.9 %fusion.1 = f32[12,128]{1,0:T(8,128)S(1)} fusion(f32[12,1152,128]{2,1,0:T(8,128)S(1)} %get-tuple-element.11, f32[12,128]{1,0:T(8,128)S(1)} %get-tuple-element.10, pred[1152]{0:T(1024)(128)(4,1)S(1)} %broadcast_bitcast_fusion), kind=kLoop, calls=%fused_computation.4 | loop fusion | flops 7076352 | bytes 7091328 | tf_op jit(solution)/shard_map/reduce_sum | solution.py:37
  67.6 0.0 copy-done.1
  67.6 1.9 %fusion.15 = bf16[1,128,12,64]{1,3,2,0:T(8,128)(2,1)S(1)} fusion(bf16[1152,12,64]{0,2,1:T(8,128)(2,1)S(1)} %bitcast.86, f32[12,1152,128]{2,1,0:T(8,128)S(1)} %get-tuple-element.11, f32[12,128]{1,0:T(8,128)S(1)} %get-tuple-element.10, pred[1152]{0:T(1024)(128)(4,1)S(1)} %broadcast_bitcast_fusion, f32[]{:T(128)} %bitcast.27, f32[128,12]{0,1:T(8,128)S(1)} %bitcast.93), kind=kOutput, calls=%fused_computation.12 | convolution fusion | flops 233865216 | bytes 9057412 | tf_op jit(solution)/shard_map/bhqk,bkhd->bqhd/dot_general | solution.py:39
  69.5 0.8 %copy.20 = bf16[1,1,128,768]{3,2,1,0:T(8,128)(2,1)} copy(bf16[1,1,128,768]{2,3,1,0:T(8,128)(2,1)S(1)} %bitcast.92) | data formatting | bytes 393216 | tf_op jit(solution)/shard_map/convert_element_type | solution.py:42
  (10 shorter events, 0.3 us)
Async XLA Ops:
  0.0 58.2 %copy-start.2 = (bf16[1,1,128,768]{3,2,1,0:T(8,128)(2,1)S(1)}, bf16[1,1,128,768]{3,2,1,0:T(8,128)(2,1)}, u32[]{:S(2)}) copy-start(bf16[1,1,128,768]{3,2,1,0:T(8,128)(2,1)} %param.6) | copy-start | bytes 589828
  0.0 58.2 %copy-start.3 = (bf16[1,1,128,768]{3,2,1,0:T(8,128)(2,1)S(1)}, bf16[1,1,128,768]{3,2,1,0:T(8,128)(2,1)}, u32[]{:S(2)}) copy-start(bf16[1,1,128,768]{3,2,1,0:T(8,128)(2,1)} %param.5) | copy-start | bytes 589828
  1.1 11.9 %collective-permute-start.1 = (bf16[2,1,1,128,768]{4,3,0,2,1:T(8,128)(2,1)S(1)}, bf16[2,1,1,128,768]{4,3,0,2,1:T(8,128)(2,1)S(1)}, u32[]{:S(2)}, u32[]{:S(2)}) collective-permute-start(bf16[2,1,1,128,768]{4,3,0,2,1:T(8,128)(2,1)S(1)} %fusion.24), channel_id=1, source_target_pairs={{64,0},{128,64},{192,128},{256,192},{320,256},{384,320},{448,384},... | collective-permute-start | bytes 1179656 | tf_op jit(solution)/shard_map/ppermute | solution.py:18
  3.0 23.1 %collective-permute-start = (bf16[2,1,1,128,768]{4,3,0,2,1:T(8,128)(2,1)S(1)}, bf16[2,1,1,128,768]{4,3,0,2,1:T(8,128)(2,1)S(1)}, u32[]{:S(2)}, u32[]{:S(2)}) collective-permute-start(bf16[2,1,1,128,768]{4,3,0,2,1:T(8,128)(2,1)S(1)} %fusion.24), channel_id=1, source_target_pairs={{0,64},{64,128},{128,192},{192,256},{256,320},{320,384},{384,448},... | collective-permute-start | bytes 1179656 | tf_op jit(solution)/shard_map/ppermute | solution.py:17
  27.3 24.4 %collective-permute-start.2 = (bf16[2,3,1,128,768]{4,3,0,2,1:T(8,128)(2,1)}, bf16[2,3,1,128,768]{4,3,0,2,1:T(8,128)(2,1)S(1)}, u32[]{:S(2)}, u32[]{:S(2)}) collective-permute-start(bf16[2,3,1,128,768]{4,3,0,2,1:T(8,128)(2,1)} %pad_maximum_fusion), channel_id=1, source_target_pairs={{0,1},{1,2},{2,3},{3,4},{4,5},{5,6},{6,7},{7,8},{8,9},{9,10},{10,1... | collective-permute-start | bytes 3538952 | tf_op jit(solution)/shard_map/ppermute | solution.py:17
  38.2 19.8 %collective-permute-start.3 = (bf16[2,3,1,128,768]{4,3,0,2,1:T(8,128)(2,1)}, bf16[2,3,1,128,768]{4,3,0,2,1:T(8,128)(2,1)S(1)}, u32[]{:S(2)}, u32[]{:S(2)}) collective-permute-start(bf16[2,3,1,128,768]{4,3,0,2,1:T(8,128)(2,1)} %pad_maximum_fusion), channel_id=1, source_target_pairs={{1,0},{2,1},{3,2},{4,3},{5,4},{6,5},{7,6},{8,7},{9,8},{10,9},{11,1... | collective-permute-start | bytes 3538952 | tf_op jit(solution)/shard_map/ppermute | solution.py:18
  60.8 2.2 %copy-start = (bf16[1,1,1152,768]{2,3,1,0:T(8,128)(2,1)S(1)}, bf16[1,1,1152,768]{2,3,1,0:T(8,128)(2,1)}, u32[]{:S(2)}) copy-start(bf16[1,1,1152,768]{2,3,1,0:T(8,128)(2,1)} %copy.17) | copy-start | bytes 5308420
  65.7 1.9 %copy-start.1 = (bf16[1,1,1152,768]{2,3,1,0:T(8,128)(2,1)S(1)}, bf16[1,1,1152,768]{2,3,1,0:T(8,128)(2,1)}, u32[]{:S(2)}) copy-start(bf16[1,1,1152,768]{2,3,1,0:T(8,128)(2,1)} %copy.16) | copy-start | bytes 5308420
where the time goes:
time: 70.7 us; the launch traced here: 70.4 us
  waiting for transfers between devices  33.6 us (48%)
  starting transfers between devices  18.2 us (26%)
  local copies, waits for them, and re-layouts  8.97 us (13%)
  matrix products  4.51 us (6%)
  other arithmetic  4.28 us (6%)
  between operations  0.82 us (1%)
    ppermute x2, waiting for transfers between devices, extended(): before = lax.ppermute(last, axis, up)  20.7 us
    ppermute x2, starting transfers between devices, extended(): before = lax.ppermute(last, axis, up)  14.3 us
    ppermute x2, waiting for transfers between devices, extended(): after = lax.ppermute(initial, axis, down)  12.9 us
    ppermute x2, starting transfers between devices, extended(): after = lax.ppermute(initial, axis, down)  3.84 us
    dot_general x1, matrix products, attend_row(): jnp.einsum('bqhd,bkhd->bhqk', query_heads, key_heads, preferred_element_t...  2.61 us
    slice x2, local copies, waits for them, and re-layouts, on_device(): gathered[0]  2.47 us
    slice x1, local copies, waits for them, and re-layouts, on_device(): gathered[1]  2.24 us
    unnamed x16, local copies, waits for them, and re-layouts  1.95 us
  transfers between devices with their start and end apart: 4, of which 4 were waited for; matrix products, arithmetic and copies ran while one was open for 5% of the time, Pallas kernels for 0%

commit v1 on v0

v1 whole, which is shorter than its diff:
```python
import functools

import jax
import jax.numpy as jnp
from jax import lax
from jax.experimental import pallas as pl
from jax.experimental.pallas import tpu as pltpu
from jax.sharding import PartitionSpec as P

HDIM = 64
HEADS = 12
PAIR = 2 * HDIM
PAIRS = HEADS // 2
TOK = 128
HD = HEADS * HDIM
LOG2E = 1.4426950408889634
SCALE = HDIM ** (-0.5) * LOG2E
NEG = -1e30
FLOOR = -1e20
VMEM = pl.BlockSpec(memory_space=pltpu.VMEM)
SMEM = pl.BlockSpec(memory_space=pltpu.SMEM)
F32 = jnp.float32
BF16 = jnp.bfloat16


def swaps(count, first):
    pairs = []
    for i in range(first, count - 1, 2):
        pairs += [(i, i + 1), (i + 1, i)]
    return pairs


def partner(i, odd):
    return ((i + 1) ^ 1) - 1 if odd else i ^ 1


def lane_low():
    return lax.broadcasted_iota(jnp.int32, (TOK, PAIR), 1) < HDIM


def position():
    return lax.axis_index("row"), lax.axis_index("col")


def tile_bias(tissue, row, col):
    rows, cols = tissue.shape
    inside = (row >= 0) & (row < rows)
    at = tissue[jnp.clip(row, 0, rows - 1), col]
    return jnp.where(inside & (at > 0), 0.0, NEG).astype(F32)


def attend_pair(query, keys, values, biases, low):
    zero = jnp.zeros_like(query)
    both = jnp.concatenate([jnp.where(low, query, zero), jnp.where(low, zero, query)], axis=0)
    scores = []
    for key, bias in zip(keys, biases):
        s = lax.dot_general(both, key, (((1,), (1,)), ((), ())), preferred_element_type=F32) * SCALE
        scores.append(s if bias is None else s + bias)
    top = functools.reduce(jnp.maximum, scores)
    top = jnp.maximum(jnp.max(top, axis=1, keepdims=True), FLOOR)
    weights = [jnp.exp2(s - top) for s in scores]
    total = jnp.sum(functools.reduce(jnp.add, weights), axis=1, keepdims=True)
    mixed = functools.reduce(
        jnp.add,
        [jnp.dot(w.astype(BF16), v, preferred_element_type=F32) for w, v in zip(weights, values)],
    )
    shape = (TOK, PAIR)
    top2 = jnp.where(low, jnp.broadcast_to(top[:TOK], shape), jnp.broadcast_to(top[TOK:], shape))
    tot2 = jnp.where(low, jnp.broadcast_to(total[:TOK], shape), jnp.broadcast_to(total[TOK:], shape))
    mix2 = jnp.where(low, mixed[:TOK], mixed[TOK:])
    return top2, tot2, mix2


def lanes(p):
    return slice(p * PAIR, (p + 1) * PAIR)


def early_kernel(tissue, q, qc, qd, k, v, ka, va, top_ref, tot_ref, mix_ref):
    row, col = position()
    low = lane_low()
    own = tile_bias(tissue, row, col)
    near = tile_bias(tissue, partner(row, False), col)
    for i, query in enumerate((q, qc, qd)):
        for p in range(PAIRS):
            at = lanes(p)
            t, l, m = attend_pair(
                query[:, at], (k[:, at], ka[:, at]), (v[:, at], va[:, at]),
                (None if i == 0 else own, near), low,
            )
            top_ref[i, :, at] = t
            tot_ref[i, :, at] = l
            mix_ref[i, :, at] = m


def late_part(query, kvb, bias, top, tot, mix, i, p, low):
    at = lanes(p)
    t, l, m = attend_pair(query[:, at], (kvb[0, :, at],), (kvb[1, :, at],), (bias,), low)
    t0 = top[i, :, at]
    best = jnp.maximum(t, t0)
    new, old = jnp.exp2(t - best), jnp.exp2(t0 - best)
    return best, l * new + tot[i, :, at] * old, m * new + mix[i, :, at] * old


def spot(p):
    return (lax.broadcasted_iota(jnp.int32, (TOK, PAIR), 1) & (HDIM - 1)) == p


def pieces(x, count):
    parts = []
    for _ in range(count):
        part = x.astype(BF16).astype(F32)
        parts.append(part)
        x = x - part
    return parts


def side_kernel(tissue, qc, qd, kvb, top, tot, mix, out_c, out_d):
    row, col = position()
    low = lane_low()
    bias = tile_bias(tissue, partner(row, True), col)
    for i, (query, out) in enumerate(((qc, out_c), (qd, out_d))):
        stats = jnp.zeros((TOK, PAIR), F32)
        for p in range(PAIRS):
            best, total, mixed = late_part(query, kvb, bias, top, tot, mix, i + 1, p, low)
            out[:, lanes(p)] = mixed.astype(BF16)
            for slot, piece in enumerate(pieces(best, 3) + pieces(total, 2)):
                stats = jnp.where(spot(p + 8 * slot), piece, stats)
        out[:, HD:] = stats.astype(BF16)


def own_kernel(tissue, q, kvb, top, tot, mix, mix_out, top_out, tot_out):
    row, col = position()
    low = lane_low()
    bias = tile_bias(tissue, partner(row, True), col)
    tops = jnp.zeros((TOK, PAIR), F32)
    tots = jnp.ones((TOK, PAIR), F32)
    for p in range(PAIRS):
        best, total, mixed = late_part(q, kvb, bias, top, tot, mix, 0, p, low)
        mix_out[:, lanes(p)] = mixed
        tops = jnp.where(spot(p), best, tops)
        tots = jnp.where(spot(p), total, tots)
    top_out[...] = tops
    tot_out[...] = tots


def merge_kernel(cols, tissue, mix, top, tot, in_c, in_d, out):
    row, col = position()
    low = lane_low()
    own = jnp.where(tissue[row, col] > 0, 1.0, 0.0).astype(F32)
    other = partner(col, True)
    missing = jnp.where((other >= 0) & (other < cols), 0.0, NEG).astype(F32)
    tops, tots = [top[...]], [tot[...]]
    for part, gap in ((in_c, None), (in_d, missing)):
        stats = part[:, HD:].astype(F32)
        slots = [stats] + [pltpu.roll(stats, PAIR - 8 * slot, 1) for slot in range(1, 5)]
        highest = slots[0] + slots[1] + slots[2]
        tops.append(highest if gap is None else highest + gap)
        tots.append(slots[3] + slots[4])
    best = functools.reduce(jnp.maximum, tops)
    shares = [jnp.exp2(t - best) for t in tops]
    total = functools.reduce(jnp.add, [s * t for s, t in zip(shares, tots)])
    shares = [s * own / total for s in shares]
    for p in range(PAIRS):
        at = lanes(p)
        acc = None
        for share, part in zip(shares, (mix, in_c, in_d)):
            shape = (TOK, PAIR)
            factor = jnp.where(
                low,
                jnp.broadcast_to(share[:, p : p + 1], shape),
                jnp.broadcast_to(share[:, HDIM + p : HDIM + p + 1], shape),
            )
            term = factor * part[:, at].astype(F32)
            acc = term if acc is None else acc + term
        out[:, at] = acc.astype(BF16)


def call(body, outs, name, units, *args):
    specs = [SMEM] + [VMEM] * (len(args) - 1)
    moved = sum(a.size * a.dtype.itemsize for a in args)
    moved += sum(o.size * o.dtype.itemsize for o in outs)
    return pl.pallas_call(
        body,
        out_shape=outs,
        in_specs=specs,
        out_specs=[VMEM] * len(outs),
        name=name,
        compiler_params=pltpu.CompilerParams(vmem_limit_bytes=16 << 20),
        cost_estimate=pl.CostEstimate(
            flops=units,
            transcendentals=0,
            bytes_accessed=1024,
        ),
    )(*args)


def shaped(*shape, dtype=F32):
    return jax.ShapeDtypeStruct(shape, dtype)


def on_device(query_states, key_states, value_states, tissue):
    q, k, v = (a.reshape(TOK, HD) for a in (query_states, key_states, value_states))
    rows, cols = tissue.shape
    far, near = swaps(rows, 1), swaps(rows, 0)
    beyond, beside = swaps(cols, 1), swaps(cols, 0)
    kvb = lax.ppermute(jnp.stack([k, v]), "row", far)
    qd = lax.ppermute(q, "col", beyond)
    qc = lax.ppermute(q, "col", beside)
    ka = lax.ppermute(k, "row", near)
    va = lax.ppermute(v, "row", near)
    state = [shaped(3, TOK, HD)] * 3
    top, tot, mix = call(early_kernel, state, "early", 6, tissue, q, qc, qd, k, v, ka, va)
    pack = shaped(TOK, HD + PAIR, dtype=BF16)
    out_c, out_d = call(side_kernel, [pack] * 2, "side", 2, tissue, qc, qd, kvb, top, tot, mix)
    in_d = lax.ppermute(out_d, "col", beyond)
    in_c = lax.ppermute(out_c, "col", beside)
    own = [shaped(TOK, HD), shaped(TOK, PAIR), shaped(TOK, PAIR)]
    mix, top, tot = call(own_kernel, own, "own", 1, tissue, q, kvb, top, tot, mix)
    (out,) = call(
        functools.partial(merge_kernel, cols), [shaped(TOK, HD, dtype=BF16)], "merge", 0,
        tissue, mix, top, tot, in_c, in_d,
    )
    return out.reshape(1, 1, TOK, HD)


def solution(mesh):
    return jax.shard_map(
        on_device,
        mesh=mesh,
        in_specs=(
            P("row", "col", None, None),
            P("row", "col", None, None),
            P("row", "col", None, None),
            P(),
        ),
        out_specs=P("row", "col", None, None),
        check_vma=False,
    )
```

time: 70.7 us -> 56.6 us (0.80)
  the two profiles are of different devices: /device:TPU:655 before, /device:TPU:127 now
where the time goes in v1:
time: 56.6 us; the launch traced here: 56.2 us
  starting transfers between devices  30.1 us (53%)
  waiting for transfers between devices  12.5 us (22%)
  Pallas kernels  8.92 us (16%)
  local copies, waits for them, and re-layouts  3.48 us (6%)
  other arithmetic  1.06 us (2%)
    ppermute x1, starting transfers between devices, on_device(): kvb = lax.ppermute(jnp.stack([k, v]), 'row', far)  12.7 us
    pallas_call x4, Pallas kernels, call(): pl.pallas_call(body, out_shape=outs, in_specs=specs, out_specs=[VMEM] * l...  8.92 us
    ppermute x1, waiting for transfers between devices, on_device(): in_d = lax.ppermute(out_d, 'col', beyond)  4.82 us
    ppermute x1, waiting for transfers between devices, on_device(): va = lax.ppermute(v, 'row', near)  4.21 us
    ppermute x1, starting transfers between devices, on_device(): qd = lax.ppermute(q, 'col', beyond)  3.71 us
    unnamed x10, local copies, waits for them, and re-layouts  3.48 us
    ppermute x1, starting transfers between devices, on_device(): va = lax.ppermute(v, 'row', near)  3.36 us
    ppermute x1, waiting for transfers between devices, on_device(): ka = lax.ppermute(k, 'row', near)  3.11 us
  transfers between devices with their start and end apart: 7, of which 4 were waited for; matrix products, arithmetic and copies ran while one was open for 0% of the time, Pallas kernels for 8%

profile of v1, /device:TPU:127, one launch (start us, length us, event | category | flops | bytes accessed | tf_op | source)
XLA Modules:
  0.0 56.2 jit_solution(18007657735133998428)
XLA Ops:
  0.0 1.1 %pad_maximum_fusion = bf16[2,128,768]{2,1,0:T(8,128)(2,1)S(1)} fusion(bf16[1,128,768]{2,1,0:T(8,128)(2,1)} %bitcast.10, bf16[1,128,768]{2,1,0:T(8,128)(2,1)} %bitcast.13), kind=kLoop, calls=%fused_computation | loop fusion | flops 196608 | bytes 786432 | tf_op jit(solution)/shard_map/stack | solution.py:206
  1.1 12.7 %collective-permute-start = (bf16[2,128,768]{2,1,0:T(8,128)(2,1)S(1)}, bf16[2,128,768]{2,1,0:T(8,128)(2,1)S(1)}, u32[]{:S(2)}, u32[]{:S(2)}) collective-permute-start(bf16[2,128,768]{2,1,0:T(8,128)(2,1)S(1)} %pad_maximum_fusion), channel_id=1, source_target_pairs={{64,128},{128,64},{192,256},{256,192},{320,384},{384,320},{448,512... | collective-permute-start | bytes 1179656 | tf_op jit(solution)/shard_map/ppermute | solution.py:206
  13.8 2.9 %collective-permute-start.1 = (bf16[128,768]{1,0:T(8,128)(2,1)}, bf16[128,768]{1,0:T(8,128)(2,1)S(1)}, u32[]{:S(2)}, u32[]{:S(2)}) collective-permute-start(bf16[128,768]{1,0:T(8,128)(2,1)} %bitcast.6), channel_id=1, source_target_pairs={{0,1},{1,0},{2,3},{3,2},{4,5},{5,4},{6,7},{7,6},{8,9},{9,8},{10,11... | collective-permute-start | bytes 589832 | tf_op jit(solution)/shard_map/ppermute | solution.py:208
  16.6 3.7 %collective-permute-start.2 = (bf16[128,768]{1,0:T(8,128)(2,1)}, bf16[128,768]{1,0:T(8,128)(2,1)S(1)}, u32[]{:S(2)}, u32[]{:S(2)}) collective-permute-start(bf16[128,768]{1,0:T(8,128)(2,1)} %bitcast.7), channel_id=1, source_target_pairs={{1,2},{2,1},{3,4},{4,3},{5,6},{6,5},{7,8},{8,7},{9,10},{10,9},{11,... | collective-permute-start | bytes 589832 | tf_op jit(solution)/shard_map/ppermute | solution.py:207
  20.3 1.9 %collective-permute-start.3 = (bf16[128,768]{1,0:T(8,128)(2,1)}, bf16[128,768]{1,0:T(8,128)(2,1)S(1)}, u32[]{:S(2)}, u32[]{:S(2)}) collective-permute-start(bf16[128,768]{1,0:T(8,128)(2,1)} %bitcast.14), channel_id=1, source_target_pairs={{0,64},{64,0},{128,192},{192,128},{256,320},{320,256},{384,448},{4... | collective-permute-start | bytes 589832 | tf_op jit(solution)/shard_map/ppermute | solution.py:209
  22.3 3.4 %collective-permute-start.4 = (bf16[128,768]{1,0:T(8,128)(2,1)}, bf16[128,768]{1,0:T(8,128)(2,1)S(1)}, u32[]{:S(2)}, u32[]{:S(2)}) collective-permute-start(bf16[128,768]{1,0:T(8,128)(2,1)} %bitcast.11), channel_id=1, source_target_pairs={{0,64},{64,0},{128,192},{192,128},{256,320},{320,256},{384,448},{4... | collective-permute-start | bytes 589832 | tf_op jit(solution)/shard_map/ppermute | solution.py:210
  25.6 0.0 collective-permute-done.1.qc
  25.7 0.4 collective-permute-done.2.qd
  26.1 3.1 %collective-permute-done.3.ka = bf16[128,768]{1,0:T(8,128)(2,1)S(1)} collective-permute-done((bf16[128,768]{1,0:T(8,128)(2,1)}, bf16[128,768]{1,0:T(8,128)(2,1)S(1)}, u32[]{:S(2)}, u32[]{:S(2)}) %collective-permute-start.3) | collective-permute-done | bytes 196640 | tf_op jit(solution)/shard_map/ppermute | solution.py:209
  29.2 4.2 %collective-permute-done.4.va = bf16[128,768]{1,0:T(8,128)(2,1)S(1)} collective-permute-done((bf16[128,768]{1,0:T(8,128)(2,1)}, bf16[128,768]{1,0:T(8,128)(2,1)S(1)}, u32[]{:S(2)}, u32[]{:S(2)}) %collective-permute-start.4) | collective-permute-done | bytes 196640 | tf_op jit(solution)/shard_map/ppermute | solution.py:210
  33.4 0.0 copy-start
  33.4 0.9 %copy-done = bf16[1,1,128,768]{3,2,1,0:T(8,128)(2,1)S(1)} copy-done((bf16[1,1,128,768]{3,2,1,0:T(8,128)(2,1)S(1)}, bf16[1,1,128,768]{3,2,1,0:T(8,128)(2,1)}, u32[]{:S(2)}) %copy-start) | copy-done | bytes 196632
  34.3 0.0 copy-start.2
  34.3 0.9 %copy-done.2 = bf16[1,1,128,768]{3,2,1,0:T(8,128)(2,1)S(1)} copy-done((bf16[1,1,128,768]{3,2,1,0:T(8,128)(2,1)S(1)}, bf16[1,1,128,768]{3,2,1,0:T(8,128)(2,1)}, u32[]{:S(2)}) %copy-start.2) | copy-done | bytes 196632
  35.2 0.0 copy-start.3
  35.2 0.9 %copy-done.3 = bf16[1,1,128,768]{3,2,1,0:T(8,128)(2,1)S(1)} copy-done((bf16[1,1,128,768]{3,2,1,0:T(8,128)(2,1)S(1)}, bf16[1,1,128,768]{3,2,1,0:T(8,128)(2,1)}, u32[]{:S(2)}) %copy-start.3) | copy-done | bytes 196632
  36.2 0.0 copy-start.4
  36.2 0.7 %copy-done.4 = s32[16,64]{1,0:T(8,128)S(1)} copy-done((s32[16,64]{1,0:T(8,128)S(1)}, s32[16,64]{1,0:T(8,128)}, u32[]{:S(2)}) %copy-start.4) | copy-done | bytes 4120
  36.9 2.7 %early.1 = (f32[3,128,768]{2,1,0:T(8,128)S(1)}, f32[3,128,768]{2,1,0:T(8,128)S(1)}, f32[3,128,768]{2,1,0:T(8,128)S(1)}) custom-call(s32[16,64]{1,0:T(8,128)S(1)} %copy-done.4, bf16[128,768]{1,0:T(8,128)(2,1)S(1)} %bitcast.8, bf16[128,768]{1,0:T(8,128)(2,1)S(1)} %collective-permute-done.1.qc, bf16[128,768]{1,0:T(8,128)(2,1)S(1)} %collective-permute-done.2.qd, ...), custom_call_target="tpu_custom_call" | custom-call | flops 6 | bytes 1024 | tf_op jit(solution)/shard_map/early/pallas_call | solution.py:182
  39.5 0.0 collective-permute-done.kvb
  39.6 0.0 copy-start.1
  39.6 2.4 %side.1 = (bf16[128,896]{1,0:T(8,128)(2,1)S(1)}, bf16[128,896]{1,0:T(8,128)(2,1)S(1)}) custom-call(s32[16,64]{1,0:T(8,128)S(1)} %copy-done.4, bf16[128,768]{1,0:T(8,128)(2,1)S(1)} %collective-permute-done.1.qc, bf16[128,768]{1,0:T(8,128)(2,1)S(1)} %collective-permute-done.2.qd, bf16[2,128,768]{2,1,0:T(8,128)(2,1)S(1)} %collective-permute-done.kvb, ...), custom_call_target="tpu_custom_call" | custom-call | flops 2 | bytes 1024 | tf_op jit(solution)/shard_map/side/pallas_call | solution.py:182
  42.0 2.5 %collective-permute-start.5 = (bf16[128,896]{1,0:T(8,128)(2,1)S(1)}, bf16[128,896]{1,0:T(8,128)(2,1)S(1)}, u32[]{:S(2)}, u32[]{:S(2)}) collective-permute-start(bf16[128,896]{1,0:T(8,128)(2,1)S(1)} %get-tuple-element.19), channel_id=1, source_target_pairs={{0,1},{1,0},{2,3},{3,2},{4,5},{5,4},{6,7},{7,6},{8,9},{9,8},{10,11... | collective-permute-start | bytes 688136 | tf_op jit(solution)/shard_map/ppermute | solution.py:216
  44.5 3.0 %collective-permute-start.6 = (bf16[128,896]{1,0:T(8,128)(2,1)S(1)}, bf16[128,896]{1,0:T(8,128)(2,1)S(1)}, u32[]{:S(2)}, u32[]{:S(2)}) collective-permute-start(bf16[128,896]{1,0:T(8,128)(2,1)S(1)} %get-tuple-element.20), channel_id=1, source_target_pairs={{1,2},{2,1},{3,4},{4,3},{5,6},{6,5},{7,8},{8,7},{9,10},{10,9},{11,... | collective-permute-start | bytes 688136 | tf_op jit(solution)/shard_map/ppermute | solution.py:215
  47.5 0.0 copy-done.1
  47.5 1.6 %own.1 = (f32[128,768]{1,0:T(8,128)S(1)}, f32[128,128]{1,0:T(8,128)S(1)}, f32[128,128]{1,0:T(8,128)S(1)}) custom-call(s32[16,64]{1,0:T(8,128)S(1)} %copy-done.4, bf16[128,768]{1,0:T(8,128)(2,1)S(1)} %bitcast.9, bf16[2,128,768]{2,1,0:T(8,128)(2,1)S(1)} %collective-permute-done.kvb, f32[3,128,768]{2,1,0:T(8,128)S(1)} %get-tuple-element.13.top, ...), custom_call_target="tpu_custom_call" | custom-call | flops 1 | bytes 1024 | tf_op jit(solution)/shard_map/own/pallas_call | solution.py:182
  49.1 0.0 collective-permute-done.5.in_c
  49.1 4.8 %collective-permute-done.6.in_d = bf16[128,896]{1,0:T(8,128)(2,1)S(1)} collective-permute-done((bf16[128,896]{1,0:T(8,128)(2,1)S(1)}, bf16[128,896]{1,0:T(8,128)(2,1)S(1)}, u32[]{:S(2)}, u32[]{:S(2)}) %collective-permute-start.6) | collective-permute-done | bytes 229408 | tf_op jit(solution)/shard_map/ppermute | solution.py:215
  54.0 2.2 %merge.1 = bf16[128,768]{1,0:T(8,128)(2,1)} custom-call(s32[16,64]{1,0:T(8,128)S(1)} %copy-done.4, f32[128,768]{1,0:T(8,128)S(1)} %get-tuple-element.16.mix, f32[128,128]{1,0:T(8,128)S(1)} %get-tuple-element.17.top, f32[128,128]{1,0:T(8,128)S(1)} %get-tuple-element.18.tot, bf16[128,896]{1,0:T(8,128)(2,1)S(1)} %collective-permute-done.5.in_c, ...), custom_call_target="tpu_custom_call" | custom-call | bytes 1024 | tf_op jit(solution)/shard_map/merge/pallas_call | solution.py:182
Async XLA Ops:
  1.1 38.5 %collective-permute-start = (bf16[2,128,768]{2,1,0:T(8,128)(2,1)S(1)}, bf16[2,128,768]{2,1,0:T(8,128)(2,1)S(1)}, u32[]{:S(2)}, u32[]{:S(2)}) collective-permute-start(bf16[2,128,768]{2,1,0:T(8,128)(2,1)S(1)} %pad_maximum_fusion), channel_id=1, source_target_pairs={{64,128},{128,64},{192,256},{256,192},{320,384},{384,320},{448,512... | collective-permute-start | bytes 1179656 | tf_op jit(solution)/shard_map/ppermute | solution.py:206
  13.8 11.9 %collective-permute-start.1 = (bf16[128,768]{1,0:T(8,128)(2,1)}, bf16[128,768]{1,0:T(8,128)(2,1)S(1)}, u32[]{:S(2)}, u32[]{:S(2)}) collective-permute-start(bf16[128,768]{1,0:T(8,128)(2,1)} %bitcast.6), channel_id=1, source_target_pairs={{0,1},{1,0},{2,3},{3,2},{4,5},{5,4},{6,7},{7,6},{8,9},{9,8},{10,11... | collective-permute-start | bytes 589832 | tf_op jit(solution)/shard_map/ppermute | solution.py:208
  16.6 9.4 %collective-permute-start.2 = (bf16[128,768]{1,0:T(8,128)(2,1)}, bf16[128,768]{1,0:T(8,128)(2,1)S(1)}, u32[]{:S(2)}, u32[]{:S(2)}) collective-permute-start(bf16[128,768]{1,0:T(8,128)(2,1)} %bitcast.7), channel_id=1, source_target_pairs={{1,2},{2,1},{3,4},{4,3},{5,6},{6,5},{7,8},{8,7},{9,10},{10,9},{11,... | collective-permute-start | bytes 589832 | tf_op jit(solution)/shard_map/ppermute | solution.py:207
  20.3 8.8 %collective-permute-start.3 = (bf16[128,768]{1,0:T(8,128)(2,1)}, bf16[128,768]{1,0:T(8,128)(2,1)S(1)}, u32[]{:S(2)}, u32[]{:S(2)}) collective-permute-start(bf16[128,768]{1,0:T(8,128)(2,1)} %bitcast.14), channel_id=1, source_target_pairs={{0,64},{64,0},{128,192},{192,128},{256,320},{320,256},{384,448},{4... | collective-permute-start | bytes 589832 | tf_op jit(solution)/shard_map/ppermute | solution.py:209
  22.3 11.1 %collective-permute-start.4 = (bf16[128,768]{1,0:T(8,128)(2,1)}, bf16[128,768]{1,0:T(8,128)(2,1)S(1)}, u32[]{:S(2)}, u32[]{:S(2)}) collective-permute-start(bf16[128,768]{1,0:T(8,128)(2,1)} %bitcast.11), channel_id=1, source_target_pairs={{0,64},{64,0},{128,192},{192,128},{256,320},{320,256},{384,448},{4... | collective-permute-start | bytes 589832 | tf_op jit(solution)/shard_map/ppermute | solution.py:210
  33.4 0.9 %copy-start = (bf16[1,1,128,768]{3,2,1,0:T(8,128)(2,1)S(1)}, bf16[1,1,128,768]{3,2,1,0:T(8,128)(2,1)}, u32[]{:S(2)}) copy-start(bf16[1,1,128,768]{3,2,1,0:T(8,128)(2,1)} %param.4) | copy-start | bytes 589828
  34.3 0.9 %copy-start.2 = (bf16[1,1,128,768]{3,2,1,0:T(8,128)(2,1)S(1)}, bf16[1,1,128,768]{3,2,1,0:T(8,128)(2,1)}, u32[]{:S(2)}) copy-start(bf16[1,1,128,768]{3,2,1,0:T(8,128)(2,1)} %param.6) | copy-start | bytes 589828
  35.2 0.9 %copy-start.3 = (bf16[1,1,128,768]{3,2,1,0:T(8,128)(2,1)S(1)}, bf16[1,1,128,768]{3,2,1,0:T(8,128)(2,1)}, u32[]{:S(2)}) copy-start(bf16[1,1,128,768]{3,2,1,0:T(8,128)(2,1)} %param.5) | copy-start | bytes 589828
  36.2 0.7 %copy-start.4 = (s32[16,64]{1,0:T(8,128)S(1)}, s32[16,64]{1,0:T(8,128)}, u32[]{:S(2)}) copy-start(s32[16,64]{1,0:T(8,128)} %tissue.7) | copy-start | bytes 12292
  39.6 8.0 %copy-start.1 = (bf16[1,1,128,768]{3,2,1,0:T(8,128)(2,1)S(1)}, bf16[1,1,128,768]{3,2,1,0:T(8,128)(2,1)}, u32[]{:S(2)}) copy-start(bf16[1,1,128,768]{3,2,1,0:T(8,128)(2,1)} %param.4) | copy-start | bytes 589828
  42.0 7.1 %collective-permute-start.5 = (bf16[128,896]{1,0:T(8,128)(2,1)S(1)}, bf16[128,896]{1,0:T(8,128)(2,1)S(1)}, u32[]{:S(2)}, u32[]{:S(2)}) collective-permute-start(bf16[128,896]{1,0:T(8,128)(2,1)S(1)} %get-tuple-element.19), channel_id=1, source_target_pairs={{0,1},{1,0},{2,3},{3,2},{4,5},{5,4},{6,7},{7,6},{8,9},{9,8},{10,11... | collective-permute-start | bytes 688136 | tf_op jit(solution)/shard_map/ppermute | solution.py:216
  44.5 9.4 %collective-permute-start.6 = (bf16[128,896]{1,0:T(8,128)(2,1)S(1)}, bf16[128,896]{1,0:T(8,128)(2,1)S(1)}, u32[]{:S(2)}, u32[]{:S(2)}) collective-permute-start(bf16[128,896]{1,0:T(8,128)(2,1)S(1)} %get-tuple-element.20), channel_id=1, source_target_pairs={{1,2},{2,1},{3,4},{4,3},{5,6},{6,5},{7,8},{8,7},{9,10},{10,9},{11,... | collective-permute-start | bytes 688136 | tf_op jit(solution)/shard_map/ppermute | solution.py:215

commit v2 on v1

--- a/solution.py
+++ b/solution.py
@@ -18,6 +18,7 @@
 NEG = -1e30
 FLOOR = -1e20
 VMEM = pl.BlockSpec(memory_space=pltpu.VMEM)
+ANY = pl.BlockSpec(memory_space=pl.ANY)
 SMEM = pl.BlockSpec(memory_space=pltpu.SMEM)
 F32 = jnp.float32
 BF16 = jnp.bfloat16
@@ -75,16 +76,30 @@
     return slice(p * PAIR, (p + 1) * PAIR)
 
 
-def early_kernel(tissue, q, qc, qd, k, v, ka, va, top_ref, tot_ref, mix_ref):
+def early_kernel(cols, tissue, q_hbm, qd, qc, k_hbm, v_hbm, kva, top_ref, tot_ref, mix_ref, flags, q, k, v, sems):
+    copies = [
+        pltpu.make_async_copy(source, target, sems.at[n])
+        for n, (source, target) in enumerate(((q_hbm, q), (k_hbm, k), (v_hbm, v)))
+    ]
+    for copy in copies:
+        copy.start()
     row, col = position()
     low = lane_low()
     own = tile_bias(tissue, row, col)
     near = tile_bias(tissue, partner(row, False), col)
-    for i, query in enumerate((q, qc, qd)):
-        for p in range(PAIRS):
-            at = lanes(p)
+    far = tile_bias(tissue, partner(row, True), col)
+    other = partner(col, True)
+    missing = jnp.where((other >= 0) & (other < cols), 0.0, NEG).astype(F32)
+    shown = jnp.where(tissue[row, col] > 0, 1.0, 0.0).astype(F32)
+    for n, value in enumerate((far, missing, shown)):
+        flags[n : n + 1, :] = jnp.full((1, PAIR), value, F32)
+    for copy in copies:
+        copy.wait()
+    for p in range(PAIRS):
+        at = lanes(p)
+        for i, query in enumerate((q, qc, qd)):
             t, l, m = attend_pair(
-                query[:, at], (k[:, at], ka[:, at]), (v[:, at], va[:, at]),
+                query[:, at], (k[:, at], kva[:TOK, at]), (v[:, at], kva[TOK:, at]),
                 (None if i == 0 else own, near), low,
             )
             top_ref[i, :, at] = t
@@ -94,7 +109,7 @@
 
 def late_part(query, kvb, bias, top, tot, mix, i, p, low):
     at = lanes(p)
-    t, l, m = attend_pair(query[:, at], (kvb[0, :, at],), (kvb[1, :, at],), (bias,), low)
+    t, l, m = attend_pair(query[:, at], (kvb[:TOK, at],), (kvb[TOK : 2 * TOK, at],), (bias,), low)
     t0 = top[i, :, at]
     best = jnp.maximum(t, t0)
     new, old = jnp.exp2(t - best), jnp.exp2(t0 - best)
@@ -114,10 +129,9 @@
     return parts
 
 
-def side_kernel(tissue, qc, qd, kvb, top, tot, mix, out_c, out_d):
-    row, col = position()
-    low = lane_low()
-    bias = tile_bias(tissue, partner(row, True), col)
+def side_kernel(flags, qd, qc, kvb, top, tot, mix, out_d, out_c):
+    low = lane_low()
+    bias = flags[0:1, :]
     for i, (query, out) in enumerate(((qc, out_c), (qd, out_d))):
         stats = jnp.zeros((TOK, PAIR), F32)
         for p in range(PAIRS):
@@ -128,10 +142,9 @@
         out[:, HD:] = stats.astype(BF16)
 
 
-def own_kernel(tissue, q, kvb, top, tot, mix, mix_out, top_out, tot_out):
-    row, col = position()
-    low = lane_low()
-    bias = tile_bias(tissue, partner(row, True), col)
+def own_kernel(flags, q, kvb, top, tot, mix, mix_out, top_out, tot_out):
+    low = lane_low()
+    bias = flags[0:1, :]
     tops = jnp.zeros((TOK, PAIR), F32)
     tots = jnp.ones((TOK, PAIR), F32)
     for p in range(PAIRS):
@@ -143,12 +156,9 @@
     tot_out[...] = tots
 
 
-def merge_kernel(cols, tissue, mix, top, tot, in_c, in_d, out):
-    row, col = position()
-    low = lane_low()
-    own = jnp.where(tissue[row, col] > 0, 1.0, 0.0).astype(F32)
-    other = partner(col, True)
-    missing = jnp.where((other >= 0) & (other < cols), 0.0, NEG).astype(F32)
+def merge_kernel(flags, mix, top, tot, in_d, in_c, out):
+    low = lane_low()
+    missing, own = flags[1:2, :], flags[2:3, :]
     tops, tots = [top[...]], [tot[...]]
     for part, gap in ((in_c, None), (in_d, missing)):
         stats = part[:, HD:].astype(F32)
@@ -175,22 +185,16 @@
         out[:, at] = acc.astype(BF16)
 
 
-def call(body, outs, name, units, *args):
-    specs = [SMEM] + [VMEM] * (len(args) - 1)
-    moved = sum(a.size * a.dtype.itemsize for a in args)
-    moved += sum(o.size * o.dtype.itemsize for o in outs)
+def call(body, outs, name, specs, *args, scratch=()):
     return pl.pallas_call(
         body,
         out_shape=outs,
         in_specs=specs,
         out_specs=[VMEM] * len(outs),
+        scratch_shapes=scratch,
         name=name,
         compiler_params=pltpu.CompilerParams(vmem_limit_bytes=16 << 20),
-        cost_estimate=pl.CostEstimate(
-            flops=units,
-            transcendentals=0,
-            bytes_accessed=1024,
-        ),
+        cost_estimate=pl.CostEstimate(flops=1, transcendentals=0, bytes_accessed=1024),
     )(*args)
 
 
@@ -203,22 +207,24 @@
     rows, cols = tissue.shape
     far, near = swaps(rows, 1), swaps(rows, 0)
     beyond, beside = swaps(cols, 1), swaps(cols, 0)
-    kvb = lax.ppermute(jnp.stack([k, v]), "row", far)
+    kvb = lax.ppermute(jnp.concatenate([k, v, jnp.zeros((8, HD), BF16)]), "row", far)
+    kva = lax.ppermute(jnp.concatenate([k, v]), "row", near)
     qd = lax.ppermute(q, "col", beyond)
     qc = lax.ppermute(q, "col", beside)
-    ka = lax.ppermute(k, "row", near)
-    va = lax.ppermute(v, "row", near)
-    state = [shaped(3, TOK, HD)] * 3
-    top, tot, mix = call(early_kernel, state, "early", 6, tissue, q, qc, qd, k, v, ka, va)
+    outs = [shaped(3, TOK, HD)] * 3 + [shaped(8, PAIR)]
+    staged = [pltpu.VMEM((TOK, HD), BF16)] * 3 + [pltpu.SemaphoreType.DMA((3,))]
+    top, tot, mix, flags = call(
+        functools.partial(early_kernel, cols), outs, "early", [SMEM, ANY, VMEM, VMEM, ANY, ANY, VMEM],
+        tissue, q, qd, qc, k, v, kva, scratch=staged,
+    )
     pack = shaped(TOK, HD + PAIR, dtype=BF16)
-    out_c, out_d = call(side_kernel, [pack] * 2, "side", 2, tissue, qc, qd, kvb, top, tot, mix)
+    out_d, out_c = call(side_kernel, [pack] * 2, "side", [VMEM] * 7, flags, qd, qc, kvb, top, tot, mix)
     in_d = lax.ppermute(out_d, "col", beyond)
     in_c = lax.ppermute(out_c, "col", beside)
     own = [shaped(TOK, HD), shaped(TOK, PAIR), shaped(TOK, PAIR)]
-    mix, top, tot = call(own_kernel, own, "own", 1, tissue, q, kvb, top, tot, mix)
+    mix, top, tot = call(own_kernel, own, "own", [VMEM] * 6, flags, q, kvb, top, tot, mix)
     (out,) = call(
-        functools.partial(merge_kernel, cols), [shaped(TOK, HD, dtype=BF16)], "merge", 0,
-        tissue, mix, top, tot, in_c, in_d,
+        merge_kernel, [shaped(TOK, HD, dtype=BF16)], "merge", [VMEM] * 6, flags, mix, top, tot, in_d, in_c
     )
     return out.reshape(1, 1, TOK, HD)
 

time: 56.6 us -> 43.7 us (0.77)
  the two profiles are of different devices: /device:TPU:127 before, /device:TPU:240 now
where the time goes in v2:
time: 43.7 us; the launch traced here: 43.4 us
  starting transfers between devices  24.6 us (56%)
  waiting for transfers between devices  8.58 us (20%)
  Pallas kernels  7.7 us (18%)
  other arithmetic  2.3 us (5%)
    ppermute x1, starting transfers between devices, on_device(): lax.ppermute(jnp.concatenate([k, v, jnp.zeros((8, HD), BF16)]), 'row', far)  12.1 us
    pallas_call x4, Pallas kernels, call(): pl.pallas_call(body, out_shape=outs, in_specs=specs, out_specs=[VMEM] * l...  7.7 us
    ppermute x1, waiting for transfers between devices, on_device(): qd = lax.ppermute(q, 'col', beyond)  5.27 us
    ppermute x1, starting transfers between devices, on_device(): in_c = lax.ppermute(out_c, 'col', beside)  3.3 us
    ppermute x1, waiting for transfers between devices, on_device(): in_d = lax.ppermute(out_d, 'col', beyond)  3.29 us
    ppermute x1, starting transfers between devices, on_device(): qd = lax.ppermute(q, 'col', beyond)  3.02 us
    ppermute x1, starting transfers between devices, on_device(): qc = lax.ppermute(q, 'col', beside)  2.4 us
    ppermute x1, starting transfers between devices, on_device(): in_d = lax.ppermute(out_d, 'col', beyond)  1.92 us
  transfers between devices with their start and end apart: 6, of which 2 were waited for; matrix products, arithmetic and copies ran while one was open for 2% of the time, Pallas kernels for 10%

profile of v2, /device:TPU:240, one launch (start us, length us, event | category | flops | bytes accessed | tf_op | source)
XLA Modules:
  0.0 43.4 jit_solution(964889356217747806)
XLA Ops:
  0.0 0.0 copy-start
  0.0 0.0 copy-start.1
  0.0 0.0 copy-start.2
  0.0 0.0 copy-start.3
  0.0 1.3 %maximum_maximum_fusion = bf16[264,768]{1,0:T(8,128)(2,1)S(1)} fusion(bf16[128,768]{1,0:T(8,128)(2,1)} %bitcast.7, bf16[128,768]{1,0:T(8,128)(2,1)} %bitcast.4, bf16[264]{0:T(512)(128)(2,1)S(1)} %pad.2.clone), kind=kLoop, calls=%fused_computation | loop fusion | flops 1216512 | bytes 799248 | tf_op jit(solution)/shard_map/concatenate | solution.py:210
  1.3 12.1 %collective-permute-start.3 = (bf16[264,768]{1,0:T(8,128)(2,1)S(1)}, bf16[264,768]{1,0:T(8,128)(2,1)S(1)}, u32[]{:S(2)}, u32[]{:S(2)}) collective-permute-start(bf16[264,768]{1,0:T(8,128)(2,1)S(1)} %maximum_maximum_fusion), channel_id=1, source_target_pairs={{64,128},{128,64},{192,256},{256,192},{320,384},{384,320},{448,512... | collective-permute-start | bytes 1216520 | tf_op jit(solution)/shard_map/ppermute | solution.py:210
  13.4 1.1 %pad_maximum_fusion = bf16[256,768]{1,0:T(8,128)(2,1)S(1)} fusion(bf16[128,768]{1,0:T(8,128)(2,1)} %bitcast.8, bf16[128,768]{1,0:T(8,128)(2,1)} %bitcast.5), kind=kLoop, calls=%fused_computation.1 | loop fusion | flops 786432 | bytes 786432 | tf_op jit(solution)/shard_map/concatenate | solution.py:211
  14.4 1.9 %collective-permute-start.2 = (bf16[256,768]{1,0:T(8,128)(2,1)S(1)}, bf16[256,768]{1,0:T(8,128)(2,1)S(1)}, u32[]{:S(2)}, u32[]{:S(2)}) collective-permute-start(bf16[256,768]{1,0:T(8,128)(2,1)S(1)} %pad_maximum_fusion), channel_id=1, source_target_pairs={{0,64},{64,0},{128,192},{192,128},{256,320},{320,256},{384,448},{4... | collective-permute-start | bytes 1179656 | tf_op jit(solution)/shard_map/ppermute | solution.py:211
  16.4 0.0 copy-done.2
  16.4 3.0 %collective-permute-start = (bf16[128,768]{1,0:T(8,128)(2,1)S(1)}, bf16[128,768]{1,0:T(8,128)(2,1)S(1)}, u32[]{:S(2)}, u32[]{:S(2)}) collective-permute-start(bf16[128,768]{1,0:T(8,128)(2,1)S(1)} %bitcast.10), channel_id=1, source_target_pairs={{1,2},{2,1},{3,4},{4,3},{5,6},{6,5},{7,8},{8,7},{9,10},{10,9},{11,... | collective-permute-start | bytes 589832 | tf_op jit(solution)/shard_map/ppermute | solution.py:212
  19.4 2.4 %collective-permute-start.1 = (bf16[128,768]{1,0:T(8,128)(2,1)S(1)}, bf16[128,768]{1,0:T(8,128)(2,1)S(1)}, u32[]{:S(2)}, u32[]{:S(2)}) collective-permute-start(bf16[128,768]{1,0:T(8,128)(2,1)S(1)} %bitcast.11), channel_id=1, source_target_pairs={{0,1},{1,0},{2,3},{3,2},{4,5},{5,4},{6,7},{7,6},{8,9},{9,8},{10,11... | collective-permute-start | bytes 589832 | tf_op jit(solution)/shard_map/ppermute | solution.py:213
  21.8 5.3 %collective-permute-done.qd = bf16[128,768]{1,0:T(8,128)(2,1)S(1)} collective-permute-done((bf16[128,768]{1,0:T(8,128)(2,1)S(1)}, bf16[128,768]{1,0:T(8,128)(2,1)S(1)}, u32[]{:S(2)}, u32[]{:S(2)}) %collective-permute-start) | collective-permute-done | bytes 196640 | tf_op jit(solution)/shard_map/ppermute | solution.py:212
  27.1 0.0 collective-permute-done.1.qc
  27.1 0.0 collective-permute-done.2.kva
  27.1 0.0 copy-done
  27.1 0.0 copy-done.1
  27.1 0.0 copy-done.3
  27.1 3.5 %early.1 = (f32[3,128,768]{2,1,0:T(8,128)S(1)}, f32[3,128,768]{2,1,0:T(8,128)S(1)}, f32[3,128,768]{2,1,0:T(8,128)S(1)}, f32[8,128]{1,0:T(8,128)S(1)}) custom-call(s32[16,64]{1,0:T(8,128)S(1)} %copy-done.3, bf16[128,768]{1,0:T(8,128)(2,1)S(1)} %bitcast.12, bf16[128,768]{1,0:T(8,128)(2,1)S(1)} %collective-permute-done.qd, ...), custom_call_target="tpu_custom_call" | custom-call | flops 1 | bytes 1024 | tf_op jit(solution)/shard_map/early/pallas_call | solution.py:189
  30.6 0.0 collective-permute-done.3.kvb
  30.6 1.8 %side.1 = (bf16[128,896]{1,0:T(8,128)(2,1)S(1)}, bf16[128,896]{1,0:T(8,128)(2,1)S(1)}) custom-call(f32[8,128]{1,0:T(8,128)S(1)} %get-tuple-element.14.flags, bf16[128,768]{1,0:T(8,128)(2,1)S(1)} %collective-permute-done.qd, bf16[128,768]{1,0:T(8,128)(2,1)S(1)} %collective-permute-done.1.qc, bf16[264,768]{1,0:T(8,128)(2,1)S(1)} %collective-permute-done.3.kvb, ...), custom_call_target="tpu_custom_call" | custom-call | flops 1 | bytes 1024 | tf_op jit(solution)/shard_map/side/pallas_call | solution.py:189
  32.4 1.9 %collective-permute-start.4 = (bf16[128,896]{1,0:T(8,128)(2,1)S(1)}, bf16[128,896]{1,0:T(8,128)(2,1)S(1)}, u32[]{:S(2)}, u32[]{:S(2)}) collective-permute-start(bf16[128,896]{1,0:T(8,128)(2,1)S(1)} %get-tuple-element.21), channel_id=1, source_target_pairs={{1,2},{2,1},{3,4},{4,3},{5,6},{6,5},{7,8},{8,7},{9,10},{10,9},{11,... | collective-permute-start | bytes 688136 | tf_op jit(solution)/shard_map/ppermute | solution.py:222
  34.3 3.3 %collective-permute-start.5 = (bf16[128,896]{1,0:T(8,128)(2,1)S(1)}, bf16[128,896]{1,0:T(8,128)(2,1)S(1)}, u32[]{:S(2)}, u32[]{:S(2)}) collective-permute-start(bf16[128,896]{1,0:T(8,128)(2,1)S(1)} %get-tuple-element.22), channel_id=1, source_target_pairs={{0,1},{1,0},{2,3},{3,2},{4,5},{5,4},{6,7},{7,6},{8,9},{9,8},{10,11... | collective-permute-start | bytes 688136 | tf_op jit(solution)/shard_map/ppermute | solution.py:223
  37.6 0.9 %own.1 = (f32[128,768]{1,0:T(8,128)S(1)}, f32[128,128]{1,0:T(8,128)S(1)}, f32[128,128]{1,0:T(8,128)S(1)}) custom-call(f32[8,128]{1,0:T(8,128)S(1)} %get-tuple-element.14.flags, bf16[128,768]{1,0:T(8,128)(2,1)S(1)} %bitcast.13, bf16[264,768]{1,0:T(8,128)(2,1)S(1)} %collective-permute-done.3.kvb, f32[3,128,768]{2,1,0:T(8,128)S(1)} %get-tuple-element.15.top, ...), custom_call_target="tpu_custom_call" | custom-call | flops 1 | bytes 1024 | tf_op jit(solution)/shard_map/own/pallas_call | solution.py:189
  38.5 3.3 %collective-permute-done.4.in_d = bf16[128,896]{1,0:T(8,128)(2,1)S(1)} collective-permute-done((bf16[128,896]{1,0:T(8,128)(2,1)S(1)}, bf16[128,896]{1,0:T(8,128)(2,1)S(1)}, u32[]{:S(2)}, u32[]{:S(2)}) %collective-permute-start.4) | collective-permute-done | bytes 229408 | tf_op jit(solution)/shard_map/ppermute | solution.py:222
  41.8 0.0 collective-permute-done.5.in_c
  41.8 1.6 %merge.1 = bf16[128,768]{1,0:T(8,128)(2,1)} custom-call(f32[8,128]{1,0:T(8,128)S(1)} %get-tuple-element.14.flags, f32[128,768]{1,0:T(8,128)S(1)} %get-tuple-element.18.mix, f32[128,128]{1,0:T(8,128)S(1)} %get-tuple-element.19.top, f32[128,128]{1,0:T(8,128)S(1)} %get-tuple-element.20.tot, bf16[128,896]{1,0:T(8,128)(2,1)S(1)} %collective-permute-done.4.in_d, ...), custom_call_target="tpu_custom_call" | custom-call | flops 1 | bytes 1024 | tf_op jit(solution)/shard_map/merge/pallas_call | solution.py:189
  (2 shorter events, 0.0 us)
Async XLA Ops:
  0.0 27.1 %copy-start = (bf16[1,1,128,768]{3,2,1,0:T(8,128)(2,1)S(1)}, bf16[1,1,128,768]{3,2,1,0:T(8,128)(2,1)}, u32[]{:S(2)}) copy-start(bf16[1,1,128,768]{3,2,1,0:T(8,128)(2,1)} %param.5) | copy-start | bytes 589828
  0.0 27.1 %copy-start.1 = (bf16[1,1,128,768]{3,2,1,0:T(8,128)(2,1)S(1)}, bf16[1,1,128,768]{3,2,1,0:T(8,128)(2,1)}, u32[]{:S(2)}) copy-start(bf16[1,1,128,768]{3,2,1,0:T(8,128)(2,1)} %param.6) | copy-start | bytes 589828
  0.0 16.4 %copy-start.2 = (bf16[1,1,128,768]{3,2,1,0:T(8,128)(2,1)S(1)}, bf16[1,1,128,768]{3,2,1,0:T(8,128)(2,1)}, u32[]{:S(2)}) copy-start(bf16[1,1,128,768]{3,2,1,0:T(8,128)(2,1)} %param.4) | copy-start | bytes 589828
  0.0 27.1 %copy-start.3 = (s32[16,64]{1,0:T(8,128)S(1)}, s32[16,64]{1,0:T(8,128)}, u32[]{:S(2)}) copy-start(s32[16,64]{1,0:T(8,128)} %tissue.1) | copy-start | bytes 12292
  1.3 29.3 %collective-permute-start.3 = (bf16[264,768]{1,0:T(8,128)(2,1)S(1)}, bf16[264,768]{1,0:T(8,128)(2,1)S(1)}, u32[]{:S(2)}, u32[]{:S(2)}) collective-permute-start(bf16[264,768]{1,0:T(8,128)(2,1)S(1)} %maximum_maximum_fusion), channel_id=1, source_target_pairs={{64,128},{128,64},{192,256},{256,192},{320,384},{384,320},{448,512... | collective-permute-start | bytes 1216520 | tf_op jit(solution)/shard_map/ppermute | solution.py:210
  14.4 12.7 %collective-permute-start.2 = (bf16[256,768]{1,0:T(8,128)(2,1)S(1)}, bf16[256,768]{1,0:T(8,128)(2,1)S(1)}, u32[]{:S(2)}, u32[]{:S(2)}) collective-permute-start(bf16[256,768]{1,0:T(8,128)(2,1)S(1)} %pad_maximum_fusion), channel_id=1, source_target_pairs={{0,64},{64,0},{128,192},{192,128},{256,320},{320,256},{384,448},{4... | collective-permute-start | bytes 1179656 | tf_op jit(solution)/shard_map/ppermute | solution.py:211
  16.4 10.7 %collective-permute-start = (bf16[128,768]{1,0:T(8,128)(2,1)S(1)}, bf16[128,768]{1,0:T(8,128)(2,1)S(1)}, u32[]{:S(2)}, u32[]{:S(2)}) collective-permute-start(bf16[128,768]{1,0:T(8,128)(2,1)S(1)} %bitcast.10), channel_id=1, source_target_pairs={{1,2},{2,1},{3,4},{4,3},{5,6},{6,5},{7,8},{8,7},{9,10},{10,9},{11,... | collective-permute-start | bytes 589832 | tf_op jit(solution)/shard_map/ppermute | solution.py:212
  19.4 7.7 %collective-permute-start.1 = (bf16[128,768]{1,0:T(8,128)(2,1)S(1)}, bf16[128,768]{1,0:T(8,128)(2,1)S(1)}, u32[]{:S(2)}, u32[]{:S(2)}) collective-permute-start(bf16[128,768]{1,0:T(8,128)(2,1)S(1)} %bitcast.11), channel_id=1, source_target_pairs={{0,1},{1,0},{2,3},{3,2},{4,5},{5,4},{6,7},{7,6},{8,9},{9,8},{10,11... | collective-permute-start | bytes 589832 | tf_op jit(solution)/shard_map/ppermute | solution.py:213
  32.4 9.4 %collective-permute-start.4 = (bf16[128,896]{1,0:T(8,128)(2,1)S(1)}, bf16[128,896]{1,0:T(8,128)(2,1)S(1)}, u32[]{:S(2)}, u32[]{:S(2)}) collective-permute-start(bf16[128,896]{1,0:T(8,128)(2,1)S(1)} %get-tuple-element.21), channel_id=1, source_target_pairs={{1,2},{2,1},{3,4},{4,3},{5,6},{6,5},{7,8},{8,7},{9,10},{10,9},{11,... | collective-permute-start | bytes 688136 | tf_op jit(solution)/shard_map/ppermute | solution.py:222
  34.3 7.5 %collective-permute-start.5 = (bf16[128,896]{1,0:T(8,128)(2,1)S(1)}, bf16[128,896]{1,0:T(8,128)(2,1)S(1)}, u32[]{:S(2)}, u32[]{:S(2)}) collective-permute-start(bf16[128,896]{1,0:T(8,128)(2,1)S(1)} %get-tuple-element.22), channel_id=1, source_target_pairs={{0,1},{1,0},{2,3},{3,2},{4,5},{5,4},{6,7},{7,6},{8,9},{9,8},{10,11... | collective-permute-start | bytes 688136 | tf_op jit(solution)/shard_map/ppermute | solution.py:223

commit v3 on v2

--- a/solution.py
+++ b/solution.py
@@ -76,13 +76,16 @@
     return slice(p * PAIR, (p + 1) * PAIR)
 
 
-def early_kernel(cols, tissue, q_hbm, qd, qc, k_hbm, v_hbm, kva, top_ref, tot_ref, mix_ref, flags, q, k, v, sems):
-    copies = [
-        pltpu.make_async_copy(source, target, sems.at[n])
-        for n, (source, target) in enumerate(((q_hbm, q), (k_hbm, k), (v_hbm, v)))
-    ]
-    for copy in copies:
-        copy.start()
+def own_tile(query, kv, bias, i, low, top_ref, tot_ref, mix_ref):
+    for p in range(PAIRS):
+        at = lanes(p)
+        t, l, m = attend_pair(query[:, at], (kv[:TOK, at],), (kv[TOK:, at],), (bias,), low)
+        top_ref[i, :, at] = t
+        tot_ref[i, :, at] = l
+        mix_ref[i, :, at] = m
+
+
+def early_kernel(cols, tissue, q, kv, top_ref, tot_ref, mix_ref, flags):
     row, col = position()
     low = lane_low()
     own = tile_bias(tissue, row, col)
@@ -91,25 +94,24 @@
     other = partner(col, True)
     missing = jnp.where((other >= 0) & (other < cols), 0.0, NEG).astype(F32)
     shown = jnp.where(tissue[row, col] > 0, 1.0, 0.0).astype(F32)
-    for n, value in enumerate((far, missing, shown)):
+    for n, value in enumerate((near, far, missing, shown, own)):
         flags[n : n + 1, :] = jnp.full((1, PAIR), value, F32)
-    for copy in copies:
-        copy.wait()
-    for p in range(PAIRS):
-        at = lanes(p)
-        for i, query in enumerate((q, qc, qd)):
-            t, l, m = attend_pair(
-                query[:, at], (k[:, at], kva[:TOK, at]), (v[:, at], kva[TOK:, at]),
-                (None if i == 0 else own, near), low,
-            )
-            top_ref[i, :, at] = t
-            tot_ref[i, :, at] = l
-            mix_ref[i, :, at] = m
-
-
-def late_part(query, kvb, bias, top, tot, mix, i, p, low):
+    own_tile(q, kv, None, 0, low, top_ref, tot_ref, mix_ref)
+
+
+def neighbour_kernel(flags, qc, qd, kv, top_ref, tot_ref, mix_ref):
+    low = lane_low()
+    own_tile(qd, kv, flags[4:5, :], 0, low, top_ref, tot_ref, mix_ref)
+    own_tile(qc, kv, flags[4:5, :], 1, low, top_ref, tot_ref, mix_ref)
+
+
+def late_part(query, kva, kvb, flags, state, i, p, low):
     at = lanes(p)
-    t, l, m = attend_pair(query[:, at], (kvb[:TOK, at],), (kvb[TOK : 2 * TOK, at],), (bias,), low)
+    t, l, m = attend_pair(
+        query[:, at], (kva[:TOK, at], kvb[:TOK, at]), (kva[TOK:, at], kvb[TOK:, at]),
+        (flags[0:1, :], flags[1:2, :]), low,
+    )
+    top, tot, mix = state
     t0 = top[i, :, at]
     best = jnp.maximum(t, t0)
     new, old = jnp.exp2(t - best), jnp.exp2(t0 - best)
@@ -129,26 +131,24 @@
     return parts
 
 
-def side_kernel(flags, qd, qc, kvb, top, tot, mix, out_d, out_c):
-    low = lane_low()
-    bias = flags[0:1, :]
-    for i, (query, out) in enumerate(((qc, out_c), (qd, out_d))):
+def side_kernel(flags, qc, qd, kva, kvb, top, tot, mix, out_d, out_c):
+    low = lane_low()
+    for i, (query, out) in enumerate(((qd, out_d), (qc, out_c))):
         stats = jnp.zeros((TOK, PAIR), F32)
         for p in range(PAIRS):
-            best, total, mixed = late_part(query, kvb, bias, top, tot, mix, i + 1, p, low)
+            best, total, mixed = late_part(query, kva, kvb, flags, (top, tot, mix), i, p, low)
             out[:, lanes(p)] = mixed.astype(BF16)
             for slot, piece in enumerate(pieces(best, 3) + pieces(total, 2)):
                 stats = jnp.where(spot(p + 8 * slot), piece, stats)
         out[:, HD:] = stats.astype(BF16)
 
 
-def own_kernel(flags, q, kvb, top, tot, mix, mix_out, top_out, tot_out):
-    low = lane_low()
-    bias = flags[0:1, :]
+def own_kernel(flags, q, kva, kvb, top, tot, mix, mix_out, top_out, tot_out):
+    low = lane_low()
     tops = jnp.zeros((TOK, PAIR), F32)
     tots = jnp.ones((TOK, PAIR), F32)
     for p in range(PAIRS):
-        best, total, mixed = late_part(q, kvb, bias, top, tot, mix, 0, p, low)
+        best, total, mixed = late_part(q, kva, kvb, flags, (top, tot, mix), 0, p, low)
         mix_out[:, lanes(p)] = mixed
         tops = jnp.where(spot(p), best, tops)
         tots = jnp.where(spot(p), total, tots)
@@ -158,7 +158,7 @@
 
 def merge_kernel(flags, mix, top, tot, in_d, in_c, out):
     low = lane_low()
-    missing, own = flags[1:2, :], flags[2:3, :]
+    missing, own = flags[2:3, :], flags[3:4, :]
     tops, tots = [top[...]], [tot[...]]
     for part, gap in ((in_c, None), (in_d, missing)):
         stats = part[:, HD:].astype(F32)
@@ -207,22 +207,26 @@
     rows, cols = tissue.shape
     far, near = swaps(rows, 1), swaps(rows, 0)
     beyond, beside = swaps(cols, 1), swaps(cols, 0)
-    kvb = lax.ppermute(jnp.concatenate([k, v, jnp.zeros((8, HD), BF16)]), "row", far)
-    kva = lax.ppermute(jnp.concatenate([k, v]), "row", near)
+    stack = jnp.concatenate([k, v])
+    kvb = lax.ppermute(stack, "row", far)
+    kva = lax.ppermute(stack, "row", near)
     qd = lax.ppermute(q, "col", beyond)
     qc = lax.ppermute(q, "col", beside)
-    outs = [shaped(3, TOK, HD)] * 3 + [shaped(8, PAIR)]
-    staged = [pltpu.VMEM((TOK, HD), BF16)] * 3 + [pltpu.SemaphoreType.DMA((3,))]
-    top, tot, mix, flags = call(
-        functools.partial(early_kernel, cols), outs, "early", [SMEM, ANY, VMEM, VMEM, ANY, ANY, VMEM],
-        tissue, q, qd, qc, k, v, kva, scratch=staged,
-    )
+    outs = [shaped(1, TOK, HD)] * 3
+    *state, flags = call(
+        functools.partial(early_kernel, cols), outs + [shaped(8, PAIR)], "early", [SMEM, VMEM, VMEM],
+        tissue, q, stack,
+    )
+    outs = [shaped(2, TOK, HD)] * 3
+    side_state = call(neighbour_kernel, outs, "neighbour", [VMEM] * 4, flags, qc, qd, stack)
     pack = shaped(TOK, HD + PAIR, dtype=BF16)
-    out_d, out_c = call(side_kernel, [pack] * 2, "side", [VMEM] * 7, flags, qd, qc, kvb, top, tot, mix)
+    out_d, out_c = call(
+        side_kernel, [pack] * 2, "side", [VMEM] * 8, flags, qc, qd, kva, kvb, *side_state
+    )
     in_d = lax.ppermute(out_d, "col", beyond)
     in_c = lax.ppermute(out_c, "col", beside)
     own = [shaped(TOK, HD), shaped(TOK, PAIR), shaped(TOK, PAIR)]
-    mix, top, tot = call(own_kernel, own, "own", [VMEM] * 6, flags, q, kvb, top, tot, mix)
+    mix, top, tot = call(own_kernel, own, "own", [VMEM] * 7, flags, q, kva, kvb, *state)
     (out,) = call(
         merge_kernel, [shaped(TOK, HD, dtype=BF16)], "merge", [VMEM] * 6, flags, mix, top, tot, in_d, in_c
     )

time: 43.7 us -> 43.4 us (level)
  the two profiles are of different devices: /device:TPU:240 before, /device:TPU:368 now
where the time goes in v3:
time: 43.4 us; the launch traced here: 43.1 us
  starting transfers between devices  22.3 us (51%)
  waiting for transfers between devices  12.2 us (28%)
  Pallas kernels  7.37 us (17%)
  other arithmetic  1.09 us (3%)
    ppermute x1, starting transfers between devices, on_device(): kvb = lax.ppermute(stack, 'row', far)  11.2 us
    pallas_call x5, Pallas kernels, call(): pl.pallas_call(body, out_shape=outs, in_specs=specs, out_specs=[VMEM] * l...  7.37 us
    ppermute x1, waiting for transfers between devices, on_device(): in_d = lax.ppermute(out_d, 'col', beyond)  4.62 us
    ppermute x1, waiting for transfers between devices, on_device(): kvb = lax.ppermute(stack, 'row', far)  3.84 us
    ppermute x1, waiting for transfers between devices, on_device(): qd = lax.ppermute(q, 'col', beyond)  3.78 us
    ppermute x1, starting transfers between devices, on_device(): qd = lax.ppermute(q, 'col', beyond)  3.02 us
    ppermute x1, starting transfers between devices, on_device(): qc = lax.ppermute(q, 'col', beside)  2.4 us
    ppermute x1, starting transfers between devices, on_device(): in_d = lax.ppermute(out_d, 'col', beyond)  1.92 us
  transfers between devices with their start and end apart: 6, of which 3 were waited for; matrix products, arithmetic and copies ran while one was open for 0% of the time, Pallas kernels for 9%

profile of v3, /device:TPU:368, one launch (start us, length us, event | category | flops | bytes accessed | tf_op | source)
XLA Modules:
  0.0 43.1 jit_solution(17815308787132359702)
XLA Ops:
  0.0 0.0 copy-start
  0.0 0.0 copy-start.1
  0.0 1.1 %pad_maximum_fusion.kv = bf16[256,768]{1,0:T(8,128)(2,1)S(1)} fusion(bf16[128,768]{1,0:T(8,128)(2,1)} %bitcast.8, bf16[128,768]{1,0:T(8,128)(2,1)} %bitcast.9), kind=kLoop, calls=%fused_computation | loop fusion | flops 786432 | bytes 786432 | tf_op jit(solution)/shard_map/concatenate | solution.py:210
  1.1 11.2 %collective-permute-start.1 = (bf16[256,768]{1,0:T(8,128)(2,1)S(1)}, bf16[256,768]{1,0:T(8,128)(2,1)S(1)}, u32[]{:S(2)}, u32[]{:S(2)}) collective-permute-start(bf16[256,768]{1,0:T(8,128)(2,1)S(1)} %pad_maximum_fusion.kv), channel_id=1, source_target_pairs={{64,128},{128,64},{192,256},{256,192},{320,384},{384,320},{448,512... | collective-permute-start | bytes 1179656 | tf_op jit(solution)/shard_map/ppermute | solution.py:211
  12.3 1.9 %collective-permute-start = (bf16[256,768]{1,0:T(8,128)(2,1)S(1)}, bf16[256,768]{1,0:T(8,128)(2,1)S(1)}, u32[]{:S(2)}, u32[]{:S(2)}) collective-permute-start(bf16[256,768]{1,0:T(8,128)(2,1)S(1)} %pad_maximum_fusion.kv), channel_id=1, source_target_pairs={{0,64},{64,0},{128,192},{192,128},{256,320},{320,256},{384,448},{4... | collective-permute-start | bytes 1179656 | tf_op jit(solution)/shard_map/ppermute | solution.py:212
  14.2 0.0 copy-done
  14.2 3.0 %collective-permute-start.3 = (bf16[128,768]{1,0:T(8,128)(2,1)S(1)}, bf16[128,768]{1,0:T(8,128)(2,1)S(1)}, u32[]{:S(2)}, u32[]{:S(2)}) collective-permute-start(bf16[128,768]{1,0:T(8,128)(2,1)S(1)} %bitcast.4), channel_id=1, source_target_pairs={{1,2},{2,1},{3,4},{4,3},{5,6},{6,5},{7,8},{8,7},{9,10},{10,9},{11,... | collective-permute-start | bytes 589832 | tf_op jit(solution)/shard_map/ppermute | solution.py:213
  17.2 2.4 %collective-permute-start.2 = (bf16[128,768]{1,0:T(8,128)(2,1)S(1)}, bf16[128,768]{1,0:T(8,128)(2,1)S(1)}, u32[]{:S(2)}, u32[]{:S(2)}) collective-permute-start(bf16[128,768]{1,0:T(8,128)(2,1)S(1)} %bitcast.5), channel_id=1, source_target_pairs={{0,1},{1,0},{2,3},{3,2},{4,5},{5,4},{6,7},{7,6},{8,9},{9,8},{10,11... | collective-permute-start | bytes 589832 | tf_op jit(solution)/shard_map/ppermute | solution.py:214
  19.6 0.0 copy-done.1
  19.7 1.5 %early.1 = (f32[1,128,768]{2,1,0:T(8,128)S(1)}, f32[1,128,768]{2,1,0:T(8,128)S(1)}, f32[1,128,768]{2,1,0:T(8,128)S(1)}, f32[8,128]{1,0:T(8,128)S(1)}) custom-call(s32[16,64]{1,0:T(8,128)S(1)} %copy-done.1, bf16[128,768]{1,0:T(8,128)(2,1)S(1)} %bitcast.6, bf16[256,768]{1,0:T(8,128)(2,1)S(1)} %pad_maximum_fusion.kv), custom_call_target="tpu_custom_call" | custom-call | flops 1 | bytes 1024 | tf_op jit(solution)/shard_map/early/pallas_call | solution.py:189
  21.1 3.8 %collective-permute-done.3.qd = bf16[128,768]{1,0:T(8,128)(2,1)S(1)} collective-permute-done((bf16[128,768]{1,0:T(8,128)(2,1)S(1)}, bf16[128,768]{1,0:T(8,128)(2,1)S(1)}, u32[]{:S(2)}, u32[]{:S(2)}) %collective-permute-start.3) | collective-permute-done | bytes 196640 | tf_op jit(solution)/shard_map/ppermute | solution.py:213
  24.9 0.0 collective-permute-done.2.qc
  24.9 1.2 %neighbour.1 = (f32[2,128,768]{2,1,0:T(8,128)S(1)}, f32[2,128,768]{2,1,0:T(8,128)S(1)}, f32[2,128,768]{2,1,0:T(8,128)S(1)}) custom-call(f32[8,128]{1,0:T(8,128)S(1)} %get-tuple-element.17.flags, bf16[128,768]{1,0:T(8,128)(2,1)S(1)} %collective-permute-done.2.qc, bf16[128,768]{1,0:T(8,128)(2,1)S(1)} %collective-permute-done.3.qd, ...), custom_call_target="tpu_custom_call" | custom-call | flops 1 | bytes 1024 | tf_op jit(solution)/shard_map/neighbour/pallas_call | solution.py:189
  26.2 3.8 %collective-permute-done.1.kvb = bf16[256,768]{1,0:T(8,128)(2,1)S(1)} collective-permute-done((bf16[256,768]{1,0:T(8,128)(2,1)S(1)}, bf16[256,768]{1,0:T(8,128)(2,1)S(1)}, u32[]{:S(2)}, u32[]{:S(2)}) %collective-permute-start.1) | collective-permute-done | bytes 393248 | tf_op jit(solution)/shard_map/ppermute | solution.py:211
  30.0 0.0 collective-permute-done.kva
  30.0 2.1 %side.1 = (bf16[128,896]{1,0:T(8,128)(2,1)S(1)}, bf16[128,896]{1,0:T(8,128)(2,1)S(1)}) custom-call(f32[8,128]{1,0:T(8,128)S(1)} %get-tuple-element.17.flags, bf16[128,768]{1,0:T(8,128)(2,1)S(1)} %collective-permute-done.2.qc, bf16[128,768]{1,0:T(8,128)(2,1)S(1)} %collective-permute-done.3.qd, bf16[256,768]{1,0:T(8,128)(2,1)S(1)} %collective-permute-done.kva, ...), custom_call_target="tpu_custom_call" | custom-call | flops 1 | bytes 1024 | tf_op jit(solution)/shard_map/side/pallas_call | solution.py:189
  32.1 1.9 %collective-permute-start.4 = (bf16[128,896]{1,0:T(8,128)(2,1)S(1)}, bf16[128,896]{1,0:T(8,128)(2,1)S(1)}, u32[]{:S(2)}, u32[]{:S(2)}) collective-permute-start(bf16[128,896]{1,0:T(8,128)(2,1)S(1)} %get-tuple-element.27), channel_id=1, source_target_pairs={{1,2},{2,1},{3,4},{4,3},{5,6},{6,5},{7,8},{8,7},{9,10},{10,9},{11,... | collective-permute-start | bytes 688136 | tf_op jit(solution)/shard_map/ppermute | solution.py:226
  34.0 1.9 %collective-permute-start.5 = (bf16[128,896]{1,0:T(8,128)(2,1)S(1)}, bf16[128,896]{1,0:T(8,128)(2,1)S(1)}, u32[]{:S(2)}, u32[]{:S(2)}) collective-permute-start(bf16[128,896]{1,0:T(8,128)(2,1)S(1)} %get-tuple-element.28), channel_id=1, source_target_pairs={{0,1},{1,0},{2,3},{3,2},{4,5},{5,4},{6,7},{7,6},{8,9},{9,8},{10,11... | collective-permute-start | bytes 688136 | tf_op jit(solution)/shard_map/ppermute | solution.py:227
  36.0 1.0 %own.1 = (f32[128,768]{1,0:T(8,128)S(1)}, f32[128,128]{1,0:T(8,128)S(1)}, f32[128,128]{1,0:T(8,128)S(1)}) custom-call(f32[8,128]{1,0:T(8,128)S(1)} %get-tuple-element.17.flags, bf16[128,768]{1,0:T(8,128)(2,1)S(1)} %bitcast.7, bf16[256,768]{1,0:T(8,128)(2,1)S(1)} %collective-permute-done.kva, bf16[256,768]{1,0:T(8,128)(2,1)S(1)} %collective-permute-done.1.kvb, ...), custom_call_target="tpu_custom_call" | custom-call | flops 1 | bytes 1024 | tf_op jit(solution)/shard_map/own/pallas_call | solution.py:189
  36.9 4.6 %collective-permute-done.4.in_d = bf16[128,896]{1,0:T(8,128)(2,1)S(1)} collective-permute-done((bf16[128,896]{1,0:T(8,128)(2,1)S(1)}, bf16[128,896]{1,0:T(8,128)(2,1)S(1)}, u32[]{:S(2)}, u32[]{:S(2)}) %collective-permute-start.4) | collective-permute-done | bytes 229408 | tf_op jit(solution)/shard_map/ppermute | solution.py:226
  41.6 0.0 collective-permute-done.5.in_c
  41.6 1.6 %merge.1 = bf16[128,768]{1,0:T(8,128)(2,1)} custom-call(f32[8,128]{1,0:T(8,128)S(1)} %get-tuple-element.17.flags, f32[128,768]{1,0:T(8,128)S(1)} %get-tuple-element.21.mix, f32[128,128]{1,0:T(8,128)S(1)} %get-tuple-element.22.top, f32[128,128]{1,0:T(8,128)S(1)} %get-tuple-element.23.tot, bf16[128,896]{1,0:T(8,128)(2,1)S(1)} %collective-permute-done.4.in_d, ...), custom_call_target="tpu_custom_call" | custom-call | flops 1 | bytes 1024 | tf_op jit(solution)/shard_map/merge/pallas_call | solution.py:189
Async XLA Ops:
  0.0 14.2 %copy-start = (bf16[1,1,128,768]{3,2,1,0:T(8,128)(2,1)S(1)}, bf16[1,1,128,768]{3,2,1,0:T(8,128)(2,1)}, u32[]{:S(2)}) copy-start(bf16[1,1,128,768]{3,2,1,0:T(8,128)(2,1)} %param.4) | copy-start | bytes 589828
  0.0 19.6 %copy-start.1 = (s32[16,64]{1,0:T(8,128)S(1)}, s32[16,64]{1,0:T(8,128)}, u32[]{:S(2)}) copy-start(s32[16,64]{1,0:T(8,128)} %tissue.1) | copy-start | bytes 12292
  1.1 28.9 %collective-permute-start.1 = (bf16[256,768]{1,0:T(8,128)(2,1)S(1)}, bf16[256,768]{1,0:T(8,128)(2,1)S(1)}, u32[]{:S(2)}, u32[]{:S(2)}) collective-permute-start(bf16[256,768]{1,0:T(8,128)(2,1)S(1)} %pad_maximum_fusion.kv), channel_id=1, source_target_pairs={{64,128},{128,64},{192,256},{256,192},{320,384},{384,320},{448,512... | collective-permute-start | bytes 1179656 | tf_op jit(solution)/shard_map/ppermute | solution.py:211
  12.3 17.7 %collective-permute-start = (bf16[256,768]{1,0:T(8,128)(2,1)S(1)}, bf16[256,768]{1,0:T(8,128)(2,1)S(1)}, u32[]{:S(2)}, u32[]{:S(2)}) collective-permute-start(bf16[256,768]{1,0:T(8,128)(2,1)S(1)} %pad_maximum_fusion.kv), channel_id=1, source_target_pairs={{0,64},{64,0},{128,192},{192,128},{256,320},{320,256},{384,448},{4... | collective-permute-start | bytes 1179656 | tf_op jit(solution)/shard_map/ppermute | solution.py:212
  14.2 10.7 %collective-permute-start.3 = (bf16[128,768]{1,0:T(8,128)(2,1)S(1)}, bf16[128,768]{1,0:T(8,128)(2,1)S(1)}, u32[]{:S(2)}, u32[]{:S(2)}) collective-permute-start(bf16[128,768]{1,0:T(8,128)(2,1)S(1)} %bitcast.4), channel_id=1, source_target_pairs={{1,2},{2,1},{3,4},{4,3},{5,6},{6,5},{7,8},{8,7},{9,10},{10,9},{11,... | collective-permute-start | bytes 589832 | tf_op jit(solution)/shard_map/ppermute | solution.py:213
  17.2 7.7 %collective-permute-start.2 = (bf16[128,768]{1,0:T(8,128)(2,1)S(1)}, bf16[128,768]{1,0:T(8,128)(2,1)S(1)}, u32[]{:S(2)}, u32[]{:S(2)}) collective-permute-start(bf16[128,768]{1,0:T(8,128)(2,1)S(1)} %bitcast.5), channel_id=1, source_target_pairs={{0,1},{1,0},{2,3},{3,2},{4,5},{5,4},{6,7},{7,6},{8,9},{9,8},{10,11... | collective-permute-start | bytes 589832 | tf_op jit(solution)/shard_map/ppermute | solution.py:214
  32.1 9.4 %collective-permute-start.4 = (bf16[128,896]{1,0:T(8,128)(2,1)S(1)}, bf16[128,896]{1,0:T(8,128)(2,1)S(1)}, u32[]{:S(2)}, u32[]{:S(2)}) collective-permute-start(bf16[128,896]{1,0:T(8,128)(2,1)S(1)} %get-tuple-element.27), channel_id=1, source_target_pairs={{1,2},{2,1},{3,4},{4,3},{5,6},{6,5},{7,8},{8,7},{9,10},{10,9},{11,... | collective-permute-start | bytes 688136 | tf_op jit(solution)/shard_map/ppermute | solution.py:226
  34.0 7.5 %collective-permute-start.5 = (bf16[128,896]{1,0:T(8,128)(2,1)S(1)}, bf16[128,896]{1,0:T(8,128)(2,1)S(1)}, u32[]{:S(2)}, u32[]{:S(2)}) collective-permute-start(bf16[128,896]{1,0:T(8,128)(2,1)S(1)} %get-tuple-element.28), channel_id=1, source_target_pairs={{0,1},{1,0},{2,3},{3,2},{4,5},{5,4},{6,7},{7,6},{8,9},{9,8},{10,11... | collective-permute-start | bytes 688136 | tf_op jit(solution)/shard_map/ppermute | solution.py:227

commit v4 on v3

--- a/solution.py
+++ b/solution.py
@@ -72,6 +72,23 @@
     return top2, tot2, mix2
 
 
+def attend_late(query, kva, kvb, flags, at, low):
+    zero = jnp.zeros_like(query)
+    both = jnp.concatenate([jnp.where(low, query, zero), jnp.where(low, zero, query)], axis=0)
+    keys = jnp.concatenate([kva[:TOK, at], kvb[:TOK, at]], axis=0)
+    values = jnp.concatenate([kva[TOK:, at], kvb[TOK:, at]], axis=0)
+    values = jnp.concatenate([values, jnp.ones_like(values)], axis=1)
+    scores = lax.dot_general(both, keys, (((1,), (1,)), ((), ())), preferred_element_type=F32) * SCALE
+    scores = scores + jnp.concatenate([flags[0:1, :], flags[1:2, :]], axis=1)
+    top = jnp.maximum(jnp.max(scores, axis=1, keepdims=True), FLOOR)
+    mixed = jnp.dot(jnp.exp2(scores - top).astype(BF16), values, preferred_element_type=F32)
+    shape = (TOK, PAIR)
+    top2 = jnp.where(low, jnp.broadcast_to(top[:TOK], shape), jnp.broadcast_to(top[TOK:], shape))
+    tot2 = jnp.where(low, mixed[:TOK, PAIR:], mixed[TOK:, PAIR:])
+    mix2 = jnp.where(low, mixed[:TOK, :PAIR], mixed[TOK:, :PAIR])
+    return top2, tot2, mix2
+
+
 def lanes(p):
     return slice(p * PAIR, (p + 1) * PAIR)
 
@@ -107,10 +124,7 @@
 
 def late_part(query, kva, kvb, flags, state, i, p, low):
     at = lanes(p)
-    t, l, m = attend_pair(
-        query[:, at], (kva[:TOK, at], kvb[:TOK, at]), (kva[TOK:, at], kvb[TOK:, at]),
-        (flags[0:1, :], flags[1:2, :]), low,
-    )
+    t, l, m = attend_late(query[:, at], kva, kvb, flags, at, low)
     top, tot, mix = state
     t0 = top[i, :, at]
     best = jnp.maximum(t, t0)
@@ -134,12 +148,16 @@
 def side_kernel(flags, qc, qd, kva, kvb, top, tot, mix, out_d, out_c):
     low = lane_low()
     for i, (query, out) in enumerate(((qd, out_d), (qc, out_c))):
-        stats = jnp.zeros((TOK, PAIR), F32)
+        tops = jnp.zeros((TOK, PAIR), F32)
+        tots = jnp.zeros((TOK, PAIR), F32)
         for p in range(PAIRS):
             best, total, mixed = late_part(query, kva, kvb, flags, (top, tot, mix), i, p, low)
             out[:, lanes(p)] = mixed.astype(BF16)
-            for slot, piece in enumerate(pieces(best, 3) + pieces(total, 2)):
-                stats = jnp.where(spot(p + 8 * slot), piece, stats)
+            tops = jnp.where(spot(p), best, tops)
+            tots = jnp.where(spot(p), total, tots)
+        stats = jnp.zeros((TOK, PAIR), F32)
+        for slot, piece in enumerate(pieces(tops, 3) + pieces(tots, 2)):
+            stats = stats + (pltpu.roll(piece, 8 * slot, 1) if slot else piece)
         out[:, HD:] = stats.astype(BF16)
 
 
@@ -169,18 +187,20 @@
     best = functools.reduce(jnp.maximum, tops)
     shares = [jnp.exp2(t - best) for t in tops]
     total = functools.reduce(jnp.add, [s * t for s, t in zip(shares, tots)])
-    shares = [s * own / total for s in shares]
+    keep = (lax.broadcasted_iota(jnp.int32, (TOK, PAIR), 1) & (HDIM - 1)) < PAIRS
+    shares = [jnp.where(keep, s * own / total, 0.0) for s in shares]
+    source = lax.broadcasted_iota(jnp.int32, (PAIR, HD), 0)
+    target = lax.broadcasted_iota(jnp.int32, (PAIR, HD), 1)
+    pick = (source == (target // PAIR + (target & HDIM))).astype(BF16)
+    pick = jnp.concatenate([pick, pick], axis=0)
+    spread = [
+        jnp.dot(jnp.concatenate(pieces(s, 2), axis=1).astype(BF16), pick, preferred_element_type=F32) for s in shares
+    ]
     for p in range(PAIRS):
         at = lanes(p)
         acc = None
-        for share, part in zip(shares, (mix, in_c, in_d)):
-            shape = (TOK, PAIR)
-            factor = jnp.where(
-                low,
-                jnp.broadcast_to(share[:, p : p + 1], shape),
-                jnp.broadcast_to(share[:, HDIM + p : HDIM + p + 1], shape),
-            )
-            term = factor * part[:, at].astype(F32)
+        for factors, part in zip(spread, (mix, in_c, in_d)):
+            term = factors[:, at] * part[:, at].astype(F32)
             acc = term if acc is None else acc + term
         out[:, at] = acc.astype(BF16)
 

time: 43.4 us -> 42.8 us (0.986)
  the two profiles are of different devices: /device:TPU:368 before, /device:TPU:768 now
where the time goes in v4:
time: 42.8 us; the launch traced here: 42.5 us
  waiting for transfers between devices  18.6 us (43%)
  starting transfers between devices  16.5 us (39%)
  Pallas kernels  6.33 us (15%)
  other arithmetic  1.09 us (3%)
    ppermute x1, waiting for transfers between devices, on_device(): kvb = lax.ppermute(stack, 'row', far)  10.3 us
    pallas_call x5, Pallas kernels, call(): pl.pallas_call(body, out_shape=outs, in_specs=specs, out_specs=[VMEM] * l...  6.33 us
    ppermute x1, starting transfers between devices, on_device(): kva = lax.ppermute(stack, 'row', near)  5.32 us
    ppermute x1, waiting for transfers between devices, on_device(): in_d = lax.ppermute(out_d, 'col', beyond)  4.71 us
    ppermute x1, waiting for transfers between devices, on_device(): qd = lax.ppermute(q, 'col', beyond)  3.57 us
    ppermute x1, starting transfers between devices, on_device(): qd = lax.ppermute(q, 'col', beyond)  2.7 us
    ppermute x1, starting transfers between devices, on_device(): qc = lax.ppermute(q, 'col', beside)  2.68 us
    ppermute x1, starting transfers between devices, on_device(): kvb = lax.ppermute(stack, 'row', far)  1.92 us
  transfers between devices with their start and end apart: 6, of which 3 were waited for; matrix products, arithmetic and copies ran while one was open for 0% of the time, Pallas kernels for 8%

profile of v4, /device:TPU:768, one launch (start us, length us, event | category | flops | bytes accessed | tf_op | source)
XLA Modules:
  0.0 42.5 jit_solution(1565869348317721220)
XLA Ops:
  0.0 0.0 copy-start
  0.0 0.0 copy-start.1
  0.0 1.1 %pad_maximum_fusion.kv = bf16[256,768]{1,0:T(8,128)(2,1)S(1)} fusion(bf16[128,768]{1,0:T(8,128)(2,1)} %bitcast.8, bf16[128,768]{1,0:T(8,128)(2,1)} %bitcast.9), kind=kLoop, calls=%fused_computation | loop fusion | flops 786432 | bytes 786432 | tf_op jit(solution)/shard_map/concatenate | solution.py:230
  1.1 1.9 %collective-permute-start.1 = (bf16[256,768]{1,0:T(8,128)(2,1)S(1)}, bf16[256,768]{1,0:T(8,128)(2,1)S(1)}, u32[]{:S(2)}, u32[]{:S(2)}) collective-permute-start(bf16[256,768]{1,0:T(8,128)(2,1)S(1)} %pad_maximum_fusion.kv), channel_id=1, source_target_pairs={{64,128},{128,64},{192,256},{256,192},{320,384},{384,320},{448,512... | collective-permute-start | bytes 1179656 | tf_op jit(solution)/shard_map/ppermute | solution.py:231
  3.0 5.3 %collective-permute-start = (bf16[256,768]{1,0:T(8,128)(2,1)S(1)}, bf16[256,768]{1,0:T(8,128)(2,1)S(1)}, u32[]{:S(2)}, u32[]{:S(2)}) collective-permute-start(bf16[256,768]{1,0:T(8,128)(2,1)S(1)} %pad_maximum_fusion.kv), channel_id=1, source_target_pairs={{0,64},{64,0},{128,192},{192,128},{256,320},{320,256},{384,448},{4... | collective-permute-start | bytes 1179656 | tf_op jit(solution)/shard_map/ppermute | solution.py:232
  8.3 0.0 copy-done
  8.4 2.7 %collective-permute-start.3 = (bf16[128,768]{1,0:T(8,128)(2,1)S(1)}, bf16[128,768]{1,0:T(8,128)(2,1)S(1)}, u32[]{:S(2)}, u32[]{:S(2)}) collective-permute-start(bf16[128,768]{1,0:T(8,128)(2,1)S(1)} %bitcast.4), channel_id=1, source_target_pairs={{1,2},{2,1},{3,4},{4,3},{5,6},{6,5},{7,8},{8,7},{9,10},{10,9},{11,... | collective-permute-start | bytes 589832 | tf_op jit(solution)/shard_map/ppermute | solution.py:233
  11.1 2.7 %collective-permute-start.2 = (bf16[128,768]{1,0:T(8,128)(2,1)S(1)}, bf16[128,768]{1,0:T(8,128)(2,1)S(1)}, u32[]{:S(2)}, u32[]{:S(2)}) collective-permute-start(bf16[128,768]{1,0:T(8,128)(2,1)S(1)} %bitcast.5), channel_id=1, source_target_pairs={{0,1},{1,0},{2,3},{3,2},{4,5},{5,4},{6,7},{7,6},{8,9},{9,8},{10,11... | collective-permute-start | bytes 589832 | tf_op jit(solution)/shard_map/ppermute | solution.py:234
  13.8 0.0 copy-done.1
  13.8 1.5 %early.1 = (f32[1,128,768]{2,1,0:T(8,128)S(1)}, f32[1,128,768]{2,1,0:T(8,128)S(1)}, f32[1,128,768]{2,1,0:T(8,128)S(1)}, f32[8,128]{1,0:T(8,128)S(1)}) custom-call(s32[16,64]{1,0:T(8,128)S(1)} %copy-done.1, bf16[128,768]{1,0:T(8,128)(2,1)S(1)} %bitcast.6, bf16[256,768]{1,0:T(8,128)(2,1)S(1)} %pad_maximum_fusion.kv), custom_call_target="tpu_custom_call" | custom-call | flops 1 | bytes 1024 | tf_op jit(solution)/shard_map/early/pallas_call | solution.py:209
  15.3 3.6 %collective-permute-done.3.qd = bf16[128,768]{1,0:T(8,128)(2,1)S(1)} collective-permute-done((bf16[128,768]{1,0:T(8,128)(2,1)S(1)}, bf16[128,768]{1,0:T(8,128)(2,1)S(1)}, u32[]{:S(2)}, u32[]{:S(2)}) %collective-permute-start.3) | collective-permute-done | bytes 196640 | tf_op jit(solution)/shard_map/ppermute | solution.py:233
  18.8 0.0 collective-permute-done.2.qc
  18.8 1.2 %neighbour.1 = (f32[2,128,768]{2,1,0:T(8,128)S(1)}, f32[2,128,768]{2,1,0:T(8,128)S(1)}, f32[2,128,768]{2,1,0:T(8,128)S(1)}) custom-call(f32[8,128]{1,0:T(8,128)S(1)} %get-tuple-element.17.flags, bf16[128,768]{1,0:T(8,128)(2,1)S(1)} %collective-permute-done.2.qc, bf16[128,768]{1,0:T(8,128)(2,1)S(1)} %collective-permute-done.3.qd, ...), custom_call_target="tpu_custom_call" | custom-call | flops 1 | bytes 1024 | tf_op jit(solution)/shard_map/neighbour/pallas_call | solution.py:209
  20.1 10.3 %collective-permute-done.1.kvb = bf16[256,768]{1,0:T(8,128)(2,1)S(1)} collective-permute-done((bf16[256,768]{1,0:T(8,128)(2,1)S(1)}, bf16[256,768]{1,0:T(8,128)(2,1)S(1)}, u32[]{:S(2)}, u32[]{:S(2)}) %collective-permute-start.1) | collective-permute-done | bytes 393248 | tf_op jit(solution)/shard_map/ppermute | solution.py:231
  30.4 0.0 collective-permute-done.kva
  30.4 1.6 %side.1 = (bf16[128,896]{1,0:T(8,128)(2,1)S(1)}, bf16[128,896]{1,0:T(8,128)(2,1)S(1)}) custom-call(f32[8,128]{1,0:T(8,128)S(1)} %get-tuple-element.17.flags, bf16[128,768]{1,0:T(8,128)(2,1)S(1)} %collective-permute-done.2.qc, bf16[128,768]{1,0:T(8,128)(2,1)S(1)} %collective-permute-done.3.qd, bf16[256,768]{1,0:T(8,128)(2,1)S(1)} %collective-permute-done.kva, ...), custom_call_target="tpu_custom_call" | custom-call | flops 1 | bytes 1024 | tf_op jit(solution)/shard_map/side/pallas_call | solution.py:209
  32.0 1.9 %collective-permute-start.4 = (bf16[128,896]{1,0:T(8,128)(2,1)S(1)}, bf16[128,896]{1,0:T(8,128)(2,1)S(1)}, u32[]{:S(2)}, u32[]{:S(2)}) collective-permute-start(bf16[128,896]{1,0:T(8,128)(2,1)S(1)} %get-tuple-element.27), channel_id=1, source_target_pairs={{1,2},{2,1},{3,4},{4,3},{5,6},{6,5},{7,8},{8,7},{9,10},{10,9},{11,... | collective-permute-start | bytes 688136 | tf_op jit(solution)/shard_map/ppermute | solution.py:246
  33.9 1.9 %collective-permute-start.5 = (bf16[128,896]{1,0:T(8,128)(2,1)S(1)}, bf16[128,896]{1,0:T(8,128)(2,1)S(1)}, u32[]{:S(2)}, u32[]{:S(2)}) collective-permute-start(bf16[128,896]{1,0:T(8,128)(2,1)S(1)} %get-tuple-element.28), channel_id=1, source_target_pairs={{0,1},{1,0},{2,3},{3,2},{4,5},{5,4},{6,7},{7,6},{8,9},{9,8},{10,11... | collective-permute-start | bytes 688136 | tf_op jit(solution)/shard_map/ppermute | solution.py:247
  35.9 0.9 %own.1 = (f32[128,768]{1,0:T(8,128)S(1)}, f32[128,128]{1,0:T(8,128)S(1)}, f32[128,128]{1,0:T(8,128)S(1)}) custom-call(f32[8,128]{1,0:T(8,128)S(1)} %get-tuple-element.17.flags, bf16[128,768]{1,0:T(8,128)(2,1)S(1)} %bitcast.7, bf16[256,768]{1,0:T(8,128)(2,1)S(1)} %collective-permute-done.kva, bf16[256,768]{1,0:T(8,128)(2,1)S(1)} %collective-permute-done.1.kvb, ...), custom_call_target="tpu_custom_call" | custom-call | flops 1 | bytes 1024 | tf_op jit(solution)/shard_map/own/pallas_call | solution.py:209
  36.7 4.7 %collective-permute-done.4.in_d = bf16[128,896]{1,0:T(8,128)(2,1)S(1)} collective-permute-done((bf16[128,896]{1,0:T(8,128)(2,1)S(1)}, bf16[128,896]{1,0:T(8,128)(2,1)S(1)}, u32[]{:S(2)}, u32[]{:S(2)}) %collective-permute-start.4) | collective-permute-done | bytes 229408 | tf_op jit(solution)/shard_map/ppermute | solution.py:246
  41.5 0.0 collective-permute-done.5.in_c
  41.5 1.1 %merge.1 = bf16[128,768]{1,0:T(8,128)(2,1)} custom-call(f32[8,128]{1,0:T(8,128)S(1)} %get-tuple-element.17.flags, f32[128,768]{1,0:T(8,128)S(1)} %get-tuple-element.21.mix, f32[128,128]{1,0:T(8,128)S(1)} %get-tuple-element.22.top, f32[128,128]{1,0:T(8,128)S(1)} %get-tuple-element.23.tot, bf16[128,896]{1,0:T(8,128)(2,1)S(1)} %collective-permute-done.4.in_d, ...), custom_call_target="tpu_custom_call" | custom-call | flops 1 | bytes 1024 | tf_op jit(solution)/shard_map/merge/pallas_call | solution.py:209
Async XLA Ops:
  0.0 8.3 %copy-start = (bf16[1,1,128,768]{3,2,1,0:T(8,128)(2,1)S(1)}, bf16[1,1,128,768]{3,2,1,0:T(8,128)(2,1)}, u32[]{:S(2)}) copy-start(bf16[1,1,128,768]{3,2,1,0:T(8,128)(2,1)} %param.4) | copy-start | bytes 589828
  0.0 13.8 %copy-start.1 = (s32[16,64]{1,0:T(8,128)S(1)}, s32[16,64]{1,0:T(8,128)}, u32[]{:S(2)}) copy-start(s32[16,64]{1,0:T(8,128)} %tissue.1) | copy-start | bytes 12292
  1.1 29.3 %collective-permute-start.1 = (bf16[256,768]{1,0:T(8,128)(2,1)S(1)}, bf16[256,768]{1,0:T(8,128)(2,1)S(1)}, u32[]{:S(2)}, u32[]{:S(2)}) collective-permute-start(bf16[256,768]{1,0:T(8,128)(2,1)S(1)} %pad_maximum_fusion.kv), channel_id=1, source_target_pairs={{64,128},{128,64},{192,256},{256,192},{320,384},{384,320},{448,512... | collective-permute-start | bytes 1179656 | tf_op jit(solution)/shard_map/ppermute | solution.py:231
  3.0 27.3 %collective-permute-start = (bf16[256,768]{1,0:T(8,128)(2,1)S(1)}, bf16[256,768]{1,0:T(8,128)(2,1)S(1)}, u32[]{:S(2)}, u32[]{:S(2)}) collective-permute-start(bf16[256,768]{1,0:T(8,128)(2,1)S(1)} %pad_maximum_fusion.kv), channel_id=1, source_target_pairs={{0,64},{64,0},{128,192},{192,128},{256,320},{320,256},{384,448},{4... | collective-permute-start | bytes 1179656 | tf_op jit(solution)/shard_map/ppermute | solution.py:232
  8.4 10.5 %collective-permute-start.3 = (bf16[128,768]{1,0:T(8,128)(2,1)S(1)}, bf16[128,768]{1,0:T(8,128)(2,1)S(1)}, u32[]{:S(2)}, u32[]{:S(2)}) collective-permute-start(bf16[128,768]{1,0:T(8,128)(2,1)S(1)} %bitcast.4), channel_id=1, source_target_pairs={{1,2},{2,1},{3,4},{4,3},{5,6},{6,5},{7,8},{8,7},{9,10},{10,9},{11,... | collective-permute-start | bytes 589832 | tf_op jit(solution)/shard_map/ppermute | solution.py:233
  11.1 7.8 %collective-permute-start.2 = (bf16[128,768]{1,0:T(8,128)(2,1)S(1)}, bf16[128,768]{1,0:T(8,128)(2,1)S(1)}, u32[]{:S(2)}, u32[]{:S(2)}) collective-permute-start(bf16[128,768]{1,0:T(8,128)(2,1)S(1)} %bitcast.5), channel_id=1, source_target_pairs={{0,1},{1,0},{2,3},{3,2},{4,5},{5,4},{6,7},{7,6},{8,9},{9,8},{10,11... | collective-permute-start | bytes 589832 | tf_op jit(solution)/shard_map/ppermute | solution.py:234
  32.0 9.4 %collective-permute-start.4 = (bf16[128,896]{1,0:T(8,128)(2,1)S(1)}, bf16[128,896]{1,0:T(8,128)(2,1)S(1)}, u32[]{:S(2)}, u32[]{:S(2)}) collective-permute-start(bf16[128,896]{1,0:T(8,128)(2,1)S(1)} %get-tuple-element.27), channel_id=1, source_target_pairs={{1,2},{2,1},{3,4},{4,3},{5,6},{6,5},{7,8},{8,7},{9,10},{10,9},{11,... | collective-permute-start | bytes 688136 | tf_op jit(solution)/shard_map/ppermute | solution.py:246
  33.9 7.5 %collective-permute-start.5 = (bf16[128,896]{1,0:T(8,128)(2,1)S(1)}, bf16[128,896]{1,0:T(8,128)(2,1)S(1)}, u32[]{:S(2)}, u32[]{:S(2)}) collective-permute-start(bf16[128,896]{1,0:T(8,128)(2,1)S(1)} %get-tuple-element.28), channel_id=1, source_target_pairs={{0,1},{1,0},{2,3},{3,2},{4,5},{5,4},{6,7},{7,6},{8,9},{9,8},{10,11... | collective-permute-start | bytes 688136 | tf_op jit(solution)/shard_map/ppermute | solution.py:247

commit v5 on v4

--- a/solution.py
+++ b/solution.py
@@ -116,10 +116,8 @@
     own_tile(q, kv, None, 0, low, top_ref, tot_ref, mix_ref)
 
 
-def neighbour_kernel(flags, qc, qd, kv, top_ref, tot_ref, mix_ref):
-    low = lane_low()
-    own_tile(qd, kv, flags[4:5, :], 0, low, top_ref, tot_ref, mix_ref)
-    own_tile(qc, kv, flags[4:5, :], 1, low, top_ref, tot_ref, mix_ref)
+def neighbour_kernel(flags, query, kv, *refs):
+    own_tile(query, kv, flags[4:5, :], 0, lane_low(), *refs[-3:])
 
 
 def late_part(query, kva, kvb, flags, state, i, p, low):
@@ -145,20 +143,21 @@
     return parts
 
 
-def side_kernel(flags, qc, qd, kva, kvb, top, tot, mix, out_d, out_c):
-    low = lane_low()
-    for i, (query, out) in enumerate(((qd, out_d), (qc, out_c))):
-        tops = jnp.zeros((TOK, PAIR), F32)
-        tots = jnp.zeros((TOK, PAIR), F32)
-        for p in range(PAIRS):
-            best, total, mixed = late_part(query, kva, kvb, flags, (top, tot, mix), i, p, low)
-            out[:, lanes(p)] = mixed.astype(BF16)
-            tops = jnp.where(spot(p), best, tops)
-            tots = jnp.where(spot(p), total, tots)
-        stats = jnp.zeros((TOK, PAIR), F32)
-        for slot, piece in enumerate(pieces(tops, 3) + pieces(tots, 2)):
-            stats = stats + (pltpu.roll(piece, 8 * slot, 1) if slot else piece)
-        out[:, HD:] = stats.astype(BF16)
+def side_kernel(flags, query, kva, kvb, top, tot, mix, out):
+    low = lane_low()
+    tops = jnp.zeros((TOK, PAIR), F32)
+    tots = jnp.zeros((TOK, PAIR), F32)
+    for p in range(PAIRS):
+        best, total, mixed = late_part(query, kva, kvb, flags, (top, tot, mix), 0, p, low)
+        out[:TOK, lanes(p)] = mixed.astype(BF16)
+        tops = jnp.where(spot(p), best, tops)
+        tots = jnp.where(spot(p), total, tots)
+    stats = jnp.zeros((TOK, PAIR), F32)
+    for slot, piece in enumerate(pieces(tops, 3) + pieces(tots, 2)):
+        stats = stats + (pltpu.roll(piece, 8 * slot, 1) if slot else piece)
+    out[:TOK, HD:] = stats.astype(BF16)
+    if out.shape[0] > TOK:
+        out[TOK:, :] = jnp.zeros((out.shape[0] - TOK, HD + PAIR), BF16)
 
 
 def own_kernel(flags, q, kva, kvb, top, tot, mix, mix_out, top_out, tot_out):
@@ -179,7 +178,7 @@
     missing, own = flags[2:3, :], flags[3:4, :]
     tops, tots = [top[...]], [tot[...]]
     for part, gap in ((in_c, None), (in_d, missing)):
-        stats = part[:, HD:].astype(F32)
+        stats = part[:TOK, HD:].astype(F32)
         slots = [stats] + [pltpu.roll(stats, PAIR - 8 * slot, 1) for slot in range(1, 5)]
         highest = slots[0] + slots[1] + slots[2]
         tops.append(highest if gap is None else highest + gap)
@@ -200,7 +199,7 @@
         at = lanes(p)
         acc = None
         for factors, part in zip(spread, (mix, in_c, in_d)):
-            term = factors[:, at] * part[:, at].astype(F32)
+            term = factors[:, at] * part[:TOK, at].astype(F32)
             acc = term if acc is None else acc + term
         out[:, at] = acc.astype(BF16)
 
@@ -237,13 +236,13 @@
         functools.partial(early_kernel, cols), outs + [shaped(8, PAIR)], "early", [SMEM, VMEM, VMEM],
         tissue, q, stack,
     )
-    outs = [shaped(2, TOK, HD)] * 3
-    side_state = call(neighbour_kernel, outs, "neighbour", [VMEM] * 4, flags, qc, qd, stack)
+    state_c = call(neighbour_kernel, outs, "neighbour", [VMEM] * 3, flags, qc, stack)
+    state_d = call(neighbour_kernel, outs, "neighbour", [VMEM] * 3 + [ANY], flags, qd, stack, state_c[0])
     pack = shaped(TOK, HD + PAIR, dtype=BF16)
-    out_d, out_c = call(
-        side_kernel, [pack] * 2, "side", [VMEM] * 8, flags, qc, qd, kva, kvb, *side_state
-    )
+    pack_d = shaped(TOK + 8, HD + PAIR, dtype=BF16)
+    (out_d,) = call(side_kernel, [pack_d], "beyond", [VMEM] * 7, flags, qd, kva, kvb, *state_d)
     in_d = lax.ppermute(out_d, "col", beyond)
+    (out_c,) = call(side_kernel, [pack], "beside", [VMEM] * 7, flags, qc, kva, kvb, *state_c)
     in_c = lax.ppermute(out_c, "col", beside)
     own = [shaped(TOK, HD), shaped(TOK, PAIR), shaped(TOK, PAIR)]
     mix, top, tot = call(own_kernel, own, "own", [VMEM] * 7, flags, q, kva, kvb, *state)

time: 42.8 us -> 41.2 us (0.963)
  waiting for transfers between devices: 18.6 us -> 15.9 us
  Pallas kernels: 6.33 us -> 6.95 us
    ppermute x1, waiting for transfers between devices: 10.3 us -> 7.71 us  [on_device(): kvb = lax.ppermute(stack, 'row', far)]
    ppermute x1, waiting for transfers between devices: 4.71 us -> 3.34 us  [on_device(): in_d = lax.ppermute(out_d, 'col', beyond)]
    ppermute x1, starting transfers between devices: 2.7 us -> 3.92 us  [on_device(): qd = lax.ppermute(q, 'col', beyond)]
    ppermute x1, starting transfers between devices: 2.68 us -> 1.92 us  [on_device(): qc = lax.ppermute(q, 'col', beside)]
    ppermute x1, waiting for transfers between devices: 3.57 us -> 4.23 us  [on_device(): qd = lax.ppermute(q, 'col', beyond)]
    pallas_call x5 -> x7, Pallas kernels: 6.33 us -> 6.95 us  [call(): pl.pallas_call(body, out_shape=outs, in_specs=specs, out_specs=[VMEM] * l...]
    ppermute x1, waiting for transfers between devices: 0.01 us -> 0.57 us  [on_device(): in_c = lax.ppermute(out_c, 'col', beside)]
  transfers between devices with their start and end apart: 6 -> 6, of which waited for: 3 -> 4; matrix products, arithmetic and copies ran while one was open for 0% -> 0% of each run, Pallas kernels for 8% -> 12%
where the time goes in v5:
time: 41.2 us; the launch traced here: 40.9 us
  starting transfers between devices  16.9 us (41%)
  waiting for transfers between devices  15.9 us (39%)
  Pallas kernels  6.95 us (17%)
  other arithmetic  1.09 us (3%)
    ppermute x1, waiting for transfers between devices, on_device(): kvb = lax.ppermute(stack, 'row', far)  7.71 us
    pallas_call x7, Pallas kernels, call(): pl.pallas_call(body, out_shape=outs, in_specs=specs, out_specs=[VMEM] * l...  6.95 us
    ppermute x1, starting transfers between devices, on_device(): kva = lax.ppermute(stack, 'row', near)  5.32 us
    ppermute x1, waiting for transfers between devices, on_device(): qd = lax.ppermute(q, 'col', beyond)  4.23 us
    ppermute x1, starting transfers between devices, on_device(): qd = lax.ppermute(q, 'col', beyond)  3.92 us
    ppermute x1, waiting for transfers between devices, on_device(): in_d = lax.ppermute(out_d, 'col', beyond)  3.34 us
    ppermute x1, starting transfers between devices, on_device(): kvb = lax.ppermute(stack, 'row', far)  1.92 us
    ppermute x1, starting transfers between devices, on_device(): qc = lax.ppermute(q, 'col', beside)  1.92 us
  transfers between devices with their start and end apart: 6, of which 4 were waited for; matrix products, arithmetic and copies ran while one was open for 0% of the time, Pallas kernels for 12%

profile of v5, /device:TPU:768, one launch (start us, length us, event | category | flops | bytes accessed | tf_op | source)
XLA Modules:
  0.0 40.9 jit_solution(2541800342637399282)
XLA Ops:
  0.0 0.0 copy-start
  0.0 0.0 copy-start.1
  0.0 1.1 %pad_maximum_fusion.kv = bf16[256,768]{1,0:T(8,128)(2,1)S(1)} fusion(bf16[128,768]{1,0:T(8,128)(2,1)} %bitcast.8, bf16[128,768]{1,0:T(8,128)(2,1)} %bitcast.9), kind=kLoop, calls=%fused_computation | loop fusion | flops 786432 | bytes 786432 | tf_op jit(solution)/shard_map/concatenate | solution.py:229
  1.1 1.9 %collective-permute-start.1 = (bf16[256,768]{1,0:T(8,128)(2,1)S(1)}, bf16[256,768]{1,0:T(8,128)(2,1)S(1)}, u32[]{:S(2)}, u32[]{:S(2)}) collective-permute-start(bf16[256,768]{1,0:T(8,128)(2,1)S(1)} %pad_maximum_fusion.kv), channel_id=1, source_target_pairs={{64,128},{128,64},{192,256},{256,192},{320,384},{384,320},{448,512... | collective-permute-start | bytes 1179656 | tf_op jit(solution)/shard_map/ppermute | solution.py:230
  3.0 5.3 %collective-permute-start = (bf16[256,768]{1,0:T(8,128)(2,1)S(1)}, bf16[256,768]{1,0:T(8,128)(2,1)S(1)}, u32[]{:S(2)}, u32[]{:S(2)}) collective-permute-start(bf16[256,768]{1,0:T(8,128)(2,1)S(1)} %pad_maximum_fusion.kv), channel_id=1, source_target_pairs={{0,64},{64,0},{128,192},{192,128},{256,320},{320,256},{384,448},{4... | collective-permute-start | bytes 1179656 | tf_op jit(solution)/shard_map/ppermute | solution.py:231
  8.3 0.0 copy-done
  8.4 1.9 %collective-permute-start.3 = (bf16[128,768]{1,0:T(8,128)(2,1)S(1)}, bf16[128,768]{1,0:T(8,128)(2,1)S(1)}, u32[]{:S(2)}, u32[]{:S(2)}) collective-permute-start(bf16[128,768]{1,0:T(8,128)(2,1)S(1)} %bitcast.4), channel_id=1, source_target_pairs={{0,1},{1,0},{2,3},{3,2},{4,5},{5,4},{6,7},{7,6},{8,9},{9,8},{10,11... | collective-permute-start | bytes 589832 | tf_op jit(solution)/shard_map/ppermute | solution.py:233
  10.3 3.9 %collective-permute-start.2 = (bf16[128,768]{1,0:T(8,128)(2,1)S(1)}, bf16[128,768]{1,0:T(8,128)(2,1)S(1)}, u32[]{:S(2)}, u32[]{:S(2)}) collective-permute-start(bf16[128,768]{1,0:T(8,128)(2,1)S(1)} %bitcast.5), channel_id=1, source_target_pairs={{1,2},{2,1},{3,4},{4,3},{5,6},{6,5},{7,8},{8,7},{9,10},{10,9},{11,... | collective-permute-start | bytes 589832 | tf_op jit(solution)/shard_map/ppermute | solution.py:232
  14.2 0.0 copy-done.1
  14.2 1.5 %early.1 = (f32[1,128,768]{2,1,0:T(8,128)S(1)}, f32[1,128,768]{2,1,0:T(8,128)S(1)}, f32[1,128,768]{2,1,0:T(8,128)S(1)}, f32[8,128]{1,0:T(8,128)S(1)}) custom-call(s32[16,64]{1,0:T(8,128)S(1)} %copy-done.1, bf16[128,768]{1,0:T(8,128)(2,1)S(1)} %bitcast.6, bf16[256,768]{1,0:T(8,128)(2,1)S(1)} %pad_maximum_fusion.kv), custom_call_target="tpu_custom_call" | custom-call | flops 1 | bytes 1024 | tf_op jit(solution)/shard_map/early/pallas_call | solution.py:208
  15.7 0.0 collective-permute-done.3.query
  15.7 0.8 %neighbour.2 = (f32[1,128,768]{2,1,0:T(8,128)S(1)}, f32[1,128,768]{2,1,0:T(8,128)S(1)}, f32[1,128,768]{2,1,0:T(8,128)S(1)}) custom-call(f32[8,128]{1,0:T(8,128)S(1)} %get-tuple-element.18.flags, bf16[128,768]{1,0:T(8,128)(2,1)S(1)} %collective-permute-done.3.query, bf16[256,768]{1,0:T(8,128)(2,1)S(1)} %pad_maximum_fusion.kv), custom_call_target="tpu_custom_call" | custom-call | flops 1 | bytes 1024 | tf_op jit(solution)/shard_map/neighbour/pallas_call | solution.py:208
  16.5 4.2 %collective-permute-done.2.query = bf16[128,768]{1,0:T(8,128)(2,1)S(1)} collective-permute-done((bf16[128,768]{1,0:T(8,128)(2,1)S(1)}, bf16[128,768]{1,0:T(8,128)(2,1)S(1)}, u32[]{:S(2)}, u32[]{:S(2)}) %collective-permute-start.2) | collective-permute-done | bytes 196640 | tf_op jit(solution)/shard_map/ppermute | solution.py:232
  20.8 0.8 %neighbour.3 = (f32[1,128,768]{2,1,0:T(8,128)S(1)}, f32[1,128,768]{2,1,0:T(8,128)S(1)}, f32[1,128,768]{2,1,0:T(8,128)S(1)}) custom-call(f32[8,128]{1,0:T(8,128)S(1)} %get-tuple-element.18.flags, bf16[128,768]{1,0:T(8,128)(2,1)S(1)} %collective-permute-done.2.query, bf16[256,768]{1,0:T(8,128)(2,1)S(1)} %pad_maximum_fusion.kv, ...), custom_call_target="tpu_custom_call" | custom-call | flops 1 | bytes 1024 | tf_op jit(solution)/shard_map/neighbour/pallas_call | solution.py:208
  21.6 7.7 %collective-permute-done.1.kvb = bf16[256,768]{1,0:T(8,128)(2,1)S(1)} collective-permute-done((bf16[256,768]{1,0:T(8,128)(2,1)S(1)}, bf16[256,768]{1,0:T(8,128)(2,1)S(1)}, u32[]{:S(2)}, u32[]{:S(2)}) %collective-permute-start.1) | collective-permute-done | bytes 393248 | tf_op jit(solution)/shard_map/ppermute | solution.py:230
  29.3 0.0 collective-permute-done.kva
  29.3 0.9 %beyond.1 = bf16[136,896]{1,0:T(8,128)(2,1)S(1)} custom-call(f32[8,128]{1,0:T(8,128)S(1)} %get-tuple-element.18.flags, bf16[128,768]{1,0:T(8,128)(2,1)S(1)} %collective-permute-done.2.query, bf16[256,768]{1,0:T(8,128)(2,1)S(1)} %collective-permute-done.kva, bf16[256,768]{1,0:T(8,128)(2,1)S(1)} %collective-permute-done.1.kvb, ...), custom_call_target="tpu_custom_call" | custom-call | flops 1 | bytes 1024 | tf_op jit(solution)/shard_map/beyond/pallas_call | solution.py:208
  30.2 1.9 %collective-permute-start.4 = (bf16[136,896]{1,0:T(8,128)(2,1)S(1)}, bf16[136,896]{1,0:T(8,128)(2,1)S(1)}, u32[]{:S(2)}, u32[]{:S(2)}) collective-permute-start(bf16[136,896]{1,0:T(8,128)(2,1)S(1)} %beyond.1), channel_id=1, source_target_pairs={{1,2},{2,1},{3,4},{4,3},{5,6},{6,5},{7,8},{8,7},{9,10},{10,9},{11,... | collective-permute-start | bytes 731144 | tf_op jit(solution)/shard_map/ppermute | solution.py:244
  32.2 0.9 %beside.1 = bf16[128,896]{1,0:T(8,128)(2,1)S(1)} custom-call(f32[8,128]{1,0:T(8,128)S(1)} %get-tuple-element.18.flags, bf16[128,768]{1,0:T(8,128)(2,1)S(1)} %collective-permute-done.3.query, bf16[256,768]{1,0:T(8,128)(2,1)S(1)} %collective-permute-done.kva, bf16[256,768]{1,0:T(8,128)(2,1)S(1)} %collective-permute-done.1.kvb, ...), custom_call_target="tpu_custom_call" | custom-call | flops 1 | bytes 1024 | tf_op jit(solution)/shard_map/beside/pallas_call | solution.py:208
  33.1 1.9 %collective-permute-start.5 = (bf16[128,896]{1,0:T(8,128)(2,1)S(1)}, bf16[128,896]{1,0:T(8,128)(2,1)S(1)}, u32[]{:S(2)}, u32[]{:S(2)}) collective-permute-start(bf16[128,896]{1,0:T(8,128)(2,1)S(1)} %beside.1), channel_id=1, source_target_pairs={{0,1},{1,0},{2,3},{3,2},{4,5},{5,4},{6,7},{7,6},{8,9},{9,8},{10,11... | collective-permute-start | bytes 688136 | tf_op jit(solution)/shard_map/ppermute | solution.py:246
  35.1 0.9 %own.1 = (f32[128,768]{1,0:T(8,128)S(1)}, f32[128,128]{1,0:T(8,128)S(1)}, f32[128,128]{1,0:T(8,128)S(1)}) custom-call(f32[8,128]{1,0:T(8,128)S(1)} %get-tuple-element.18.flags, bf16[128,768]{1,0:T(8,128)(2,1)S(1)} %bitcast.7, bf16[256,768]{1,0:T(8,128)(2,1)S(1)} %collective-permute-done.kva, bf16[256,768]{1,0:T(8,128)(2,1)S(1)} %collective-permute-done.1.kvb, ...), custom_call_target="tpu_custom_call" | custom-call | flops 1 | bytes 1024 | tf_op jit(solution)/shard_map/own/pallas_call | solution.py:208
  35.9 0.6 %collective-permute-done.5.in_c = bf16[128,896]{1,0:T(8,128)(2,1)S(1)} collective-permute-done((bf16[128,896]{1,0:T(8,128)(2,1)S(1)}, bf16[128,896]{1,0:T(8,128)(2,1)S(1)}, u32[]{:S(2)}, u32[]{:S(2)}) %collective-permute-start.5) | collective-permute-done | bytes 229408 | tf_op jit(solution)/shard_map/ppermute | solution.py:246
  36.5 3.3 %collective-permute-done.4.in_d = bf16[136,896]{1,0:T(8,128)(2,1)S(1)} collective-permute-done((bf16[136,896]{1,0:T(8,128)(2,1)S(1)}, bf16[136,896]{1,0:T(8,128)(2,1)S(1)}, u32[]{:S(2)}, u32[]{:S(2)}) %collective-permute-start.4) | collective-permute-done | bytes 243744 | tf_op jit(solution)/shard_map/ppermute | solution.py:244
  39.9 1.1 %merge.1 = bf16[128,768]{1,0:T(8,128)(2,1)} custom-call(f32[8,128]{1,0:T(8,128)S(1)} %get-tuple-element.18.flags, f32[128,768]{1,0:T(8,128)S(1)} %get-tuple-element.22.mix, f32[128,128]{1,0:T(8,128)S(1)} %get-tuple-element.23.top, f32[128,128]{1,0:T(8,128)S(1)} %get-tuple-element.24.tot, bf16[136,896]{1,0:T(8,128)(2,1)S(1)} %collective-permute-done.4.in_d, ...), custom_call_target="tpu_custom_call" | custom-call | flops 1 | bytes 1024 | tf_op jit(solution)/shard_map/merge/pallas_call | solution.py:208
Async XLA Ops:
  0.0 8.3 %copy-start = (bf16[1,1,128,768]{3,2,1,0:T(8,128)(2,1)S(1)}, bf16[1,1,128,768]{3,2,1,0:T(8,128)(2,1)}, u32[]{:S(2)}) copy-start(bf16[1,1,128,768]{3,2,1,0:T(8,128)(2,1)} %param.4) | copy-start | bytes 589828
  0.0 14.2 %copy-start.1 = (s32[16,64]{1,0:T(8,128)S(1)}, s32[16,64]{1,0:T(8,128)}, u32[]{:S(2)}) copy-start(s32[16,64]{1,0:T(8,128)} %tissue.1) | copy-start | bytes 12292
  1.1 28.2 %collective-permute-start.1 = (bf16[256,768]{1,0:T(8,128)(2,1)S(1)}, bf16[256,768]{1,0:T(8,128)(2,1)S(1)}, u32[]{:S(2)}, u32[]{:S(2)}) collective-permute-start(bf16[256,768]{1,0:T(8,128)(2,1)S(1)} %pad_maximum_fusion.kv), channel_id=1, source_target_pairs={{64,128},{128,64},{192,256},{256,192},{320,384},{384,320},{448,512... | collective-permute-start | bytes 1179656 | tf_op jit(solution)/shard_map/ppermute | solution.py:230
  3.0 26.3 %collective-permute-start = (bf16[256,768]{1,0:T(8,128)(2,1)S(1)}, bf16[256,768]{1,0:T(8,128)(2,1)S(1)}, u32[]{:S(2)}, u32[]{:S(2)}) collective-permute-start(bf16[256,768]{1,0:T(8,128)(2,1)S(1)} %pad_maximum_fusion.kv), channel_id=1, source_target_pairs={{0,64},{64,0},{128,192},{192,128},{256,320},{320,256},{384,448},{4... | collective-permute-start | bytes 1179656 | tf_op jit(solution)/shard_map/ppermute | solution.py:231
  8.4 7.4 %collective-permute-start.3 = (bf16[128,768]{1,0:T(8,128)(2,1)S(1)}, bf16[128,768]{1,0:T(8,128)(2,1)S(1)}, u32[]{:S(2)}, u32[]{:S(2)}) collective-permute-start(bf16[128,768]{1,0:T(8,128)(2,1)S(1)} %bitcast.4), channel_id=1, source_target_pairs={{0,1},{1,0},{2,3},{3,2},{4,5},{5,4},{6,7},{7,6},{8,9},{9,8},{10,11... | collective-permute-start | bytes 589832 | tf_op jit(solution)/shard_map/ppermute | solution.py:233
  10.3 10.5 %collective-permute-start.2 = (bf16[128,768]{1,0:T(8,128)(2,1)S(1)}, bf16[128,768]{1,0:T(8,128)(2,1)S(1)}, u32[]{:S(2)}, u32[]{:S(2)}) collective-permute-start(bf16[128,768]{1,0:T(8,128)(2,1)S(1)} %bitcast.5), channel_id=1, source_target_pairs={{1,2},{2,1},{3,4},{4,3},{5,6},{6,5},{7,8},{8,7},{9,10},{10,9},{11,... | collective-permute-start | bytes 589832 | tf_op jit(solution)/shard_map/ppermute | solution.py:232
  30.2 9.6 %collective-permute-start.4 = (bf16[136,896]{1,0:T(8,128)(2,1)S(1)}, bf16[136,896]{1,0:T(8,128)(2,1)S(1)}, u32[]{:S(2)}, u32[]{:S(2)}) collective-permute-start(bf16[136,896]{1,0:T(8,128)(2,1)S(1)} %beyond.1), channel_id=1, source_target_pairs={{1,2},{2,1},{3,4},{4,3},{5,6},{6,5},{7,8},{8,7},{9,10},{10,9},{11,... | collective-permute-start | bytes 731144 | tf_op jit(solution)/shard_map/ppermute | solution.py:244
  33.1 3.4 %collective-permute-start.5 = (bf16[128,896]{1,0:T(8,128)(2,1)S(1)}, bf16[128,896]{1,0:T(8,128)(2,1)S(1)}, u32[]{:S(2)}, u32[]{:S(2)}) collective-permute-start(bf16[128,896]{1,0:T(8,128)(2,1)S(1)} %beside.1), channel_id=1, source_target_pairs={{0,1},{1,0},{2,3},{3,2},{4,5},{5,4},{6,7},{7,6},{8,9},{9,8},{10,11... | collective-permute-start | bytes 688136 | tf_op jit(solution)/shard_map/ppermute | solution.py:246

commit v6 on v5

--- a/solution.py
+++ b/solution.py
@@ -50,61 +50,48 @@
     return jnp.where(inside & (at > 0), 0.0, NEG).astype(F32)
 
 
-def attend_pair(query, keys, values, biases, low):
-    zero = jnp.zeros_like(query)
-    both = jnp.concatenate([jnp.where(low, query, zero), jnp.where(low, zero, query)], axis=0)
-    scores = []
-    for key, bias in zip(keys, biases):
-        s = lax.dot_general(both, key, (((1,), (1,)), ((), ())), preferred_element_type=F32) * SCALE
-        scores.append(s if bias is None else s + bias)
-    top = functools.reduce(jnp.maximum, scores)
-    top = jnp.maximum(jnp.max(top, axis=1, keepdims=True), FLOOR)
-    weights = [jnp.exp2(s - top) for s in scores]
-    total = jnp.sum(functools.reduce(jnp.add, weights), axis=1, keepdims=True)
-    mixed = functools.reduce(
-        jnp.add,
-        [jnp.dot(w.astype(BF16), v, preferred_element_type=F32) for w, v in zip(weights, values)],
-    )
-    shape = (TOK, PAIR)
-    top2 = jnp.where(low, jnp.broadcast_to(top[:TOK], shape), jnp.broadcast_to(top[TOK:], shape))
-    tot2 = jnp.where(low, jnp.broadcast_to(total[:TOK], shape), jnp.broadcast_to(total[TOK:], shape))
-    mix2 = jnp.where(low, mixed[:TOK], mixed[TOK:])
-    return top2, tot2, mix2
-
-
-def attend_late(query, kva, kvb, flags, at, low):
-    zero = jnp.zeros_like(query)
-    both = jnp.concatenate([jnp.where(low, query, zero), jnp.where(low, zero, query)], axis=0)
-    keys = jnp.concatenate([kva[:TOK, at], kvb[:TOK, at]], axis=0)
-    values = jnp.concatenate([kva[TOK:, at], kvb[TOK:, at]], axis=0)
-    values = jnp.concatenate([values, jnp.ones_like(values)], axis=1)
-    scores = lax.dot_general(both, keys, (((1,), (1,)), ((), ())), preferred_element_type=F32) * SCALE
-    scores = scores + jnp.concatenate([flags[0:1, :], flags[1:2, :]], axis=1)
-    top = jnp.maximum(jnp.max(scores, axis=1, keepdims=True), FLOOR)
-    mixed = jnp.dot(jnp.exp2(scores - top).astype(BF16), values, preferred_element_type=F32)
-    shape = (TOK, PAIR)
-    top2 = jnp.where(low, jnp.broadcast_to(top[:TOK], shape), jnp.broadcast_to(top[TOK:], shape))
-    tot2 = jnp.where(low, mixed[:TOK, PAIR:], mixed[TOK:, PAIR:])
-    mix2 = jnp.where(low, mixed[:TOK, :PAIR], mixed[TOK:, :PAIR])
-    return top2, tot2, mix2
+def attend(query, tiles, biases):
+    low = lane_low()
+    bias = jnp.concatenate(biases, axis=1)
+    scores, weights, tops, results = [], [], [], []
+    for p in range(PAIRS):
+        part = query[:, lanes(p)]
+        zero = jnp.zeros_like(part)
+        both = jnp.concatenate([jnp.where(low, part, zero), jnp.where(low, zero, part)], axis=0)
+        keys = jnp.concatenate([tile[:TOK, lanes(p)] for tile in tiles], axis=0)
+        product = lax.dot_general(both, keys, (((1,), (1,)), ((), ())), preferred_element_type=F32)
+        scores.append(product * SCALE + bias)
+    for s in scores:
+        top = jnp.maximum(jnp.max(s, axis=1, keepdims=True), FLOOR)
+        tops.append(top)
+        weights.append(jnp.exp2(s - top).astype(BF16))
+    for p, (top, w) in enumerate(zip(tops, weights)):
+        values = jnp.concatenate([tile[TOK:, lanes(p)] for tile in tiles], axis=0)
+        mixed = jnp.dot(
+            w, jnp.concatenate([values, jnp.ones_like(values)], axis=1), preferred_element_type=F32
+        )
+        shape = (TOK, PAIR)
+        results.append((
+            jnp.where(low, jnp.broadcast_to(top[:TOK], shape), jnp.broadcast_to(top[TOK:], shape)),
+            jnp.where(low, mixed[:TOK, PAIR:], mixed[TOK:, PAIR:]),
+            jnp.where(low, mixed[:TOK, :PAIR], mixed[TOK:, :PAIR]),
+        ))
+    return results
 
 
 def lanes(p):
     return slice(p * PAIR, (p + 1) * PAIR)
 
 
-def own_tile(query, kv, bias, i, low, top_ref, tot_ref, mix_ref):
-    for p in range(PAIRS):
-        at = lanes(p)
-        t, l, m = attend_pair(query[:, at], (kv[:TOK, at],), (kv[TOK:, at],), (bias,), low)
-        top_ref[i, :, at] = t
-        tot_ref[i, :, at] = l
-        mix_ref[i, :, at] = m
+def own_tile(query, kv, bias, top_ref, tot_ref, mix_ref):
+    for p, (top, total, mixed) in enumerate(attend(query, (kv,), (bias,))):
+        top_ref[:, lanes(p)] = top
+        tot_ref[:, lanes(p)] = total
+        mix_ref[:, lanes(p)] = mixed
 
 
 def early_kernel(cols, tissue, q, kv, top_ref, tot_ref, mix_ref, flags):
     row, col = position()
-    low = lane_low()
     own = tile_bias(tissue, row, col)
     near = tile_bias(tissue, partner(row, False), col)
     far = tile_bias(tissue, partner(row, True), col)
@@ -113,21 +100,19 @@
     shown = jnp.where(tissue[row, col] > 0, 1.0, 0.0).astype(F32)
     for n, value in enumerate((near, far, missing, shown, own)):
         flags[n : n + 1, :] = jnp.full((1, PAIR), value, F32)
-    own_tile(q, kv, None, 0, low, top_ref, tot_ref, mix_ref)
+    own_tile(q, kv, jnp.zeros((1, PAIR), F32), top_ref, tot_ref, mix_ref)
 
 
 def neighbour_kernel(flags, query, kv, *refs):
-    own_tile(query, kv, flags[4:5, :], 0, lane_low(), *refs[-3:])
-
-
-def late_part(query, kva, kvb, flags, state, i, p, low):
-    at = lanes(p)
-    t, l, m = attend_late(query[:, at], kva, kvb, flags, at, low)
-    top, tot, mix = state
-    t0 = top[i, :, at]
-    best = jnp.maximum(t, t0)
-    new, old = jnp.exp2(t - best), jnp.exp2(t0 - best)
-    return best, l * new + tot[i, :, at] * old, m * new + mix[i, :, at] * old
+    own_tile(query, kv, flags[4:5, :], *refs[-3:])
+
+
+def attend_late(query, kva, kvb, flags, top, tot, mix):
+    for p, (t, l, m) in enumerate(attend(query, (kva, kvb), (flags[0:1, :], flags[1:2, :]))):
+        t0 = top[:, lanes(p)]
+        best = jnp.maximum(t, t0)
+        new, old = jnp.exp2(t - best), jnp.exp2(t0 - best)
+        yield p, best, l * new + tot[:, lanes(p)] * old, m * new + mix[:, lanes(p)] * old
 
 
 def spot(p):
@@ -144,11 +129,9 @@
 
 
 def side_kernel(flags, query, kva, kvb, top, tot, mix, out):
-    low = lane_low()
     tops = jnp.zeros((TOK, PAIR), F32)
     tots = jnp.zeros((TOK, PAIR), F32)
-    for p in range(PAIRS):
-        best, total, mixed = late_part(query, kva, kvb, flags, (top, tot, mix), 0, p, low)
+    for p, best, total, mixed in attend_late(query, kva, kvb, flags, top, tot, mix):
         out[:TOK, lanes(p)] = mixed.astype(BF16)
         tops = jnp.where(spot(p), best, tops)
         tots = jnp.where(spot(p), total, tots)
@@ -161,11 +144,9 @@
 
 
 def own_kernel(flags, q, kva, kvb, top, tot, mix, mix_out, top_out, tot_out):
-    low = lane_low()
     tops = jnp.zeros((TOK, PAIR), F32)
     tots = jnp.ones((TOK, PAIR), F32)
-    for p in range(PAIRS):
-        best, total, mixed = late_part(q, kva, kvb, flags, (top, tot, mix), 0, p, low)
+    for p, best, total, mixed in attend_late(q, kva, kvb, flags, top, tot, mix):
         mix_out[:, lanes(p)] = mixed
         tops = jnp.where(spot(p), best, tops)
         tots = jnp.where(spot(p), total, tots)
@@ -174,7 +155,6 @@
 
 
 def merge_kernel(flags, mix, top, tot, in_d, in_c, out):
-    low = lane_low()
     missing, own = flags[2:3, :], flags[3:4, :]
     tops, tots = [top[...]], [tot[...]]
     for part, gap in ((in_c, None), (in_d, missing)):
@@ -231,7 +211,7 @@
     kva = lax.ppermute(stack, "row", near)
     qd = lax.ppermute(q, "col", beyond)
     qc = lax.ppermute(q, "col", beside)
-    outs = [shaped(1, TOK, HD)] * 3
+    outs = [shaped(TOK, HD)] * 3
     *state, flags = call(
         functools.partial(early_kernel, cols), outs + [shaped(8, PAIR)], "early", [SMEM, VMEM, VMEM],
         tissue, q, stack,

time: 41.2 us -> 41.1 us (level)
  Pallas kernels: 6.95 us -> 6.16 us
  waiting for transfers between devices: 15.9 us -> 16.6 us
    pallas_call x7, Pallas kernels: 6.95 us -> 6.16 us  [call(): pl.pallas_call(body, out_shape=outs, in_specs=specs, out_specs=[VMEM] * l...]
  transfers between devices with their start and end apart: 6 -> 6, of which waited for: 4 -> 4; matrix products, arithmetic and copies ran while one was open for 0% -> 0% of each run, Pallas kernels for 12% -> 10%
where the time goes in v6:
time: 41.1 us; the launch traced here: 40.9 us
  starting transfers between devices  16.9 us (41%)
  waiting for transfers between devices  16.6 us (40%)
  Pallas kernels  6.16 us (15%)
  other arithmetic  1.09 us (3%)
    ppermute x1, waiting for transfers between devices, on_device(): kvb = lax.ppermute(stack, 'row', far)  7.92 us
    pallas_call x7, Pallas kernels, call(): pl.pallas_call(body, out_shape=outs, in_specs=specs, out_specs=[VMEM] * l...  6.16 us
    ppermute x1, starting transfers between devices, on_device(): kva = lax.ppermute(stack, 'row', near)  5.32 us
    ppermute x1, waiting for transfers between devices, on_device(): qd = lax.ppermute(q, 'col', beyond)  4.64 us
    ppermute x1, starting transfers between devices, on_device(): qd = lax.ppermute(q, 'col', beyond)  3.92 us
    ppermute x1, waiting for transfers between devices, on_device(): in_d = lax.ppermute(out_d, 'col', beyond)  3.39 us
    ppermute x1, starting transfers between devices, on_device(): in_c = lax.ppermute(out_c, 'col', beside)  1.92 us
    ppermute x1, starting transfers between devices, on_device(): kvb = lax.ppermute(stack, 'row', far)  1.92 us
  transfers between devices with their start and end apart: 6, of which 4 were waited for; matrix products, arithmetic and copies ran while one was open for 0% of the time, Pallas kernels for 10%

profile of v6, /device:TPU:768, one launch (start us, length us, event | category | flops | bytes accessed | tf_op | source)
XLA Modules:
  0.0 40.9 jit_solution(7158356081990617846)
XLA Ops:
  0.0 0.0 copy-start
  0.0 0.0 copy-start.1
  0.0 1.1 %pad_maximum_fusion.kv = bf16[256,768]{1,0:T(8,128)(2,1)S(1)} fusion(bf16[128,768]{1,0:T(8,128)(2,1)} %bitcast.8, bf16[128,768]{1,0:T(8,128)(2,1)} %bitcast.9), kind=kLoop, calls=%fused_computation | loop fusion | flops 786432 | bytes 786432 | tf_op jit(solution)/shard_map/concatenate | solution.py:209
  1.1 1.9 %collective-permute-start.1 = (bf16[256,768]{1,0:T(8,128)(2,1)S(1)}, bf16[256,768]{1,0:T(8,128)(2,1)S(1)}, u32[]{:S(2)}, u32[]{:S(2)}) collective-permute-start(bf16[256,768]{1,0:T(8,128)(2,1)S(1)} %pad_maximum_fusion.kv), channel_id=1, source_target_pairs={{64,128},{128,64},{192,256},{256,192},{320,384},{384,320},{448,512... | collective-permute-start | bytes 1179656 | tf_op jit(solution)/shard_map/ppermute | solution.py:210
  3.0 5.3 %collective-permute-start = (bf16[256,768]{1,0:T(8,128)(2,1)S(1)}, bf16[256,768]{1,0:T(8,128)(2,1)S(1)}, u32[]{:S(2)}, u32[]{:S(2)}) collective-permute-start(bf16[256,768]{1,0:T(8,128)(2,1)S(1)} %pad_maximum_fusion.kv), channel_id=1, source_target_pairs={{0,64},{64,0},{128,192},{192,128},{256,320},{320,256},{384,448},{4... | collective-permute-start | bytes 1179656 | tf_op jit(solution)/shard_map/ppermute | solution.py:211
  8.3 0.0 copy-done
  8.4 1.9 %collective-permute-start.3 = (bf16[128,768]{1,0:T(8,128)(2,1)S(1)}, bf16[128,768]{1,0:T(8,128)(2,1)S(1)}, u32[]{:S(2)}, u32[]{:S(2)}) collective-permute-start(bf16[128,768]{1,0:T(8,128)(2,1)S(1)} %bitcast.4), channel_id=1, source_target_pairs={{0,1},{1,0},{2,3},{3,2},{4,5},{5,4},{6,7},{7,6},{8,9},{9,8},{10,11... | collective-permute-start | bytes 589832 | tf_op jit(solution)/shard_map/ppermute | solution.py:213
  10.3 3.9 %collective-permute-start.2 = (bf16[128,768]{1,0:T(8,128)(2,1)S(1)}, bf16[128,768]{1,0:T(8,128)(2,1)S(1)}, u32[]{:S(2)}, u32[]{:S(2)}) collective-permute-start(bf16[128,768]{1,0:T(8,128)(2,1)S(1)} %bitcast.5), channel_id=1, source_target_pairs={{1,2},{2,1},{3,4},{4,3},{5,6},{6,5},{7,8},{8,7},{9,10},{10,9},{11,... | collective-permute-start | bytes 589832 | tf_op jit(solution)/shard_map/ppermute | solution.py:212
  14.2 0.0 copy-done.1
  14.2 1.3 %early.1 = (f32[128,768]{1,0:T(8,128)S(1)}, f32[128,768]{1,0:T(8,128)S(1)}, f32[128,768]{1,0:T(8,128)S(1)}, f32[8,128]{1,0:T(8,128)S(1)}) custom-call(s32[16,64]{1,0:T(8,128)S(1)} %copy-done.1, bf16[128,768]{1,0:T(8,128)(2,1)S(1)} %bitcast.6, bf16[256,768]{1,0:T(8,128)(2,1)S(1)} %pad_maximum_fusion.kv), custom_call_target="tpu_custom_call" | custom-call | flops 1 | bytes 1024 | tf_op jit(solution)/shard_map/early/pallas_call | solution.py:188
  15.5 0.0 collective-permute-done.3.query
  15.5 0.6 %neighbour.2 = (f32[128,768]{1,0:T(8,128)S(1)}, f32[128,768]{1,0:T(8,128)S(1)}, f32[128,768]{1,0:T(8,128)S(1)}) custom-call(f32[8,128]{1,0:T(8,128)S(1)} %get-tuple-element.18.flags, bf16[128,768]{1,0:T(8,128)(2,1)S(1)} %collective-permute-done.3.query, bf16[256,768]{1,0:T(8,128)(2,1)S(1)} %pad_maximum_fusion.kv), custom_call_target="tpu_custom_call" | custom-call | flops 1 | bytes 1024 | tf_op jit(solution)/shard_map/neighbour/pallas_call | solution.py:188
  16.1 4.6 %collective-permute-done.2.query = bf16[128,768]{1,0:T(8,128)(2,1)S(1)} collective-permute-done((bf16[128,768]{1,0:T(8,128)(2,1)S(1)}, bf16[128,768]{1,0:T(8,128)(2,1)S(1)}, u32[]{:S(2)}, u32[]{:S(2)}) %collective-permute-start.2) | collective-permute-done | bytes 196640 | tf_op jit(solution)/shard_map/ppermute | solution.py:212
  20.8 0.6 %neighbour.3 = (f32[128,768]{1,0:T(8,128)S(1)}, f32[128,768]{1,0:T(8,128)S(1)}, f32[128,768]{1,0:T(8,128)S(1)}) custom-call(f32[8,128]{1,0:T(8,128)S(1)} %get-tuple-element.18.flags, bf16[128,768]{1,0:T(8,128)(2,1)S(1)} %collective-permute-done.2.query, bf16[256,768]{1,0:T(8,128)(2,1)S(1)} %pad_maximum_fusion.kv, f32[128,768]{1,0:T(8,128)S(1)} %get-tuple-element.25.refs_0_.top), custom_call_target="tpu_custom_call" | custom-call | flops 1 | bytes 1024 | tf_op jit(solution)/shard_map/neighbour/pallas_call | solution.py:188
  21.4 7.9 %collective-permute-done.1.kvb = bf16[256,768]{1,0:T(8,128)(2,1)S(1)} collective-permute-done((bf16[256,768]{1,0:T(8,128)(2,1)S(1)}, bf16[256,768]{1,0:T(8,128)(2,1)S(1)}, u32[]{:S(2)}, u32[]{:S(2)}) %collective-permute-start.1) | collective-permute-done | bytes 393248 | tf_op jit(solution)/shard_map/ppermute | solution.py:210
  29.3 0.0 collective-permute-done.kva
  29.3 0.9 %beyond.1 = bf16[136,896]{1,0:T(8,128)(2,1)S(1)} custom-call(f32[8,128]{1,0:T(8,128)S(1)} %get-tuple-element.18.flags, bf16[128,768]{1,0:T(8,128)(2,1)S(1)} %collective-permute-done.2.query, bf16[256,768]{1,0:T(8,128)(2,1)S(1)} %collective-permute-done.kva, bf16[256,768]{1,0:T(8,128)(2,1)S(1)} %collective-permute-done.1.kvb, ...), custom_call_target="tpu_custom_call" | custom-call | flops 1 | bytes 1024 | tf_op jit(solution)/shard_map/beyond/pallas_call | solution.py:188
  30.2 1.9 %collective-permute-start.4 = (bf16[136,896]{1,0:T(8,128)(2,1)S(1)}, bf16[136,896]{1,0:T(8,128)(2,1)S(1)}, u32[]{:S(2)}, u32[]{:S(2)}) collective-permute-start(bf16[136,896]{1,0:T(8,128)(2,1)S(1)} %beyond.1), channel_id=1, source_target_pairs={{1,2},{2,1},{3,4},{4,3},{5,6},{6,5},{7,8},{8,7},{9,10},{10,9},{11,... | collective-permute-start | bytes 731144 | tf_op jit(solution)/shard_map/ppermute | solution.py:224
  32.1 0.9 %beside.1 = bf16[128,896]{1,0:T(8,128)(2,1)S(1)} custom-call(f32[8,128]{1,0:T(8,128)S(1)} %get-tuple-element.18.flags, bf16[128,768]{1,0:T(8,128)(2,1)S(1)} %collective-permute-done.3.query, bf16[256,768]{1,0:T(8,128)(2,1)S(1)} %collective-permute-done.kva, bf16[256,768]{1,0:T(8,128)(2,1)S(1)} %collective-permute-done.1.kvb, ...), custom_call_target="tpu_custom_call" | custom-call | flops 1 | bytes 1024 | tf_op jit(solution)/shard_map/beside/pallas_call | solution.py:188
  33.0 1.9 %collective-permute-start.5 = (bf16[128,896]{1,0:T(8,128)(2,1)S(1)}, bf16[128,896]{1,0:T(8,128)(2,1)S(1)}, u32[]{:S(2)}, u32[]{:S(2)}) collective-permute-start(bf16[128,896]{1,0:T(8,128)(2,1)S(1)} %beside.1), channel_id=1, source_target_pairs={{0,1},{1,0},{2,3},{3,2},{4,5},{5,4},{6,7},{7,6},{8,9},{9,8},{10,11... | collective-permute-start | bytes 688136 | tf_op jit(solution)/shard_map/ppermute | solution.py:226
  35.0 0.8 %own.1 = (f32[128,768]{1,0:T(8,128)S(1)}, f32[128,128]{1,0:T(8,128)S(1)}, f32[128,128]{1,0:T(8,128)S(1)}) custom-call(f32[8,128]{1,0:T(8,128)S(1)} %get-tuple-element.18.flags, bf16[128,768]{1,0:T(8,128)(2,1)S(1)} %bitcast.7, bf16[256,768]{1,0:T(8,128)(2,1)S(1)} %collective-permute-done.kva, bf16[256,768]{1,0:T(8,128)(2,1)S(1)} %collective-permute-done.1.kvb, ...), custom_call_target="tpu_custom_call" | custom-call | flops 1 | bytes 1024 | tf_op jit(solution)/shard_map/own/pallas_call | solution.py:188
  35.8 0.6 %collective-permute-done.5.in_c = bf16[128,896]{1,0:T(8,128)(2,1)S(1)} collective-permute-done((bf16[128,896]{1,0:T(8,128)(2,1)S(1)}, bf16[128,896]{1,0:T(8,128)(2,1)S(1)}, u32[]{:S(2)}, u32[]{:S(2)}) %collective-permute-start.5) | collective-permute-done | bytes 229408 | tf_op jit(solution)/shard_map/ppermute | solution.py:226
  36.4 3.4 %collective-permute-done.4.in_d = bf16[136,896]{1,0:T(8,128)(2,1)S(1)} collective-permute-done((bf16[136,896]{1,0:T(8,128)(2,1)S(1)}, bf16[136,896]{1,0:T(8,128)(2,1)S(1)}, u32[]{:S(2)}, u32[]{:S(2)}) %collective-permute-start.4) | collective-permute-done | bytes 243744 | tf_op jit(solution)/shard_map/ppermute | solution.py:224
  39.8 1.1 %merge.1 = bf16[128,768]{1,0:T(8,128)(2,1)} custom-call(f32[8,128]{1,0:T(8,128)S(1)} %get-tuple-element.18.flags, f32[128,768]{1,0:T(8,128)S(1)} %get-tuple-element.22.mix, f32[128,128]{1,0:T(8,128)S(1)} %get-tuple-element.23.top, f32[128,128]{1,0:T(8,128)S(1)} %get-tuple-element.24.tot, bf16[136,896]{1,0:T(8,128)(2,1)S(1)} %collective-permute-done.4.in_d, ...), custom_call_target="tpu_custom_call" | custom-call | flops 1 | bytes 1024 | tf_op jit(solution)/shard_map/merge/pallas_call | solution.py:188
Async XLA Ops:
  0.0 8.3 %copy-start = (bf16[1,1,128,768]{3,2,1,0:T(8,128)(2,1)S(1)}, bf16[1,1,128,768]{3,2,1,0:T(8,128)(2,1)}, u32[]{:S(2)}) copy-start(bf16[1,1,128,768]{3,2,1,0:T(8,128)(2,1)} %param.4) | copy-start | bytes 589828
  0.0 14.2 %copy-start.1 = (s32[16,64]{1,0:T(8,128)S(1)}, s32[16,64]{1,0:T(8,128)}, u32[]{:S(2)}) copy-start(s32[16,64]{1,0:T(8,128)} %tissue.1) | copy-start | bytes 12292
  1.1 28.2 %collective-permute-start.1 = (bf16[256,768]{1,0:T(8,128)(2,1)S(1)}, bf16[256,768]{1,0:T(8,128)(2,1)S(1)}, u32[]{:S(2)}, u32[]{:S(2)}) collective-permute-start(bf16[256,768]{1,0:T(8,128)(2,1)S(1)} %pad_maximum_fusion.kv), channel_id=1, source_target_pairs={{64,128},{128,64},{192,256},{256,192},{320,384},{384,320},{448,512... | collective-permute-start | bytes 1179656 | tf_op jit(solution)/shard_map/ppermute | solution.py:210
  3.0 26.3 %collective-permute-start = (bf16[256,768]{1,0:T(8,128)(2,1)S(1)}, bf16[256,768]{1,0:T(8,128)(2,1)S(1)}, u32[]{:S(2)}, u32[]{:S(2)}) collective-permute-start(bf16[256,768]{1,0:T(8,128)(2,1)S(1)} %pad_maximum_fusion.kv), channel_id=1, source_target_pairs={{0,64},{64,0},{128,192},{192,128},{256,320},{320,256},{384,448},{4... | collective-permute-start | bytes 1179656 | tf_op jit(solution)/shard_map/ppermute | solution.py:211
  8.4 7.2 %collective-permute-start.3 = (bf16[128,768]{1,0:T(8,128)(2,1)S(1)}, bf16[128,768]{1,0:T(8,128)(2,1)S(1)}, u32[]{:S(2)}, u32[]{:S(2)}) collective-permute-start(bf16[128,768]{1,0:T(8,128)(2,1)S(1)} %bitcast.4), channel_id=1, source_target_pairs={{0,1},{1,0},{2,3},{3,2},{4,5},{5,4},{6,7},{7,6},{8,9},{9,8},{10,11... | collective-permute-start | bytes 589832 | tf_op jit(solution)/shard_map/ppermute | solution.py:213
  10.3 10.5 %collective-permute-start.2 = (bf16[128,768]{1,0:T(8,128)(2,1)S(1)}, bf16[128,768]{1,0:T(8,128)(2,1)S(1)}, u32[]{:S(2)}, u32[]{:S(2)}) collective-permute-start(bf16[128,768]{1,0:T(8,128)(2,1)S(1)} %bitcast.5), channel_id=1, source_target_pairs={{1,2},{2,1},{3,4},{4,3},{5,6},{6,5},{7,8},{8,7},{9,10},{10,9},{11,... | collective-permute-start | bytes 589832 | tf_op jit(solution)/shard_map/ppermute | solution.py:212
  30.2 9.6 %collective-permute-start.4 = (bf16[136,896]{1,0:T(8,128)(2,1)S(1)}, bf16[136,896]{1,0:T(8,128)(2,1)S(1)}, u32[]{:S(2)}, u32[]{:S(2)}) collective-permute-start(bf16[136,896]{1,0:T(8,128)(2,1)S(1)} %beyond.1), channel_id=1, source_target_pairs={{1,2},{2,1},{3,4},{4,3},{5,6},{6,5},{7,8},{8,7},{9,10},{10,9},{11,... | collective-permute-start | bytes 731144 | tf_op jit(solution)/shard_map/ppermute | solution.py:224
  33.0 3.4 %collective-permute-start.5 = (bf16[128,896]{1,0:T(8,128)(2,1)S(1)}, bf16[128,896]{1,0:T(8,128)(2,1)S(1)}, u32[]{:S(2)}, u32[]{:S(2)}) collective-permute-start(bf16[128,896]{1,0:T(8,128)(2,1)S(1)} %beside.1), channel_id=1, source_target_pairs={{0,1},{1,0},{2,3},{3,2},{4,5},{5,4},{6,7},{7,6},{8,9},{9,8},{10,11... | collective-permute-start | bytes 688136 | tf_op jit(solution)/shard_map/ppermute | solution.py:226

commit v7 on v6

--- a/solution.py
+++ b/solution.py
@@ -128,7 +128,7 @@
     return parts
 
 
-def side_kernel(flags, query, kva, kvb, top, tot, mix, out):
+def partial_sums(out, flags, query, kva, kvb, top, tot, mix):
     tops = jnp.zeros((TOK, PAIR), F32)
     tots = jnp.zeros((TOK, PAIR), F32)
     for p, best, total, mixed in attend_late(query, kva, kvb, flags, top, tot, mix):
@@ -139,8 +139,28 @@
     for slot, piece in enumerate(pieces(tops, 3) + pieces(tots, 2)):
         stats = stats + (pltpu.roll(piece, 8 * slot, 1) if slot else piece)
     out[:TOK, HD:] = stats.astype(BF16)
-    if out.shape[0] > TOK:
-        out[TOK:, :] = jnp.zeros((out.shape[0] - TOK, HD + PAIR), BF16)
+
+
+def waits(rows):
+    row, col = position()
+    return ((col & 1) == 1) & ((row == rows // 2 - 1) | (row == rows // 2))
+
+
+def beyond_kernel(rows, flags, kva, kvb, qd, top_d, tot_d, mix_d, qc, top_c, tot_c, mix_c, out_d, out_c):
+    out_d[TOK:, :] = jnp.zeros((out_d.shape[0] - TOK, HD + PAIR), BF16)
+    partial_sums(out_d, flags, qd, kva, kvb, top_d, tot_d, mix_d)
+
+    @pl.when(waits(rows))
+    def _():
+        partial_sums(out_c, flags, qc, kva, kvb, top_c, tot_c, mix_c)
+
+
+def beside_kernel(rows, flags, kva, kvb, qc, top_c, tot_c, mix_c, done, out_c):
+    del done
+
+    @pl.when(jnp.logical_not(waits(rows)))
+    def _():
+        partial_sums(out_c, flags, qc, kva, kvb, top_c, tot_c, mix_c)
 
 
 def own_kernel(flags, q, kva, kvb, top, tot, mix, mix_out, top_out, tot_out):
@@ -154,43 +174,49 @@
     tot_out[...] = tots
 
 
-def merge_kernel(flags, mix, top, tot, in_d, in_c, out):
-    missing, own = flags[2:3, :], flags[3:4, :]
-    tops, tots = [top[...]], [tot[...]]
-    for part, gap in ((in_c, None), (in_d, missing)):
-        stats = part[:TOK, HD:].astype(F32)
-        slots = [stats] + [pltpu.roll(stats, PAIR - 8 * slot, 1) for slot in range(1, 5)]
-        highest = slots[0] + slots[1] + slots[2]
-        tops.append(highest if gap is None else highest + gap)
-        tots.append(slots[3] + slots[4])
-    best = functools.reduce(jnp.maximum, tops)
-    shares = [jnp.exp2(t - best) for t in tops]
-    total = functools.reduce(jnp.add, [s * t for s, t in zip(shares, tots)])
+def unpack(part):
+    stats = part[:TOK, HD:].astype(F32)
+    slots = [stats] + [pltpu.roll(stats, PAIR - 8 * slot, 1) for slot in range(1, 5)]
+    return slots[0] + slots[1] + slots[2], slots[3] + slots[4]
+
+
+def spread(share):
     keep = (lax.broadcasted_iota(jnp.int32, (TOK, PAIR), 1) & (HDIM - 1)) < PAIRS
-    shares = [jnp.where(keep, s * own / total, 0.0) for s in shares]
     source = lax.broadcasted_iota(jnp.int32, (PAIR, HD), 0)
     target = lax.broadcasted_iota(jnp.int32, (PAIR, HD), 1)
     pick = (source == (target // PAIR + (target & HDIM))).astype(BF16)
-    pick = jnp.concatenate([pick, pick], axis=0)
-    spread = [
-        jnp.dot(jnp.concatenate(pieces(s, 2), axis=1).astype(BF16), pick, preferred_element_type=F32) for s in shares
-    ]
-    for p in range(PAIRS):
-        at = lanes(p)
-        acc = None
-        for factors, part in zip(spread, (mix, in_c, in_d)):
-            term = factors[:, at] * part[:TOK, at].astype(F32)
-            acc = term if acc is None else acc + term
-        out[:, at] = acc.astype(BF16)
-
-
-def call(body, outs, name, specs, *args, scratch=()):
+    parts = jnp.concatenate(pieces(jnp.where(keep, share, 0.0), 2), axis=1).astype(BF16)
+    return jnp.dot(parts, jnp.concatenate([pick, pick], axis=0), preferred_element_type=F32)
+
+
+def join_kernel(mix, top, tot, in_c, mix_out, top_out, tot_out):
+    other, total = unpack(in_c)
+    best = jnp.maximum(top[...], other)
+    mine, theirs = jnp.exp2(top[...] - best), jnp.exp2(other - best)
+    top_out[...] = best
+    tot_out[...] = tot[...] * mine + total * theirs
+    mix_out[...] = mix[...] * spread(mine) + in_c[:TOK, :HD].astype(F32) * spread(theirs)
+
+
+def merge_kernel(flags, mix, top, tot, in_d, out):
+    other, total = unpack(in_d)
+    other = other + flags[2:3, :]
+    best = jnp.maximum(top[...], other)
+    mine, theirs = jnp.exp2(top[...] - best), jnp.exp2(other - best)
+    factor = flags[3:4, :] / (tot[...] * mine + total * theirs)
+    out[...] = (
+        mix[...] * spread(mine * factor) + in_d[:TOK, :HD].astype(F32) * spread(theirs * factor)
+    ).astype(BF16)
+
+
+def call(body, outs, name, specs, *args, scratch=(), aliases={}):
     return pl.pallas_call(
         body,
         out_shape=outs,
         in_specs=specs,
         out_specs=[VMEM] * len(outs),
         scratch_shapes=scratch,
+        input_output_aliases=aliases,
         name=name,
         compiler_params=pltpu.CompilerParams(vmem_limit_bytes=16 << 20),
         cost_estimate=pl.CostEstimate(flops=1, transcendentals=0, bytes_accessed=1024),
@@ -220,15 +246,18 @@
     state_d = call(neighbour_kernel, outs, "neighbour", [VMEM] * 3 + [ANY], flags, qd, stack, state_c[0])
     pack = shaped(TOK, HD + PAIR, dtype=BF16)
     pack_d = shaped(TOK + 8, HD + PAIR, dtype=BF16)
-    (out_d,) = call(side_kernel, [pack_d], "beyond", [VMEM] * 7, flags, qd, kva, kvb, *state_d)
+    out_d, out_c = call(
+        functools.partial(beyond_kernel, rows), [pack_d, pack], "beyond", [VMEM] * 11, flags, kva, kvb, qd, *state_d, qc, *state_c
+    )
     in_d = lax.ppermute(out_d, "col", beyond)
-    (out_c,) = call(side_kernel, [pack], "beside", [VMEM] * 7, flags, qc, kva, kvb, *state_c)
+    (out_c,) = call(
+        functools.partial(beside_kernel, rows), [pack], "beside", [VMEM] * 8, flags, kva, kvb, qc, *state_c, out_c, aliases={7: 0}
+    )
     in_c = lax.ppermute(out_c, "col", beside)
     own = [shaped(TOK, HD), shaped(TOK, PAIR), shaped(TOK, PAIR)]
     mix, top, tot = call(own_kernel, own, "own", [VMEM] * 7, flags, q, kva, kvb, *state)
-    (out,) = call(
-        merge_kernel, [shaped(TOK, HD, dtype=BF16)], "merge", [VMEM] * 6, flags, mix, top, tot, in_d, in_c
-    )
+    mix, top, tot = call(join_kernel, own, "join", [VMEM] * 4, mix, top, tot, in_c)
+    (out,) = call(merge_kernel, [shaped(TOK, HD, dtype=BF16)], "merge", [VMEM] * 5, flags, mix, top, tot, in_d)
     return out.reshape(1, 1, TOK, HD)
 
 

time: 41.1 us -> 41.2 us (level)
  the two profiles are of different devices: /device:TPU:768 before, /device:TPU:255 now
where the time goes in v7:
time: 41.2 us; the launch traced here: 41 us
  starting transfers between devices  26.8 us (65%)
  waiting for transfers between devices  6.47 us (16%)
  Pallas kernels  6.46 us (16%)
  other arithmetic  1.09 us (3%)
    ppermute x1, starting transfers between devices, on_device(): kvb = lax.ppermute(stack, 'row', far)  11.8 us
    pallas_call x8, Pallas kernels, call(): pl.pallas_call(body, out_shape=outs, in_specs=specs, out_specs=[VMEM] * l...  6.46 us
    ppermute x1, starting transfers between devices, on_device(): in_d = lax.ppermute(out_d, 'col', beyond)  4.61 us
    ppermute x1, waiting for transfers between devices, on_device(): qd = lax.ppermute(q, 'col', beyond)  4.57 us
    ppermute x1, starting transfers between devices, on_device(): qd = lax.ppermute(q, 'col', beyond)  3.71 us
    ppermute x1, starting transfers between devices, on_device(): qc = lax.ppermute(q, 'col', beside)  2.86 us
    ppermute x1, starting transfers between devices, on_device(): kva = lax.ppermute(stack, 'row', near)  1.92 us
    ppermute x1, starting transfers between devices, on_device(): in_c = lax.ppermute(out_c, 'col', beside)  1.92 us
  transfers between devices with their start and end apart: 6, of which 3 were waited for; matrix products, arithmetic and copies ran while one was open for 0% of the time, Pallas kernels for 9%

profile of v7, /device:TPU:255, one launch (start us, length us, event | category | flops | bytes accessed | tf_op | source)
XLA Modules:
  0.0 41.0 jit_solution(8568185596373652217)
XLA Ops:
  0.0 0.0 copy-start
  0.0 0.0 copy-start.1
  0.0 1.1 %pad_maximum_fusion.kv = bf16[256,768]{1,0:T(8,128)(2,1)S(1)} fusion(bf16[128,768]{1,0:T(8,128)(2,1)} %bitcast.8, bf16[128,768]{1,0:T(8,128)(2,1)} %bitcast.9), kind=kLoop, calls=%fused_computation | loop fusion | flops 786432 | bytes 786432 | tf_op jit(solution)/shard_map/concatenate | solution.py:235
  1.1 11.8 %collective-permute-start.1 = (bf16[256,768]{1,0:T(8,128)(2,1)S(1)}, bf16[256,768]{1,0:T(8,128)(2,1)S(1)}, u32[]{:S(2)}, u32[]{:S(2)}) collective-permute-start(bf16[256,768]{1,0:T(8,128)(2,1)S(1)} %pad_maximum_fusion.kv), channel_id=1, source_target_pairs={{64,128},{128,64},{192,256},{256,192},{320,384},{384,320},{448,512... | collective-permute-start | bytes 1179656 | tf_op jit(solution)/shard_map/ppermute | solution.py:236
  12.9 1.9 %collective-permute-start = (bf16[256,768]{1,0:T(8,128)(2,1)S(1)}, bf16[256,768]{1,0:T(8,128)(2,1)S(1)}, u32[]{:S(2)}, u32[]{:S(2)}) collective-permute-start(bf16[256,768]{1,0:T(8,128)(2,1)S(1)} %pad_maximum_fusion.kv), channel_id=1, source_target_pairs={{0,64},{64,0},{128,192},{192,128},{256,320},{320,256},{384,448},{4... | collective-permute-start | bytes 1179656 | tf_op jit(solution)/shard_map/ppermute | solution.py:237
  14.8 0.0 copy-done
  14.8 2.9 %collective-permute-start.2 = (bf16[128,768]{1,0:T(8,128)(2,1)S(1)}, bf16[128,768]{1,0:T(8,128)(2,1)S(1)}, u32[]{:S(2)}, u32[]{:S(2)}) collective-permute-start(bf16[128,768]{1,0:T(8,128)(2,1)S(1)} %bitcast.4), channel_id=1, source_target_pairs={{0,1},{1,0},{2,3},{3,2},{4,5},{5,4},{6,7},{7,6},{8,9},{9,8},{10,11... | collective-permute-start | bytes 589832 | tf_op jit(solution)/shard_map/ppermute | solution.py:239
  17.7 3.7 %collective-permute-start.3 = (bf16[128,768]{1,0:T(8,128)(2,1)S(1)}, bf16[128,768]{1,0:T(8,128)(2,1)S(1)}, u32[]{:S(2)}, u32[]{:S(2)}) collective-permute-start(bf16[128,768]{1,0:T(8,128)(2,1)S(1)} %bitcast.5), channel_id=1, source_target_pairs={{1,2},{2,1},{3,4},{4,3},{5,6},{6,5},{7,8},{8,7},{9,10},{10,9},{11,... | collective-permute-start | bytes 589832 | tf_op jit(solution)/shard_map/ppermute | solution.py:238
  21.4 0.0 copy-done.1
  21.4 1.3 %early.1 = (f32[128,768]{1,0:T(8,128)S(1)}, f32[128,768]{1,0:T(8,128)S(1)}, f32[128,768]{1,0:T(8,128)S(1)}, f32[8,128]{1,0:T(8,128)S(1)}) custom-call(s32[16,64]{1,0:T(8,128)S(1)} %copy-done.1, bf16[128,768]{1,0:T(8,128)(2,1)S(1)} %bitcast.6, bf16[256,768]{1,0:T(8,128)(2,1)S(1)} %pad_maximum_fusion.kv), custom_call_target="tpu_custom_call" | custom-call | flops 1 | bytes 1024 | tf_op jit(solution)/shard_map/early/pallas_call | solution.py:213
  22.7 0.0 collective-permute-done.2.query.qc
  22.7 0.6 %neighbour.2 = (f32[128,768]{1,0:T(8,128)S(1)}, f32[128,768]{1,0:T(8,128)S(1)}, f32[128,768]{1,0:T(8,128)S(1)}) custom-call(f32[8,128]{1,0:T(8,128)S(1)} %get-tuple-element.23.flags, bf16[128,768]{1,0:T(8,128)(2,1)S(1)} %collective-permute-done.2.query.qc, bf16[256,768]{1,0:T(8,128)(2,1)S(1)} %pad_maximum_fusion.kv), custom_call_target="tpu_custom_call" | custom-call | flops 1 | bytes 1024 | tf_op jit(solution)/shard_map/neighbour/pallas_call | solution.py:213
  23.3 4.6 %collective-permute-done.3.query.qd = bf16[128,768]{1,0:T(8,128)(2,1)S(1)} collective-permute-done((bf16[128,768]{1,0:T(8,128)(2,1)S(1)}, bf16[128,768]{1,0:T(8,128)(2,1)S(1)}, u32[]{:S(2)}, u32[]{:S(2)}) %collective-permute-start.3) | collective-permute-done | bytes 196640 | tf_op jit(solution)/shard_map/ppermute | solution.py:238
  27.9 0.6 %neighbour.3 = (f32[128,768]{1,0:T(8,128)S(1)}, f32[128,768]{1,0:T(8,128)S(1)}, f32[128,768]{1,0:T(8,128)S(1)}) custom-call(f32[8,128]{1,0:T(8,128)S(1)} %get-tuple-element.23.flags, bf16[128,768]{1,0:T(8,128)(2,1)S(1)} %collective-permute-done.3.query.qd, bf16[256,768]{1,0:T(8,128)(2,1)S(1)} %pad_maximum_fusion.kv, ...), custom_call_target="tpu_custom_call" | custom-call | flops 1 | bytes 1024 | tf_op jit(solution)/shard_map/neighbour/pallas_call | solution.py:213
  28.5 0.0 collective-permute-done.1.kvb
  28.5 0.0 collective-permute-done.kva
  28.5 1.8 %beyond.1 = (bf16[136,896]{1,0:T(8,128)(2,1)S(1)}, bf16[128,896]{1,0:T(8,128)(2,1)S(1)}) custom-call(f32[8,128]{1,0:T(8,128)S(1)} %get-tuple-element.23.flags, bf16[256,768]{1,0:T(8,128)(2,1)S(1)} %collective-permute-done.kva, bf16[256,768]{1,0:T(8,128)(2,1)S(1)} %collective-permute-done.1.kvb, bf16[128,768]{1,0:T(8,128)(2,1)S(1)} %collective-permute-done.3.query.qd, ...), custom_call_target="tpu_custom_call" | custom-call | flops 1 | bytes 1024 | tf_op jit(solution)/shard_map/beyond/pallas_call | solution.py:213
  30.3 4.6 %collective-permute-start.5 = (bf16[136,896]{1,0:T(8,128)(2,1)S(1)}, bf16[136,896]{1,0:T(8,128)(2,1)S(1)}, u32[]{:S(2)}, u32[]{:S(2)}) collective-permute-start(bf16[136,896]{1,0:T(8,128)(2,1)S(1)} %get-tuple-element.40), channel_id=1, source_target_pairs={{1,2},{2,1},{3,4},{4,3},{5,6},{6,5},{7,8},{8,7},{9,10},{10,9},{11,... | collective-permute-start | bytes 731144 | tf_op jit(solution)/shard_map/ppermute | solution.py:252
  35.0 1.9 %collective-permute-start.4 = (bf16[128,896]{1,0:T(8,128)(2,1)S(1)}, bf16[128,896]{1,0:T(8,128)(2,1)S(1)}, u32[]{:S(2)}, u32[]{:S(2)}) collective-permute-start(bf16[128,896]{1,0:T(8,128)(2,1)S(1)} %beside.1), channel_id=1, source_target_pairs={{0,1},{1,0},{2,3},{3,2},{4,5},{5,4},{6,7},{7,6},{8,9},{9,8},{10,11... | collective-permute-start | bytes 688136 | tf_op jit(solution)/shard_map/ppermute | solution.py:256
  36.9 0.8 %own.1 = (f32[128,768]{1,0:T(8,128)S(1)}, f32[128,128]{1,0:T(8,128)S(1)}, f32[128,128]{1,0:T(8,128)S(1)}) custom-call(f32[8,128]{1,0:T(8,128)S(1)} %get-tuple-element.23.flags, bf16[128,768]{1,0:T(8,128)(2,1)S(1)} %bitcast.7, bf16[256,768]{1,0:T(8,128)(2,1)S(1)} %collective-permute-done.kva, bf16[256,768]{1,0:T(8,128)(2,1)S(1)} %collective-permute-done.1.kvb, ...), custom_call_target="tpu_custom_call" | custom-call | flops 1 | bytes 1024 | tf_op jit(solution)/shard_map/own/pallas_call | solution.py:213
  37.7 0.6 %collective-permute-done.4.in_c = bf16[128,896]{1,0:T(8,128)(2,1)S(1)} collective-permute-done((bf16[128,896]{1,0:T(8,128)(2,1)S(1)}, bf16[128,896]{1,0:T(8,128)(2,1)S(1)}, u32[]{:S(2)}, u32[]{:S(2)}) %collective-permute-start.4) | collective-permute-done | bytes 229408 | tf_op jit(solution)/shard_map/ppermute | solution.py:256
  38.3 0.3 join.1
  38.7 1.2 %collective-permute-done.5.in_d = bf16[136,896]{1,0:T(8,128)(2,1)S(1)} collective-permute-done((bf16[136,896]{1,0:T(8,128)(2,1)S(1)}, bf16[136,896]{1,0:T(8,128)(2,1)S(1)}, u32[]{:S(2)}, u32[]{:S(2)}) %collective-permute-start.5) | collective-permute-done | bytes 243744 | tf_op jit(solution)/shard_map/ppermute | solution.py:252
  39.9 1.0 %merge.1 = bf16[128,768]{1,0:T(8,128)(2,1)} custom-call(f32[8,128]{1,0:T(8,128)S(1)} %get-tuple-element.23.flags, f32[128,768]{1,0:T(8,128)S(1)} %get-tuple-element.37.mix, f32[128,128]{1,0:T(8,128)S(1)} %get-tuple-element.38.top, f32[128,128]{1,0:T(8,128)S(1)} %get-tuple-element.39.tot, bf16[136,896]{1,0:T(8,128)(2,1)S(1)} %collective-permute-done.5.in_d), custom_call_target="tpu_custom_call" | custom-call | flops 1 | bytes 1024 | tf_op jit(solution)/shard_map/merge/pallas_call | solution.py:213
  (1 shorter events, 0.0 us)
Async XLA Ops:
  0.0 14.8 %copy-start = (bf16[1,1,128,768]{3,2,1,0:T(8,128)(2,1)S(1)}, bf16[1,1,128,768]{3,2,1,0:T(8,128)(2,1)}, u32[]{:S(2)}) copy-start(bf16[1,1,128,768]{3,2,1,0:T(8,128)(2,1)} %param.4) | copy-start | bytes 589828
  0.0 21.4 %copy-start.1 = (s32[16,64]{1,0:T(8,128)S(1)}, s32[16,64]{1,0:T(8,128)}, u32[]{:S(2)}) copy-start(s32[16,64]{1,0:T(8,128)} %tissue.1) | copy-start | bytes 12292
  1.1 27.4 %collective-permute-start.1 = (bf16[256,768]{1,0:T(8,128)(2,1)S(1)}, bf16[256,768]{1,0:T(8,128)(2,1)S(1)}, u32[]{:S(2)}, u32[]{:S(2)}) collective-permute-start(bf16[256,768]{1,0:T(8,128)(2,1)S(1)} %pad_maximum_fusion.kv), channel_id=1, source_target_pairs={{64,128},{128,64},{192,256},{256,192},{320,384},{384,320},{448,512... | collective-permute-start | bytes 1179656 | tf_op jit(solution)/shard_map/ppermute | solution.py:236
  12.9 15.6 %collective-permute-start = (bf16[256,768]{1,0:T(8,128)(2,1)S(1)}, bf16[256,768]{1,0:T(8,128)(2,1)S(1)}, u32[]{:S(2)}, u32[]{:S(2)}) collective-permute-start(bf16[256,768]{1,0:T(8,128)(2,1)S(1)} %pad_maximum_fusion.kv), channel_id=1, source_target_pairs={{0,64},{64,0},{128,192},{192,128},{256,320},{320,256},{384,448},{4... | collective-permute-start | bytes 1179656 | tf_op jit(solution)/shard_map/ppermute | solution.py:237
  14.8 7.9 %collective-permute-start.2 = (bf16[128,768]{1,0:T(8,128)(2,1)S(1)}, bf16[128,768]{1,0:T(8,128)(2,1)S(1)}, u32[]{:S(2)}, u32[]{:S(2)}) collective-permute-start(bf16[128,768]{1,0:T(8,128)(2,1)S(1)} %bitcast.4), channel_id=1, source_target_pairs={{0,1},{1,0},{2,3},{3,2},{4,5},{5,4},{6,7},{7,6},{8,9},{9,8},{10,11... | collective-permute-start | bytes 589832 | tf_op jit(solution)/shard_map/ppermute | solution.py:239
  17.7 10.2 %collective-permute-start.3 = (bf16[128,768]{1,0:T(8,128)(2,1)S(1)}, bf16[128,768]{1,0:T(8,128)(2,1)S(1)}, u32[]{:S(2)}, u32[]{:S(2)}) collective-permute-start(bf16[128,768]{1,0:T(8,128)(2,1)S(1)} %bitcast.5), channel_id=1, source_target_pairs={{1,2},{2,1},{3,4},{4,3},{5,6},{6,5},{7,8},{8,7},{9,10},{10,9},{11,... | collective-permute-start | bytes 589832 | tf_op jit(solution)/shard_map/ppermute | solution.py:238
  30.3 9.6 %collective-permute-start.5 = (bf16[136,896]{1,0:T(8,128)(2,1)S(1)}, bf16[136,896]{1,0:T(8,128)(2,1)S(1)}, u32[]{:S(2)}, u32[]{:S(2)}) collective-permute-start(bf16[136,896]{1,0:T(8,128)(2,1)S(1)} %get-tuple-element.40), channel_id=1, source_target_pairs={{1,2},{2,1},{3,4},{4,3},{5,6},{6,5},{7,8},{8,7},{9,10},{10,9},{11,... | collective-permute-start | bytes 731144 | tf_op jit(solution)/shard_map/ppermute | solution.py:252
  35.0 3.4 %collective-permute-start.4 = (bf16[128,896]{1,0:T(8,128)(2,1)S(1)}, bf16[128,896]{1,0:T(8,128)(2,1)S(1)}, u32[]{:S(2)}, u32[]{:S(2)}) collective-permute-start(bf16[128,896]{1,0:T(8,128)(2,1)S(1)} %beside.1), channel_id=1, source_target_pairs={{0,1},{1,0},{2,3},{3,2},{4,5},{5,4},{6,7},{7,6},{8,9},{9,8},{10,11... | collective-permute-start | bytes 688136 | tf_op jit(solution)/shard_map/ppermute | solution.py:256

commit v8 on v7

--- a/solution.py
+++ b/solution.py
@@ -143,7 +143,7 @@
 
 def waits(rows):
     row, col = position()
-    return ((col & 1) == 1) & ((row == rows // 2 - 1) | (row == rows // 2))
+    return ((col & 1) == 1) & ((col & 15) != 15) & ((row == rows // 2 - 1) | (row == rows // 2))
 
 
 def beyond_kernel(rows, flags, kva, kvb, qd, top_d, tot_d, mix_d, qc, top_c, tot_c, mix_c, out_d, out_c):

time: 41.2 us -> 41.1 us (level)
  the two profiles are of different devices: /device:TPU:255 before, /device:TPU:768 now
where the time goes in v8:
time: 41.1 us; the launch traced here: 40.8 us
  starting transfers between devices  16.9 us (41%)
  waiting for transfers between devices  16.2 us (39%)
  Pallas kernels  6.47 us (16%)
  other arithmetic  1.09 us (3%)
    ppermute x1, waiting for transfers between devices, on_device(): kvb = lax.ppermute(stack, 'row', far)  7.91 us
    pallas_call x8, Pallas kernels, call(): pl.pallas_call(body, out_shape=outs, in_specs=specs, out_specs=[VMEM] * l...  6.47 us
    ppermute x1, starting transfers between devices, on_device(): kva = lax.ppermute(stack, 'row', near)  5.32 us
    ppermute x1, waiting for transfers between devices, on_device(): qd = lax.ppermute(q, 'col', beyond)  4.64 us
    ppermute x1, starting transfers between devices, on_device(): qd = lax.ppermute(q, 'col', beyond)  3.92 us
    ppermute x1, waiting for transfers between devices, on_device(): in_d = lax.ppermute(out_d, 'col', beyond)  3.04 us
    ppermute x1, starting transfers between devices, on_device(): qc = lax.ppermute(q, 'col', beside)  1.92 us
    ppermute x1, starting transfers between devices, on_device(): kvb = lax.ppermute(stack, 'row', far)  1.92 us
  transfers between devices with their start and end apart: 6, of which 4 were waited for; matrix products, arithmetic and copies ran while one was open for 0% of the time, Pallas kernels for 11%

profile of v8, /device:TPU:768, one launch (start us, length us, event | category | flops | bytes accessed | tf_op | source)
XLA Modules:
  0.0 40.8 jit_solution(9377991686107343873)
XLA Ops:
  0.0 0.0 copy-start
  0.0 0.0 copy-start.1
  0.0 1.1 %pad_maximum_fusion.kv = bf16[256,768]{1,0:T(8,128)(2,1)S(1)} fusion(bf16[128,768]{1,0:T(8,128)(2,1)} %bitcast.8, bf16[128,768]{1,0:T(8,128)(2,1)} %bitcast.9), kind=kLoop, calls=%fused_computation | loop fusion | flops 786432 | bytes 786432 | tf_op jit(solution)/shard_map/concatenate | solution.py:235
  1.1 1.9 %collective-permute-start.1 = (bf16[256,768]{1,0:T(8,128)(2,1)S(1)}, bf16[256,768]{1,0:T(8,128)(2,1)S(1)}, u32[]{:S(2)}, u32[]{:S(2)}) collective-permute-start(bf16[256,768]{1,0:T(8,128)(2,1)S(1)} %pad_maximum_fusion.kv), channel_id=1, source_target_pairs={{64,128},{128,64},{192,256},{256,192},{320,384},{384,320},{448,512... | collective-permute-start | bytes 1179656 | tf_op jit(solution)/shard_map/ppermute | solution.py:236
  3.0 5.3 %collective-permute-start = (bf16[256,768]{1,0:T(8,128)(2,1)S(1)}, bf16[256,768]{1,0:T(8,128)(2,1)S(1)}, u32[]{:S(2)}, u32[]{:S(2)}) collective-permute-start(bf16[256,768]{1,0:T(8,128)(2,1)S(1)} %pad_maximum_fusion.kv), channel_id=1, source_target_pairs={{0,64},{64,0},{128,192},{192,128},{256,320},{320,256},{384,448},{4... | collective-permute-start | bytes 1179656 | tf_op jit(solution)/shard_map/ppermute | solution.py:237
  8.3 0.0 copy-done
  8.4 1.9 %collective-permute-start.2 = (bf16[128,768]{1,0:T(8,128)(2,1)S(1)}, bf16[128,768]{1,0:T(8,128)(2,1)S(1)}, u32[]{:S(2)}, u32[]{:S(2)}) collective-permute-start(bf16[128,768]{1,0:T(8,128)(2,1)S(1)} %bitcast.4), channel_id=1, source_target_pairs={{0,1},{1,0},{2,3},{3,2},{4,5},{5,4},{6,7},{7,6},{8,9},{9,8},{10,11... | collective-permute-start | bytes 589832 | tf_op jit(solution)/shard_map/ppermute | solution.py:239
  10.3 3.9 %collective-permute-start.3 = (bf16[128,768]{1,0:T(8,128)(2,1)S(1)}, bf16[128,768]{1,0:T(8,128)(2,1)S(1)}, u32[]{:S(2)}, u32[]{:S(2)}) collective-permute-start(bf16[128,768]{1,0:T(8,128)(2,1)S(1)} %bitcast.5), channel_id=1, source_target_pairs={{1,2},{2,1},{3,4},{4,3},{5,6},{6,5},{7,8},{8,7},{9,10},{10,9},{11,... | collective-permute-start | bytes 589832 | tf_op jit(solution)/shard_map/ppermute | solution.py:238
  14.2 0.0 copy-done.1
  14.2 1.3 %early.1 = (f32[128,768]{1,0:T(8,128)S(1)}, f32[128,768]{1,0:T(8,128)S(1)}, f32[128,768]{1,0:T(8,128)S(1)}, f32[8,128]{1,0:T(8,128)S(1)}) custom-call(s32[16,64]{1,0:T(8,128)S(1)} %copy-done.1, bf16[128,768]{1,0:T(8,128)(2,1)S(1)} %bitcast.6, bf16[256,768]{1,0:T(8,128)(2,1)S(1)} %pad_maximum_fusion.kv), custom_call_target="tpu_custom_call" | custom-call | flops 1 | bytes 1024 | tf_op jit(solution)/shard_map/early/pallas_call | solution.py:213
  15.5 0.0 collective-permute-done.2.query.qc
  15.5 0.6 %neighbour.2 = (f32[128,768]{1,0:T(8,128)S(1)}, f32[128,768]{1,0:T(8,128)S(1)}, f32[128,768]{1,0:T(8,128)S(1)}) custom-call(f32[8,128]{1,0:T(8,128)S(1)} %get-tuple-element.23.flags, bf16[128,768]{1,0:T(8,128)(2,1)S(1)} %collective-permute-done.2.query.qc, bf16[256,768]{1,0:T(8,128)(2,1)S(1)} %pad_maximum_fusion.kv), custom_call_target="tpu_custom_call" | custom-call | flops 1 | bytes 1024 | tf_op jit(solution)/shard_map/neighbour/pallas_call | solution.py:213
  16.1 4.6 %collective-permute-done.3.query.qd = bf16[128,768]{1,0:T(8,128)(2,1)S(1)} collective-permute-done((bf16[128,768]{1,0:T(8,128)(2,1)S(1)}, bf16[128,768]{1,0:T(8,128)(2,1)S(1)}, u32[]{:S(2)}, u32[]{:S(2)}) %collective-permute-start.3) | collective-permute-done | bytes 196640 | tf_op jit(solution)/shard_map/ppermute | solution.py:238
  20.8 0.6 %neighbour.3 = (f32[128,768]{1,0:T(8,128)S(1)}, f32[128,768]{1,0:T(8,128)S(1)}, f32[128,768]{1,0:T(8,128)S(1)}) custom-call(f32[8,128]{1,0:T(8,128)S(1)} %get-tuple-element.23.flags, bf16[128,768]{1,0:T(8,128)(2,1)S(1)} %collective-permute-done.3.query.qd, bf16[256,768]{1,0:T(8,128)(2,1)S(1)} %pad_maximum_fusion.kv, ...), custom_call_target="tpu_custom_call" | custom-call | flops 1 | bytes 1024 | tf_op jit(solution)/shard_map/neighbour/pallas_call | solution.py:213
  21.4 7.9 %collective-permute-done.1.kvb = bf16[256,768]{1,0:T(8,128)(2,1)S(1)} collective-permute-done((bf16[256,768]{1,0:T(8,128)(2,1)S(1)}, bf16[256,768]{1,0:T(8,128)(2,1)S(1)}, u32[]{:S(2)}, u32[]{:S(2)}) %collective-permute-start.1) | collective-permute-done | bytes 393248 | tf_op jit(solution)/shard_map/ppermute | solution.py:236
  29.3 0.0 collective-permute-done.kva
  29.3 0.9 %beyond.1 = (bf16[136,896]{1,0:T(8,128)(2,1)S(1)}, bf16[128,896]{1,0:T(8,128)(2,1)S(1)}) custom-call(f32[8,128]{1,0:T(8,128)S(1)} %get-tuple-element.23.flags, bf16[256,768]{1,0:T(8,128)(2,1)S(1)} %collective-permute-done.kva, bf16[256,768]{1,0:T(8,128)(2,1)S(1)} %collective-permute-done.1.kvb, bf16[128,768]{1,0:T(8,128)(2,1)S(1)} %collective-permute-done.3.query.qd, ...), custom_call_target="tpu_custom_call" | custom-call | flops 1 | bytes 1024 | tf_op jit(solution)/shard_map/beyond/pallas_call | solution.py:213
  30.2 1.9 %collective-permute-start.5 = (bf16[136,896]{1,0:T(8,128)(2,1)S(1)}, bf16[136,896]{1,0:T(8,128)(2,1)S(1)}, u32[]{:S(2)}, u32[]{:S(2)}) collective-permute-start(bf16[136,896]{1,0:T(8,128)(2,1)S(1)} %get-tuple-element.40), channel_id=1, source_target_pairs={{1,2},{2,1},{3,4},{4,3},{5,6},{6,5},{7,8},{8,7},{9,10},{10,9},{11,... | collective-permute-start | bytes 731144 | tf_op jit(solution)/shard_map/ppermute | solution.py:252
  32.1 0.9 %beside.1 = bf16[128,896]{1,0:T(8,128)(2,1)S(1)} custom-call(f32[8,128]{1,0:T(8,128)S(1)} %get-tuple-element.23.flags, bf16[256,768]{1,0:T(8,128)(2,1)S(1)} %collective-permute-done.kva, bf16[256,768]{1,0:T(8,128)(2,1)S(1)} %collective-permute-done.1.kvb, bf16[128,768]{1,0:T(8,128)(2,1)S(1)} %collective-permute-done.2.query.qc, ...), custom_call_target="tpu_custom_call", output_to_operand_aliasing={{}: (7, {})} | custom-call | flops 1 | bytes 1024 | tf_op jit(solution)/shard_map/beside/pallas_call | solution.py:213
  33.0 1.9 %collective-permute-start.4 = (bf16[128,896]{1,0:T(8,128)(2,1)S(1)}, bf16[128,896]{1,0:T(8,128)(2,1)S(1)}, u32[]{:S(2)}, u32[]{:S(2)}) collective-permute-start(bf16[128,896]{1,0:T(8,128)(2,1)S(1)} %beside.1), channel_id=1, source_target_pairs={{0,1},{1,0},{2,3},{3,2},{4,5},{5,4},{6,7},{7,6},{8,9},{9,8},{10,11... | collective-permute-start | bytes 688136 | tf_op jit(solution)/shard_map/ppermute | solution.py:256
  35.0 0.8 %own.1 = (f32[128,768]{1,0:T(8,128)S(1)}, f32[128,128]{1,0:T(8,128)S(1)}, f32[128,128]{1,0:T(8,128)S(1)}) custom-call(f32[8,128]{1,0:T(8,128)S(1)} %get-tuple-element.23.flags, bf16[128,768]{1,0:T(8,128)(2,1)S(1)} %bitcast.7, bf16[256,768]{1,0:T(8,128)(2,1)S(1)} %collective-permute-done.kva, bf16[256,768]{1,0:T(8,128)(2,1)S(1)} %collective-permute-done.1.kvb, ...), custom_call_target="tpu_custom_call" | custom-call | flops 1 | bytes 1024 | tf_op jit(solution)/shard_map/own/pallas_call | solution.py:213
  35.8 0.6 %collective-permute-done.4.in_c = bf16[128,896]{1,0:T(8,128)(2,1)S(1)} collective-permute-done((bf16[128,896]{1,0:T(8,128)(2,1)S(1)}, bf16[128,896]{1,0:T(8,128)(2,1)S(1)}, u32[]{:S(2)}, u32[]{:S(2)}) %collective-permute-start.4) | collective-permute-done | bytes 229408 | tf_op jit(solution)/shard_map/ppermute | solution.py:256
  36.4 0.3 join.1
  36.8 3.0 %collective-permute-done.5.in_d = bf16[136,896]{1,0:T(8,128)(2,1)S(1)} collective-permute-done((bf16[136,896]{1,0:T(8,128)(2,1)S(1)}, bf16[136,896]{1,0:T(8,128)(2,1)S(1)}, u32[]{:S(2)}, u32[]{:S(2)}) %collective-permute-start.5) | collective-permute-done | bytes 243744 | tf_op jit(solution)/shard_map/ppermute | solution.py:252
  39.8 1.0 %merge.1 = bf16[128,768]{1,0:T(8,128)(2,1)} custom-call(f32[8,128]{1,0:T(8,128)S(1)} %get-tuple-element.23.flags, f32[128,768]{1,0:T(8,128)S(1)} %get-tuple-element.37.mix, f32[128,128]{1,0:T(8,128)S(1)} %get-tuple-element.38.top, f32[128,128]{1,0:T(8,128)S(1)} %get-tuple-element.39.tot, bf16[136,896]{1,0:T(8,128)(2,1)S(1)} %collective-permute-done.5.in_d), custom_call_target="tpu_custom_call" | custom-call | flops 1 | bytes 1024 | tf_op jit(solution)/shard_map/merge/pallas_call | solution.py:213
Async XLA Ops:
  0.0 8.3 %copy-start = (bf16[1,1,128,768]{3,2,1,0:T(8,128)(2,1)S(1)}, bf16[1,1,128,768]{3,2,1,0:T(8,128)(2,1)}, u32[]{:S(2)}) copy-start(bf16[1,1,128,768]{3,2,1,0:T(8,128)(2,1)} %param.4) | copy-start | bytes 589828
  0.0 14.2 %copy-start.1 = (s32[16,64]{1,0:T(8,128)S(1)}, s32[16,64]{1,0:T(8,128)}, u32[]{:S(2)}) copy-start(s32[16,64]{1,0:T(8,128)} %tissue.1) | copy-start | bytes 12292
  1.1 28.2 %collective-permute-start.1 = (bf16[256,768]{1,0:T(8,128)(2,1)S(1)}, bf16[256,768]{1,0:T(8,128)(2,1)S(1)}, u32[]{:S(2)}, u32[]{:S(2)}) collective-permute-start(bf16[256,768]{1,0:T(8,128)(2,1)S(1)} %pad_maximum_fusion.kv), channel_id=1, source_target_pairs={{64,128},{128,64},{192,256},{256,192},{320,384},{384,320},{448,512... | collective-permute-start | bytes 1179656 | tf_op jit(solution)/shard_map/ppermute | solution.py:236
  3.0 26.3 %collective-permute-start = (bf16[256,768]{1,0:T(8,128)(2,1)S(1)}, bf16[256,768]{1,0:T(8,128)(2,1)S(1)}, u32[]{:S(2)}, u32[]{:S(2)}) collective-permute-start(bf16[256,768]{1,0:T(8,128)(2,1)S(1)} %pad_maximum_fusion.kv), channel_id=1, source_target_pairs={{0,64},{64,0},{128,192},{192,128},{256,320},{320,256},{384,448},{4... | collective-permute-start | bytes 1179656 | tf_op jit(solution)/shard_map/ppermute | solution.py:237
  8.4 7.2 %collective-permute-start.2 = (bf16[128,768]{1,0:T(8,128)(2,1)S(1)}, bf16[128,768]{1,0:T(8,128)(2,1)S(1)}, u32[]{:S(2)}, u32[]{:S(2)}) collective-permute-start(bf16[128,768]{1,0:T(8,128)(2,1)S(1)} %bitcast.4), channel_id=1, source_target_pairs={{0,1},{1,0},{2,3},{3,2},{4,5},{5,4},{6,7},{7,6},{8,9},{9,8},{10,11... | collective-permute-start | bytes 589832 | tf_op jit(solution)/shard_map/ppermute | solution.py:239
  10.3 10.5 %collective-permute-start.3 = (bf16[128,768]{1,0:T(8,128)(2,1)S(1)}, bf16[128,768]{1,0:T(8,128)(2,1)S(1)}, u32[]{:S(2)}, u32[]{:S(2)}) collective-permute-start(bf16[128,768]{1,0:T(8,128)(2,1)S(1)} %bitcast.5), channel_id=1, source_target_pairs={{1,2},{2,1},{3,4},{4,3},{5,6},{6,5},{7,8},{8,7},{9,10},{10,9},{11,... | collective-permute-start | bytes 589832 | tf_op jit(solution)/shard_map/ppermute | solution.py:238
  30.2 9.6 %collective-permute-start.5 = (bf16[136,896]{1,0:T(8,128)(2,1)S(1)}, bf16[136,896]{1,0:T(8,128)(2,1)S(1)}, u32[]{:S(2)}, u32[]{:S(2)}) collective-permute-start(bf16[136,896]{1,0:T(8,128)(2,1)S(1)} %get-tuple-element.40), channel_id=1, source_target_pairs={{1,2},{2,1},{3,4},{4,3},{5,6},{6,5},{7,8},{8,7},{9,10},{10,9},{11,... | collective-permute-start | bytes 731144 | tf_op jit(solution)/shard_map/ppermute | solution.py:252
  33.0 3.4 %collective-permute-start.4 = (bf16[128,896]{1,0:T(8,128)(2,1)S(1)}, bf16[128,896]{1,0:T(8,128)(2,1)S(1)}, u32[]{:S(2)}, u32[]{:S(2)}) collective-permute-start(bf16[128,896]{1,0:T(8,128)(2,1)S(1)} %beside.1), channel_id=1, source_target_pairs={{0,1},{1,0},{2,3},{3,2},{4,5},{5,4},{6,7},{7,6},{8,9},{9,8},{10,11... | collective-permute-start | bytes 688136 | tf_op jit(solution)/shard_map/ppermute | solution.py:256
